TPU v7x, 32 devices: a whole 2x2x4 slice. The times are simulated.
32 devices in a mesh: groups: 2 (over y), expert: 4 (over z), tensor: 2 (over x), dp: 2 (over core).
Axes of the slice: x: 2, y: 2, z: 4, core: 2. Of those that a mesh axis runs over, the one named last changes fastest.
Arguments:
- attn: bfloat16 [1024, 4096], P(('groups', 'expert', 'dp'), 'tensor'), parts along dimension 0, may hold values from -6 to 6
- o_weight: bfloat16 [4096, 4096], P('tensor', 'dp'), may hold values from -0.09375 to 0.09375
- residual: bfloat16 [1024, 4096], P(('groups', 'expert', 'dp'), 'tensor'), parts along dimension 0, may hold values from -100 to 100
- norm_gain: bfloat16 [4096], replicated, may hold values from 0.099609375 to 1.8984375
- expert_ids: int32 [1024, 8], P(('groups', 'expert', 'dp')), parts along dimension 0, may hold values from 0 to 31, all different within a row; in each aligned block of 64 rows (0 to 63, 64 to 127, ...) at most 24 rows name the same one
- route_weights: float32 [1024, 8], P(('groups', 'expert', 'dp')), parts along dimension 0, may hold values from 0.1 to 1
- w_gate: bfloat16 [32, 4096, 1024], P(('expert', 'dp'), None, 'tensor'), may hold values from -0.09375 to 0.09375
- w_up: bfloat16 [32, 4096, 1024], P(('expert', 'dp'), None, 'tensor'), may hold values from -0.09375 to 0.09375
- w_down: bfloat16 [32, 1024, 4096], P(('expert', 'dp'), 'tensor'), may hold values from -0.25 to 0.25
Outputs:
- moe_out: bfloat16 [1024, 4096], P(('groups', 'expert', 'dp'), 'tensor'), parts along dimension 0
There are 2 independent parts, one for each index of `groups`. A program takes and returns all parts, laid end to end along the dimension named above; an argument that names none is the same for every part. Nothing has to cross between parts.
Inputs may be any that keep to these rules, and one draw needn't show every extreme that they name: `expert_ids`: each row names 8 different experts. Within each aligned block of 64 rows (the rows of one device) no expert is named by more than 24 rows, and in every draw some block has an expert named by exactly 24 rows.
All inputs are finite; a program needn't handle non-finite values.
Results may differ from a plain program's by a relative error of at most 0.024.
Values may be sent and summed in bfloat16 or wider, within the bound.
No kernel may reach another device: no remote copies, remote signals or barrier semaphores. Data moves between devices by JAX's collectives and lax.ppermute only.
A program may use at most 128 MiB of HBM per device.

v0:
```python
import jax
import jax.numpy as jnp
from jax import lax
from jax.sharding import PartitionSpec as P

EXPERTS = 32
SLOT = 24


epsilon = 1e-06


def on_device(attn, o_weight, residual, norm_gain, expert_ids, route_weights, w_gate, w_up, w_down):
    rows_here = attn.shape[0]
    width = norm_gain.shape[0]
    pieces = lax.axis_size("tensor")
    quarter = width // pieces
    offset = lax.axis_index("tensor") * quarter
    partial_value = jnp.dot(
        attn, lax.all_gather(o_weight, "dp", axis=1, tiled=True), preferred_element_type=jnp.float32
    )
    own_cols = lax.dynamic_slice_in_dim(partial_value, offset, quarter, 1) + residual.astype(
        jnp.float32
    )
    partial_value = lax.dynamic_update_slice_in_dim(partial_value, own_cols, offset, 1)
    summed = lax.psum(partial_value.astype(jnp.bfloat16), "tensor")
    rounded = lax.optimization_barrier(summed)
    hidden_f = rounded.astype(jnp.float32)
    inverse = lax.rsqrt(jnp.mean(hidden_f * hidden_f, axis=1) + epsilon)
    payload = (hidden_f * inverse[:, None] * norm_gain.astype(jnp.float32)[None, :]).astype(
        jnp.bfloat16
    )
    onehot = (expert_ids[:, :, None] == jnp.arange(EXPERTS, dtype=jnp.int32)).astype(jnp.float32)
    chosen = jnp.sum(onehot, axis=1)
    row_ids = jnp.arange(rows_here)
    earlier = (row_ids[:, None] > row_ids[None, :]).astype(jnp.float32)
    before = jnp.dot(earlier, chosen, precision=lax.Precision.HIGHEST)
    slot_ids = jnp.arange(SLOT, dtype=jnp.float32)
    placing = (
        (before.T[:, None, :] == slot_ids[None, :, None]) & (chosen.T[:, None, :] > 0.5)
    ).astype(jnp.float32)
    outgoing = jnp.einsum(
        "ecr,rd->ecd", placing.astype(jnp.bfloat16), payload, preferred_element_type=jnp.float32
    ).astype(jnp.bfloat16)
    sources = lax.axis_size(("expert", "dp"))
    held_experts = w_gate.shape[0]
    outgoing = outgoing.reshape(sources, held_experts, SLOT, payload.shape[1])
    arrived_rows = lax.all_to_all(
        outgoing, ("expert", "dp"), split_axis=0, concat_axis=0, tiled=True
    )
    gate_acc = jnp.einsum(
        "sjcd,jdf->sjcf", arrived_rows, w_gate, preferred_element_type=jnp.float32
    )
    up_acc = jnp.einsum("sjcd,jdf->sjcf", arrived_rows, w_up, preferred_element_type=jnp.float32)
    activated = (jax.nn.silu(gate_acc) * up_acc).astype(jnp.bfloat16)
    partials = jnp.einsum("sjcf,jfd->sjcd", activated, w_down, preferred_element_type=jnp.float32)
    outputs = lax.psum_scatter(
        partials.astype(jnp.bfloat16), "tensor", scatter_dimension=3, tiled=True
    )
    returned = lax.all_to_all(outputs, ("expert", "dp"), split_axis=0, concat_axis=0, tiled=True)
    returned = returned.reshape(EXPERTS, SLOT, quarter).astype(jnp.float32)
    weight_map = jnp.sum(route_weights[:, :, None] * onehot, axis=1)
    weighted = placing * weight_map.T[:, None, :]
    moe_out = jnp.einsum(
        "ecr,ecd->rd",
        weighted,
        returned,
        precision=lax.Precision.HIGHEST,
        preferred_element_type=jnp.float32,
    )
    return moe_out.astype(jnp.bfloat16)


def solution(mesh):
    placed = (
        P(("groups", "expert", "dp"), "tensor"),
        P("tensor", "dp"),
        P(("groups", "expert", "dp"), "tensor"),
        P(),
        P(("groups", "expert", "dp"), None),
        P(("groups", "expert", "dp"), None),
        P(("expert", "dp"), None, "tensor"),
        P(("expert", "dp"), None, "tensor"),
        P(("expert", "dp"), "tensor", None),
    )
    return jax.shard_map(
        on_device,
        mesh=mesh,
        in_specs=placed,
        out_specs=P(("groups", "expert", "dp"), "tensor"),
        check_vma=False,
    )
```

profile of v0, /device:TPU:0, one launch (start us, length us, event | category | flops | bytes accessed | tf_op | source)
XLA Modules:
  0.0 422.2 jit_solution(4321058223457081654)
XLA Ops:
  6.5 0.0 copy-start
  6.5 0.0 all-gather.2.cloned.1.call-start
  6.5 0.7 all-gather.2.cloned.1.call-update
  7.3 0.0 all-reduce.2.cloned.1.call-start
  7.3 0.0 copy-done.4
  7.3 0.0 copy-done.5
  7.4 0.0 copy-start.2
  7.4 0.0 copy-start.3
  7.4 34.3 %all-gather.2.cloned.1.call-done = bf16[2048,4096]{1,0:T(8,128)(2,1)} async-done(((bf16[2048,2048]{1,0:T(8,128)(2,1)}), bf16[2048,4096]{1,0:T(8,128)(2,1)}) %all-gather.2.cloned.1.call-update) | async-done | bytes 16777232 | tf_op jit(solution)/shard_map/all_gather | solution.py:20
  41.7 0.0 copy-done
  41.7 8.8 %fusion.47 = f32[64,4096]{1,0:T(8,128)S(1)} fusion(bf16[64,2048]{1,0:T(8,128)(2,1)S(1)} %copy-done, bf16[2048,4096]{1,0:T(8,128)(2,1)} %all-gather.2.cloned.1.call-done), kind=kOutput, calls=%fused_computation.48 | convolution fusion | flops 1073741824 | bytes 18087936 | tf_op jit(solution)/shard_map/dot_general | solution.py:19
  50.5 0.0 copy-done.2
  50.5 0.1 add_dynamic-update-slice_fusion
  50.6 0.8 convert_element_type.45
  51.5 0.0 all-reduce.2.cloned.1.call-update
  51.5 0.0 reduce-scatter.2.cloned.1.call-start
  51.6 0.0 copy-done.3
  51.6 0.1 fusion.45
  51.7 0.1 convert_convert_fusion
  51.8 29.7 %all-reduce.2.cloned.1.call-done = bf16[64,4096]{1,0:T(8,128)(2,1)} async-done(((bf16[64,4096]{1,0:T(8,128)(2,1)}), bf16[64,4096]{1,0:T(8,128)(2,1)}) %all-reduce.2.cloned.1.call-update) | async-done | bytes 524304 | tf_op jit(solution)/shard_map/psum | solution.py:26
  81.5 1.2 fusion.30
  82.7 2.9 convolution_convert_fusion
  85.7 143.3 %all_to_all.10 = bf16[8,4,24,4096]{3,2,1,0:T(8,128)(2,1)S(1)} all-to-all(bf16[8,4,24,4096]{3,2,1,0:T(8,128)(2,1)S(1)} %bitcast.56), channel_id=1, replica_groups=mesh['groups'=2,'expert'=4,'tensor'=2,'dp'=2] {'expert','dp'}, dimensions={0} | all-to-all | bytes 12582912 | tf_op jit(solution)/shard_map/all_to_all | solution.py:48
  229.0 7.7 %fusion.4 = f32[4,8,24,512]{3,2,1,0:T(8,128)S(1)} fusion(bf16[4,4096,512]{2,1,0:T(8,128)(2,1)} %param.15, bf16[8,4,24,4096]{3,2,1,0:T(8,128)(2,1)S(1)} %all_to_all.10), kind=kOutput, calls=%fused_computation.4 | convolution fusion | flops 3221225472 | bytes 24641536 | tf_op jit(solution)/shard_map/sjcd,jdf->sjcf/dot_general | solution.py:51
  236.8 9.6 %fusion.22 = bf16[8,4,24,512]{3,2,0,1:T(8,128)(2,1)S(1)} fusion(f32[4,8,24,512]{3,2,1,0:T(8,128)S(1)} %fusion.4, bf16[4,4096,512]{2,1,0:T(8,128)(2,1)} %param.16, bf16[8,4,24,4096]{3,2,1,0:T(8,128)(2,1)S(1)} %all_to_all.10), kind=kOutput, calls=%fused_computation.16 | convolution fusion | flops 3223584768 | bytes 25427968 | tf_op jit(solution)/shard_map/sjcd,jdf->sjcf/dot_general | solution.py:54
  246.3 11.9 %fusion.9 = bf16[8,4,24,4096]{3,2,0,1:T(8,128)(2,1)} fusion(bf16[8,4,24,512]{3,2,0,1:T(8,128)(2,1)S(1)} %fusion.22, bf16[4,512,4096]{2,1,0:T(8,128)(2,1)} %param.17), kind=kOutput, calls=%fused_computation.8 | convolution fusion | flops 3224371200 | bytes 23855104 | tf_op jit(solution)/shard_map/sjcf,jfd->sjcd/dot_general | solution.py:56
  258.2 0.0 reduce-scatter.2.cloned.1.call-update
  258.2 75.3 %reduce-scatter.2.cloned.1.call-done = bf16[8,4,24,2048]{3,2,0,1:T(8,128)(2,1)} async-done(((bf16[8,4,24,4096]{3,2,0,1:T(8,128)(2,1)}), bf16[8,4,24,2048]{3,2,0,1:T(8,128)(2,1)}) %reduce-scatter.2.cloned.1.call-update) | async-done | bytes 3145744 | tf_op jit(solution)/shard_map/reduce_scatter | solution.py:57
  333.5 2.3 copy.30
  335.8 75.9 %all_to_all.11 = bf16[8,4,24,2048]{3,2,1,0:T(8,128)(2,1)S(1)} all-to-all(bf16[8,4,24,2048]{3,2,1,0:T(8,128)(2,1)S(1)} %copy.30), channel_id=1, replica_groups=mesh['groups'=2,'expert'=4,'tensor'=2,'dp'=2] {'expert','dp'}, dimensions={0} | all-to-all | bytes 6291456 | tf_op jit(solution)/shard_map/all_to_all | solution.py:60
  411.7 3.9 fusion.19
  415.6 0.0 copy-done.1
  (7 shorter events, 0.1 us)
Async XLA Ops:
  6.5 35.2 %copy-start = (bf16[64,2048]{1,0:T(8,128)(2,1)S(1)}, bf16[64,2048]{1,0:T(8,128)(2,1)}, u32[]{:S(2)}) copy-start(bf16[64,2048]{1,0:T(8,128)(2,1)} %param.9) | copy-start | bytes 786436
  6.5 0.8 copy-start.4
  6.5 0.8 copy-start.5
  6.5 35.2 %all-gather.2.cloned.1.call-start = ((), (), s32[]{:S(2)}) async-start(), calls=%async_computation.3 | async-start | bytes 25165824 | tf_op jit(solution)/shard_map/all_gather | solution.py:20
  7.3 74.2 %all-reduce.2.cloned.1.call-start = ((), (), s32[]{:S(2)}) async-start(), calls=%async_computation.4 | async-start | bytes 1048576 | tf_op jit(solution)/shard_map/psum | solution.py:26
  7.4 43.1 %copy-start.2 = (bf16[64,2048]{1,0:T(8,128)(2,1)S(1)}, bf16[64,2048]{1,0:T(8,128)(2,1)}, u32[]{:S(2)}) copy-start(bf16[64,2048]{1,0:T(8,128)(2,1)} %param.11) | copy-start | bytes 786436
  7.4 44.2 %copy-start.3 = (bf16[4096]{0:T(1024)(128)(2,1)S(1)}, bf16[4096]{0:T(1024)(128)(2,1)}, u32[]{:S(2)}) copy-start(bf16[4096]{0:T(1024)(128)(2,1)} %param.12) | copy-start | bytes 24580
  51.5 282.0 %reduce-scatter.2.cloned.1.call-start = ((), (), s32[]{:S(2)}) async-start(), calls=%async_computation.5 | async-start | bytes 9437184 | tf_op jit(solution)/shard_map/reduce_scatter | solution.py:57
  333.5 82.1 %copy-start.1 = (bf16[64,2048]{1,0:T(8,128)(2,1)S(1)}, bf16[64,2048]{1,0:T(8,128)(2,1)}, u32[]{:S(2)}) copy-start(bf16[64,2048]{1,0:T(8,128)(2,1)} %param.9) | copy-start | bytes 786436
Sparse Core Ops, SparseCore 0:
  8.9 32.7 all-gather.1
  51.6 29.8 all-reduce.1
  258.4 75.0 reduce-scatter.1
where the time goes:
time: 423 us; the launch traced here: 422 us
  blocking collectives  219 us (52%)
  waiting for transfers between devices  140 us (33%)
  matrix products  44.9 us (11%)
  between operations  13.2 us (3%)
    all_to_all x1, blocking collectives, on_device(): lax.all_to_all(outgoing, ('expert', 'dp'), split_axis=0, concat_axis=0, t...  143 us
    all_to_all x1, blocking collectives, on_device(): lax.all_to_all(outputs, ('expert', 'dp'), split_axis=0, concat_axis=0, ti...  75.9 us
    reduce_scatter x1, waiting for transfers between devices, on_device(): lax.psum_scatter(partials.astype(jnp.bfloat16), 'tensor', scatter_dimensi...  75.3 us
    all_gather x1, waiting for transfers between devices, on_device(): lax.all_gather(o_weight, 'dp', axis=1, tiled=True)  34.3 us
    psum x1, waiting for transfers between devices, on_device(): summed = lax.psum(partial_value.astype(jnp.bfloat16), 'tensor')  29.7 us
    dot_general x1, matrix products, on_device(): jnp.einsum('sjcf,jfd->sjcd', activated, w_down, preferred_element_type=jn...  11.9 us
    dot_general x1, matrix products, on_device(): jnp.einsum('sjcd,jdf->sjcf', arrived_rows, w_up, preferred_element_type=j...  9.58 us
    dot_general x1, matrix products, on_device(): jnp.dot(attn, lax.all_gather(o_weight, 'dp', axis=1, tiled=True), preferr...  8.78 us
  transfers between devices with their start and end apart: 3, of which 3 were waited for; matrix products, arithmetic and copies ran while one was open for 0% of the time, Pallas kernels for 0%

commit v1 on v0

v1 whole, which is shorter than its diff:
```python
import functools

import jax
import jax.numpy as jnp
from jax import lax
from jax.experimental import pallas as pl
from jax.experimental.pallas import tpu as pltpu
from jax.sharding import PartitionSpec as P

SLOT = 24

epsilon = 1e-06

CHUNKS = (4, 4)


def fetch(value, axis, step):
    size = lax.axis_size(axis)
    if step % size == 0:
        return value
    return lax.ppermute(value, axis, [((i + step) % size, i) for i in range(size)])


def pick(stacked, index):
    return lax.dynamic_index_in_dim(stacked, index, 0, keepdims=False)


def slot_codes(expert_ids, experts):
    rows_here = expert_ids.shape[0]
    onehot = (expert_ids[:, :, None] == jnp.arange(experts, dtype=jnp.int32)).astype(jnp.float32)
    chosen = jnp.sum(onehot, axis=1)
    row_ids = jnp.arange(rows_here)
    earlier = (row_ids[:, None] > row_ids[None, :]).astype(jnp.bfloat16)
    before = jnp.dot(
        earlier, chosen.astype(jnp.bfloat16), preferred_element_type=jnp.float32
    )
    slot = jnp.sum(onehot * before[:, None, :], axis=2)
    return expert_ids.astype(jnp.float32) * SLOT + slot


STEP = 512

F32, BF16 = jnp.float32, jnp.bfloat16
ANY = pl.BlockSpec(memory_space=pl.ANY)
VMEM = pl.BlockSpec(memory_space=pltpu.VMEM)
SMEM = pl.BlockSpec(memory_space=pltpu.SMEM)
PARAMS = pltpu.CompilerParams(vmem_limit_bytes=60 * 1024 * 1024)


def down_copies(sel_ref, wd_ref, wds_ref, sem_ref, first):
    tensors, held, _, span = wds_ref.shape
    copies = []
    for t in range(tensors):
        at = pl.multiple_of(sel_ref[t] + first, 128)
        for j in range(held):
            copies.append(
                pltpu.make_async_copy(
                    wd_ref.at[j, :, pl.ds(at, span)], wds_ref.at[t, j], sem_ref.at[t, j]
                )
            )
    return copies


def down_and_combine(sel_ref, back_ref, act_ref, wds_ref, outs_ref, mixed_ref, groups, tensors):
    held, slots, _ = act_ref.shape
    cores, _, group_slots = back_ref.shape
    span = wds_ref.shape[-1]
    step = min(STEP, span)
    per = slots // groups
    for t in range(tensors):

        @pl.loop(0, span // step)
        def _(n):
            cols = pl.ds(pl.multiple_of(n * step, step), step)
            for j in range(held):
                out = jnp.dot(act_ref[j], wds_ref[t, j, :, cols], preferred_element_type=F32)
                out = out.astype(BF16)
                for g in range(groups):
                    mixed_ref[g, j * per : (j + 1) * per, :] = out[g * per : (g + 1) * per]
            for i in range(cores):
                mixed = mixed_ref[i if groups > 1 else 0]
                rows = jnp.dot(back_ref[i], mixed, preferred_element_type=F32)
                outs_ref[i][t, :, cols] = rows.astype(BF16)


def first_kernel(
    dims, sel_ref, place_ref, back_ref, weight_ref, *rest
):
    cores, tensors, depth, groups, first = dims
    lengths = depth if groups > 1 else 1
    count = cores * tensors * lengths
    pieces, rest = rest[:count], rest[count:]
    wg_ref, wu_ref, wd_ref, act_ref = rest[:4]
    outs_ref = rest[4 : 4 + cores]
    x_ref, s_ref, wgs_ref, wus_ref, wds_ref, mixed_ref, x_sem, w_sem, d_sem = rest[4 + cores :]
    held = wg_ref.shape[0]
    part, cols = pieces[0].shape
    width = x_ref.shape[-1]
    copies = []
    for i in range(cores):
        at = pl.multiple_of(sel_ref[tensors + groups + i], 128)
        for k in range(tensors):
            for o in range(lengths):
                n = (i * tensors + k) * lengths + o
                g, row = (k, o) if groups > 1 else (0, k)
                copies.append(
                    pltpu.make_async_copy(
                        pieces[n],
                        x_ref.at[g, pl.ds(row * part, part), pl.ds(at, cols)],
                        x_sem.at[n],
                    )
                )
    for copy in copies:
        copy.start()
    weights = []
    for j in range(held):
        for n, (src, dst) in enumerate(((wg_ref, wgs_ref), (wu_ref, wus_ref))):
            weights.append(pltpu.make_async_copy(src.at[j], dst.at[j], w_sem.at[n, j]))
    for copy in weights:
        copy.start()
    downs = down_copies(sel_ref, wd_ref, wds_ref, d_sem, first)
    for copy in downs:
        copy.start()
    for copy in copies:
        copy.wait()

    per = s_ref.shape[1] // groups
    step = min(STEP, width)
    for g in range(groups):
        kk = sel_ref[tensors + g]

        @pl.loop(0, width // step)
        def _(n):
            at = pl.ds(pl.multiple_of(n * step, step), step)
            rows = jnp.dot(place_ref[g], x_ref[kk, :, at], preferred_element_type=F32)
            rows = rows.astype(BF16)
            for j in range(held):
                s_ref[j, g * per : (g + 1) * per, at] = rows[j * per : (j + 1) * per]

    @pl.loop(0, held)
    def _(j):
        pltpu.make_async_copy(wg_ref.at[j], wgs_ref.at[j], w_sem.at[0, j]).wait()
        gate = jnp.dot(s_ref[j], wgs_ref[j], preferred_element_type=F32)
        pltpu.make_async_copy(wu_ref.at[j], wus_ref.at[j], w_sem.at[1, j]).wait()
        up = jnp.dot(s_ref[j], wus_ref[j], preferred_element_type=F32)
        value = gate / (1.0 + jnp.exp(-gate)) * up * weight_ref[j]
        act_ref[j] = value.astype(BF16)

    for copy in downs:
        copy.wait()
    down_and_combine(sel_ref, back_ref, act_ref, wds_ref, outs_ref, mixed_ref, groups, tensors)


def later_kernel(dims, sel_ref, back_ref, act_ref, wd_ref, *rest):
    cores, tensors, groups, first = dims
    outs_ref = rest[:cores]
    wds_ref, mixed_ref, d_sem = rest[cores:]
    downs = down_copies(sel_ref, wd_ref, wds_ref, d_sem, first)
    for copy in downs:
        copy.start()
    for copy in downs:
        copy.wait()
    down_and_combine(sel_ref, back_ref, act_ref, wds_ref, outs_ref, mixed_ref, groups, tensors)


def on_device(attn, o_weight, residual, norm_gain, expert_ids, route_weights, w_gate, w_up, w_down):
    cores, tensors, depth = (lax.axis_size(a) for a in ("dp", "tensor", "expert"))
    d, x, z = (lax.axis_index(a) for a in ("dp", "tensor", "expert"))
    rows = attn.shape[0]
    width = norm_gain.shape[0]
    held, _, hidden_units = w_gate.shape
    experts = held * depth * cores
    sub = tensors // cores
    part = rows * cores // tensors
    cols_core = width // cores
    cols_out = width // tensors
    choices = expert_ids.shape[1]

    attn_all = jnp.concatenate([fetch(attn, "dp", i) for i in range(cores)], axis=0)
    res_all = jnp.concatenate([fetch(residual, "dp", i) for i in range(cores)], axis=0)
    partial = jnp.dot(attn_all, o_weight, preferred_element_type=F32)
    res_here = jnp.where(x // sub == d, res_all.astype(F32), 0.0)
    if sub == 1:
        partial = partial + res_here
    else:
        at = (x % sub) * cols_out
        partial = lax.dynamic_update_slice_in_dim(
            partial, lax.dynamic_slice_in_dim(partial, at, cols_out, 1) + res_here, at, 1
        )
    parts = partial.reshape(tensors, part, cols_core)

    def place(p):
        return ((p // sub - d) % cores) * sub + p % sub

    hidden = pick(parts, place(x))
    for k in range(1, tensors):
        sent = pick(parts, place((x - k) % tensors)).astype(BF16)
        hidden = hidden + fetch(sent, "tensor", k).astype(F32)
    hidden = hidden.astype(BF16).astype(F32)
    squares = jnp.sum(hidden * hidden, axis=1, keepdims=True)
    total = squares
    for i in range(1, cores):
        total = total + fetch(squares, "dp", i)
    inverse = lax.rsqrt(total / width + epsilon)
    gain = lax.dynamic_slice_in_dim(norm_gain, d * cols_core, cols_core, 0)
    normed = (hidden * inverse * gain.astype(F32)[None, :]).astype(BF16)

    codes = slot_codes(expert_ids, experts)
    route = jnp.concatenate([codes.T, route_weights.T], axis=0)
    normed, route = lax.optimization_barrier((normed, route))

    along = [fetch(normed, "expert", o) for o in range(depth)]
    if sub > 1:
        along = [jnp.concatenate(along, axis=0)]
    mine = [fetch(v, "tensor", k) for k in range(tensors) for v in along]
    pieces = [fetch(v, "dp", i) for i in range(cores) for v in mine]

    route = jnp.stack([fetch(route, "dp", i) for i in range(cores)])
    route = jnp.stack([fetch(route, "expert", o) for o in range(depth)])
    groups = tensors if sub == 1 else 1
    blocks = depth * cores // groups
    group_slots = held * blocks * SLOT
    local = route[:, :, :choices] - ((z * cores + d) * held * SLOT).astype(F32)
    valid = (local >= 0) & (local < held * SLOT)
    which = jnp.floor(local / SLOT)
    block_ids = jnp.arange(depth, dtype=F32)[:, None, None, None]
    if groups == 1:
        block_ids = block_ids * cores + jnp.arange(cores, dtype=F32)[None, :, None, None]
    slot = which * (blocks * SLOT) + block_ids * SLOT + (local - which * SLOT)
    slot = jnp.where(valid, slot, -1.0)
    weights = route[:, :, choices:]
    by_core = slot.transpose(1, 2, 0, 3).reshape(cores, choices, depth * rows)
    slot_ids = jnp.arange(group_slots, dtype=F32)
    back = jnp.any(by_core[..., None] == slot_ids, axis=1).astype(BF16)
    if groups > 1:
        table = jnp.concatenate([slot, weights], axis=2)
        table = table.transpose(1, 2, 0, 3).reshape(groups, 2 * choices, depth * rows)
    else:
        table = jnp.concatenate([slot, weights], axis=2)
        table = table.reshape(depth, cores, 2 * choices, sub, part)
        table = table.transpose(1, 3, 2, 0, 4).reshape(tensors, 2 * choices, depth * part)
        table = jnp.stack([pick(table, place((x + k) % tensors)) for k in range(tensors)])
        table = table.transpose(1, 0, 2).reshape(1, 2 * choices, -1)
    hit = table[:, :choices, None, :] == slot_ids[None, None, :, None]
    placing = jnp.any(hit, axis=1).astype(BF16)
    slot_weight = jnp.sum(jnp.where(hit, table[:, choices:, None, :], 0.0), axis=(1, 3))
    slot_weight = slot_weight.reshape(groups, held, blocks * SLOT).transpose(1, 0, 2)
    slot_weight = slot_weight.reshape(held, groups * blocks * SLOT, 1)

    starts = [((x + t) % tensors) * cols_out for t in range(tensors)]
    starts += [(d + g - x) % tensors if groups > 1 else d * 0 for g in range(groups)]
    starts += [((d + i) % cores) * cols_core for i in range(cores)]
    sel = jnp.stack(starts).astype(jnp.int32)

    slots = groups * blocks * SLOT
    spans = [cols_out * n // 8 for n in CHUNKS]
    out_rows = depth * rows

    def out_shapes(span):
        return [jax.ShapeDtypeStruct((tensors, out_rows, span), BF16)] * cores

    def scratch(span):
        return [
            pltpu.VMEM((tensors, held, hidden_units, span), BF16),
            pltpu.VMEM((groups, group_slots, min(STEP, span)), BF16),
        ]

    activated, *outs = pl.pallas_call(
        functools.partial(first_kernel, (cores, tensors, depth, groups, 0)),
        out_shape=[jax.ShapeDtypeStruct((held, slots, hidden_units), BF16)] + out_shapes(spans[0]),
        in_specs=[SMEM, VMEM, VMEM, VMEM] + [ANY] * (len(pieces) + 3),
        out_specs=[VMEM] * (1 + cores),
        scratch_shapes=[
            pltpu.VMEM((groups, tensors // groups * depth * part, width), BF16),
            pltpu.VMEM((held, slots, width), BF16),
            pltpu.VMEM(w_gate.shape, BF16),
            pltpu.VMEM(w_up.shape, BF16),
        ]
        + scratch(spans[0])
        + [
            pltpu.SemaphoreType.DMA((len(pieces),)),
            pltpu.SemaphoreType.DMA((2, held)),
            pltpu.SemaphoreType.DMA((tensors, held)),
        ],
        compiler_params=PARAMS,
        name="experts_first",
    )(sel, placing, back, slot_weight, *pieces, w_gate, w_up, w_down)

    results = []
    at = 0
    for n, span in enumerate(spans):
        if n > 0:
            outs = pl.pallas_call(
                functools.partial(later_kernel, (cores, tensors, groups, at)),
                out_shape=out_shapes(span),
                in_specs=[SMEM, VMEM, VMEM, ANY],
                out_specs=[VMEM] * cores,
                scratch_shapes=scratch(span) + [pltpu.SemaphoreType.DMA((tensors, held))],
                compiler_params=PARAMS,
                cost_estimate=pl.CostEstimate(
                    flops=4 * slots * held * hidden_units * span * tensors,
                    bytes_accessed=2 * held * hidden_units * span * tensors,
                    transcendentals=0,
                ),
                name="experts_later",
            )(sel, back, activated, w_down)
        at += span
        summed = outs[0].astype(F32)
        for i in range(1, cores):
            summed = summed + fetch(outs[i], "dp", -i).astype(F32)
        narrow = summed[0]
        for t in range(1, tensors):
            narrow = narrow + fetch(summed[t].astype(BF16), "tensor", -t).astype(F32)
        narrow = narrow.reshape(depth, rows, span)
        result = narrow[0]
        for o in range(1, depth):
            result = result + fetch(narrow[o].astype(BF16), "expert", -o).astype(F32)
        results.append(result.astype(BF16))
    return jnp.concatenate(results, axis=1)


def solution(mesh):
    placed = (
        P(("groups", "expert", "dp"), "tensor"),
        P("tensor", "dp"),
        P(("groups", "expert", "dp"), "tensor"),
        P(),
        P(("groups", "expert", "dp"), None),
        P(("groups", "expert", "dp"), None),
        P(("expert", "dp"), None, "tensor"),
        P(("expert", "dp"), None, "tensor"),
        P(("expert", "dp"), "tensor", None),
    )
    return jax.shard_map(
        on_device,
        mesh=mesh,
        in_specs=placed,
        out_specs=P(("groups", "expert", "dp"), "tensor"),
        check_vma=False,
    )
```

time: 423 us -> 155 us (0.37)
  blocking collectives: 219 us -> 0 us
  waiting for transfers between devices: 140 us -> 62.9 us
  Pallas kernels: 0 us -> 42.3 us
  matrix products: 44.9 us -> 4.84 us
  starting transfers between devices: 0.08 us -> 31.8 us
  between operations: 13.2 us -> 0.42 us
  other arithmetic: 2.34 us -> 9.55 us
    all_to_all x2 -> x0, blocking collectives: 219 us -> none  [the longest x1 143 us: on_device(): lax.all_to_all(outgoing, ('expert', 'dp'), split_axis=0, concat_axis=0, t...]
    reduce_scatter x1 -> x0, waiting for transfers between devices: 75.3 us -> none  [on_device(): lax.psum_scatter(partials.astype(jnp.bfloat16), 'tensor', scatter_dimensi...]
    ppermute x0 -> x33, waiting for transfers between devices: none -> 62.9 us  [fetch(): lax.ppermute(value, axis, [((i + step) % size, i) for i in range(size)])]
    pallas_call x0 -> x2, Pallas kernels: none -> 42.3 us  [the longest x1 32.6 us: on_device(): pl.pallas_call(functools.partial(first_kernel, (cores, tensors, depth, gr...]
    dot_general x7 -> x2, matrix products: 44.9 us -> 4.84 us  [the longest x1 4.71 us: on_device(): partial = jnp.dot(attn_all, o_weight, preferred_element_type=F32)]
    all_gather x1 -> x0, waiting for transfers between devices: 34.3 us -> none  [on_device(): lax.all_gather(o_weight, 'dp', axis=1, tiled=True)]
    ppermute x0 -> x33, starting transfers between devices: none -> 31.8 us  [fetch(): lax.ppermute(value, axis, [((i + step) % size, i) for i in range(size)])]
    psum x1 -> x0, waiting for transfers between devices: 29.7 us -> none  [on_device(): summed = lax.psum(partial_value.astype(jnp.bfloat16), 'tensor')]
  transfers between devices with their start and end apart: 3 -> 33, of which waited for: 3 -> 14; matrix products, arithmetic and copies ran while one was open for 0% -> 7% of each run, Pallas kernels for 0% -> 6%
where the time goes in v1:
time: 155 us
  waiting for transfers between devices  62.9 us (41%)
  Pallas kernels  42.3 us (27%)
  starting transfers between devices  31.8 us (21%)
  other arithmetic  9.55 us (6%)
  matrix products  4.84 us (3%)
  local copies, waits for them, and re-layouts  2.86 us (2%)
    ppermute x33, waiting for transfers between devices, fetch(): lax.ppermute(value, axis, [((i + step) % size, i) for i in range(size)])  62.9 us
    pallas_call x1, Pallas kernels, on_device(): pl.pallas_call(functools.partial(first_kernel, (cores, tensors, depth, gr...  32.6 us
    ppermute x33, starting transfers between devices, fetch(): lax.ppermute(value, axis, [((i + step) % size, i) for i in range(size)])  31.8 us
    pallas_call x1, Pallas kernels, on_device(): pl.pallas_call(functools.partial(later_kernel, (cores, tensors, groups, a...  9.66 us
    dot_general x1, matrix products, on_device(): partial = jnp.dot(attn_all, o_weight, preferred_element_type=F32)  4.71 us
  transfers between devices with their start and end apart: 33, of which 14 were waited for; matrix products, arithmetic and copies ran while one was open for 7% of the time, Pallas kernels for 6%

profile of v1, /device:TPU:0, one launch (start us, length us, event | category | flops | bytes accessed | tf_op | source)
XLA Modules:
  0.0 154.7 jit_solution(15576310081099609713)
XLA Ops:
  2.2 4.7 %convolution_add_fusion = f32[128,2048]{1,0:T(8,128)S(1)} fusion(bf16[2048,2048]{1,0:T(8,128)(2,1)} %param.10, bf16[64,2048]{1,0:T(8,128)(2,1)S(1)} %collective-permute-done, bf16[64,2048]{1,0:T(8,128)(2,1)} %param.9, bf16[64,2048]{1,0:T(8,128)(2,1)S(1)} %collective-permute-done.1, bf16[64,2048]{1,0:T(8,128)(2,1)} %param.11, pred[]{:T(512)S(6)} %eq.56), kind=kOutput, calls=%fused_computation.5 | convolution fusion | flops 1076363264 | bytes 10485761 | tf_op jit(solution)/shard_map/dot_general | solution.py:181
  7.0 2.9 %collective-permute-start.2 = (bf16[64,2048]{1,0:T(8,128)(2,1)S(1)}, bf16[64,2048]{1,0:T(8,128)(2,1)S(1)}, u32[]{:S(2)}, u32[]{:S(2)}) collective-permute-start(bf16[64,2048]{1,0:T(8,128)(2,1)S(1)} %fusion.13), channel_id=1, source_target_pairs={{2,0},{0,2},{3,1},{1,3},{6,4},{4,6},{7,5},{5,7},{10,8},{8,10},{11,... | collective-permute-start | bytes 786440 | tf_op jit(solution)/shard_map/ppermute | solution.py:21
  10.0 6.6 %collective-permute-done.2 = bf16[64,2048]{1,0:T(8,128)(2,1)S(1)} collective-permute-done((bf16[64,2048]{1,0:T(8,128)(2,1)S(1)}, bf16[64,2048]{1,0:T(8,128)(2,1)S(1)}, u32[]{:S(2)}, u32[]{:S(2)}) %collective-permute-start.2) | collective-permute-done | bytes 262176 | tf_op jit(solution)/shard_map/ppermute | solution.py:21
  16.8 1.1 collective-permute-done.3
  18.3 1.0 collective-permute-done.4
  19.3 2.8 %collective-permute-start.6 = (f32[2,16,64]{2,1,0:T(8,128)S(1)}, f32[2,16,64]{2,1,0:T(8,128)S(1)}, u32[]{:S(2)}, u32[]{:S(2)}) collective-permute-start(f32[2,16,64]{2,1,0:T(8,128)S(1)} %get-tuple-element.36), channel_id=1, source_target_pairs={{8,0},{12,4},{0,8},{4,12},{9,1},{13,5},{1,9},{5,13},{10,2},{14,6},... | collective-permute-start | bytes 24584 | tf_op jit(solution)/shard_map/ppermute | solution.py:21
  22.2 1.3 collective-permute-start.5
  24.8 1.5 collective-permute-start.11
  26.3 1.6 %collective-permute-start.10 = (bf16[64,2048]{1,0:T(8,128)(2,1)S(1)}, bf16[64,2048]{1,0:T(8,128)(2,1)S(1)}, u32[]{:S(2)}, u32[]{:S(2)}) collective-permute-start(bf16[64,2048]{1,0:T(8,128)(2,1)S(1)} %fusion.6.rest_0_), channel_id=1, source_target_pairs={{12,0},{0,4},{4,8},{8,12},{13,1},{1,5},{5,9},{9,13},{14,2},{2,6},{... | collective-permute-start | bytes 786440 | tf_op jit(solution)/shard_map/ppermute | solution.py:21
  27.9 2.1 %collective-permute-start.9 = (bf16[64,2048]{1,0:T(8,128)(2,1)S(1)}, bf16[64,2048]{1,0:T(8,128)(2,1)S(1)}, u32[]{:S(2)}, u32[]{:S(2)}) collective-permute-start(bf16[64,2048]{1,0:T(8,128)(2,1)S(1)} %fusion.6.rest_0_), channel_id=1, source_target_pairs={{8,0},{12,4},{0,8},{4,12},{9,1},{13,5},{1,9},{5,13},{10,2},{14,6},... | collective-permute-start | bytes 786440 | tf_op jit(solution)/shard_map/ppermute | solution.py:21
  30.8 6.7 %collective-permute-done.10.rest_3_ = bf16[64,2048]{1,0:T(8,128)(2,1)S(1)} collective-permute-done((bf16[64,2048]{1,0:T(8,128)(2,1)S(1)}, bf16[64,2048]{1,0:T(8,128)(2,1)S(1)}, u32[]{:S(2)}, u32[]{:S(2)}) %collective-permute-start.10) | collective-permute-done | bytes 262176 | tf_op jit(solution)/shard_map/ppermute | solution.py:21
  38.2 9.7 %collective-permute-done.9.rest_2_ = bf16[64,2048]{1,0:T(8,128)(2,1)S(1)} collective-permute-done((bf16[64,2048]{1,0:T(8,128)(2,1)S(1)}, bf16[64,2048]{1,0:T(8,128)(2,1)S(1)}, u32[]{:S(2)}, u32[]{:S(2)}) %collective-permute-start.9) | collective-permute-done | bytes 262176 | tf_op jit(solution)/shard_map/ppermute | solution.py:21
  48.5 1.5 collective-permute-start.12
  51.4 5.7 %collective-permute-done.13.rest_6_ = bf16[64,2048]{1,0:T(8,128)(2,1)S(1)} collective-permute-done((bf16[64,2048]{1,0:T(8,128)(2,1)S(1)}, bf16[64,2048]{1,0:T(8,128)(2,1)S(1)}, u32[]{:S(2)}, u32[]{:S(2)}) %collective-permute-start.13) | collective-permute-done | bytes 262176 | tf_op jit(solution)/shard_map/ppermute | solution.py:21
  57.1 4.6 %collective-permute-done.12.rest_5_ = bf16[64,2048]{1,0:T(8,128)(2,1)S(1)} collective-permute-done((bf16[64,2048]{1,0:T(8,128)(2,1)S(1)}, bf16[64,2048]{1,0:T(8,128)(2,1)S(1)}, u32[]{:S(2)}, u32[]{:S(2)}) %collective-permute-start.12) | collective-permute-done | bytes 262176 | tf_op jit(solution)/shard_map/ppermute | solution.py:21
  61.7 1.0 fusion.1
  63.6 1.0 fusion
  64.6 0.8 convert_element_type.111.place_ref
  65.5 1.0 reshape.48.weight_ref
  67.2 32.6 %experts_first.1 = (bf16[4,192,512]{2,1,0:T(8,128)(2,1)}, bf16[2,256,1024]{2,1,0:T(8,128)(2,1)}, bf16[2,256,1024]{2,1,0:T(8,128)(2,1)}) custom-call(s32[6]{0:T(128)} %stack.51.sel_ref, bf16[2,384,256]{2,1,0:T(8,128)(2,1)} %convert_element_type.111.place_ref, bf16[2,256,384]{2,1,0:T(8,128)(2,1)} %convert_element_type.112.back_ref, ...), custom_call_target="tpu_custom_call" | custom-call | tf_op jit(solution)/shard_map/experts_first/pallas_call | solution.py:268
  100.5 9.7 %experts_later.1 = (bf16[2,256,1024]{2,1,0:T(8,128)(2,1)}, bf16[2,256,1024]{2,1,0:T(8,128)(2,1)}) custom-call(s32[6]{0:T(128)} %stack.51.sel_ref, bf16[2,256,384]{2,1,0:T(8,128)(2,1)} %convert_element_type.112.back_ref, bf16[4,192,512]{2,1,0:T(8,128)(2,1)} %get-tuple-element.16.act_ref, bf16[4,512,4096]{2,1,0:T(8,128)(2,1)} %wd_ref.1), custom_call_target="tpu_custom_call" | custom-call | flops 3221225472 | bytes 8388608 | tf_op jit(solution)/shard_map/experts_later/pallas_call | solution.py:293
  111.3 1.8 %collective-permute-done.28 = bf16[2,256,1024]{2,1,0:T(8,128)(2,1)S(1)} collective-permute-done((bf16[2,256,1024]{2,1,0:T(8,128)(2,1)}, bf16[2,256,1024]{2,1,0:T(8,128)(2,1)S(1)}, u32[]{:S(2)}, u32[]{:S(2)}) %collective-permute-start.28) | collective-permute-done | bytes 1048608 | tf_op jit(solution)/shard_map/ppermute | solution.py:21
  113.1 1.6 %convert_add_fusion = f32[2,256,1024]{2,1,0:T(8,128)S(1)} fusion(bf16[2,256,1024]{2,1,0:T(8,128)(2,1)S(1)} %collective-permute-done.28, bf16[2,256,1024]{2,1,0:T(8,128)(2,1)} %get-tuple-element.17), kind=kLoop, calls=%fused_computation.6 | loop fusion | flops 1572864 | bytes 4194304 | tf_op jit(solution)/shard_map/add | solution.py:310
  115.3 10.2 %collective-permute-done.24 = bf16[256,1024]{1,0:T(8,128)(2,1)S(1)} collective-permute-done((bf16[256,1024]{1,0:T(8,128)(2,1)S(1)}, bf16[256,1024]{1,0:T(8,128)(2,1)S(1)}, u32[]{:S(2)}, u32[]{:S(2)}) %collective-permute-start.24) | collective-permute-done | bytes 524320 | tf_op jit(solution)/shard_map/ppermute | solution.py:21
  125.8 2.8 %collective-permute-start.25 = (bf16[64,1024]{1,0:T(8,128)(2,1)S(1)}, bf16[64,1024]{1,0:T(8,128)(2,1)S(1)}, u32[]{:S(2)}, u32[]{:S(2)}) collective-permute-start(bf16[64,1024]{1,0:T(8,128)(2,1)S(1)} %get-tuple-element.25), channel_id=1, source_target_pairs={{12,0},{0,4},{4,8},{8,12},{13,1},{1,5},{5,9},{9,13},{14,2},{2,6},{... | collective-permute-start | bytes 393224 | tf_op jit(solution)/shard_map/ppermute | solution.py:21
  128.6 2.9 %collective-permute-start.27 = (bf16[64,1024]{1,0:T(8,128)(2,1)S(1)}, bf16[64,1024]{1,0:T(8,128)(2,1)S(1)}, u32[]{:S(2)}, u32[]{:S(2)}) collective-permute-start(bf16[64,1024]{1,0:T(8,128)(2,1)S(1)} %get-tuple-element.26), channel_id=1, source_target_pairs={{4,0},{8,4},{12,8},{0,12},{5,1},{9,5},{13,9},{1,13},{6,2},{10,6},{... | collective-permute-start | bytes 393224 | tf_op jit(solution)/shard_map/ppermute | solution.py:21
  132.0 4.3 %collective-permute-done.29 = bf16[256,1024]{1,0:T(8,128)(2,1)S(1)} collective-permute-done((bf16[256,1024]{1,0:T(8,128)(2,1)S(1)}, bf16[256,1024]{1,0:T(8,128)(2,1)S(1)}, u32[]{:S(2)}, u32[]{:S(2)}) %collective-permute-start.29) | collective-permute-done | bytes 524320 | tf_op jit(solution)/shard_map/ppermute | solution.py:21
  136.6 2.8 %collective-permute-start.30 = (bf16[64,1024]{1,0:T(8,128)(2,1)S(1)}, bf16[64,1024]{1,0:T(8,128)(2,1)S(1)}, u32[]{:S(2)}, u32[]{:S(2)}) collective-permute-start(bf16[64,1024]{1,0:T(8,128)(2,1)S(1)} %get-tuple-element.28), channel_id=1, source_target_pairs={{12,0},{0,4},{4,8},{8,12},{13,1},{1,5},{5,9},{9,13},{14,2},{2,6},{... | collective-permute-start | bytes 393224 | tf_op jit(solution)/shard_map/ppermute | solution.py:21
  139.4 2.9 %collective-permute-start.32 = (bf16[64,1024]{1,0:T(8,128)(2,1)S(1)}, bf16[64,1024]{1,0:T(8,128)(2,1)S(1)}, u32[]{:S(2)}, u32[]{:S(2)}) collective-permute-start(bf16[64,1024]{1,0:T(8,128)(2,1)S(1)} %get-tuple-element.29), channel_id=1, source_target_pairs={{4,0},{8,4},{12,8},{0,12},{5,1},{9,5},{13,9},{1,13},{6,2},{10,6},{... | collective-permute-start | bytes 393224 | tf_op jit(solution)/shard_map/ppermute | solution.py:21
  142.8 3.7 %collective-permute-done.30 = bf16[64,1024]{1,0:T(8,128)(2,1)S(1)} collective-permute-done((bf16[64,1024]{1,0:T(8,128)(2,1)S(1)}, bf16[64,1024]{1,0:T(8,128)(2,1)S(1)}, u32[]{:S(2)}, u32[]{:S(2)}) %collective-permute-start.30) | collective-permute-done | bytes 131104 | tf_op jit(solution)/shard_map/ppermute | solution.py:21
  146.5 1.7 %collective-permute-done.32 = bf16[64,1024]{1,0:T(8,128)(2,1)S(1)} collective-permute-done((bf16[64,1024]{1,0:T(8,128)(2,1)S(1)}, bf16[64,1024]{1,0:T(8,128)(2,1)S(1)}, u32[]{:S(2)}, u32[]{:S(2)}) %collective-permute-start.32) | collective-permute-done | bytes 131104 | tf_op jit(solution)/shard_map/ppermute | solution.py:21
  148.3 5.6 %collective-permute-done.31 = bf16[64,1024]{1,0:T(8,128)(2,1)S(1)} collective-permute-done((bf16[64,1024]{1,0:T(8,128)(2,1)S(1)}, bf16[64,1024]{1,0:T(8,128)(2,1)S(1)}, u32[]{:S(2)}, u32[]{:S(2)}) %collective-permute-start.31) | collective-permute-done | bytes 131104 | tf_op jit(solution)/shard_map/ppermute | solution.py:21
  (109 shorter events, 13.8 us)
Async XLA Ops:
  0.0 2.1 %collective-permute-start = (bf16[64,2048]{1,0:T(8,128)(2,1)}, bf16[64,2048]{1,0:T(8,128)(2,1)S(1)}, u32[]{:S(2)}, u32[]{:S(2)}) collective-permute-start(bf16[64,2048]{1,0:T(8,128)(2,1)} %param.9), channel_id=1, source_target_pairs={{1,0},{0,1},{3,2},{2,3},{5,4},{4,5},{7,6},{6,7},{9,8},{8,9},{11,10... | collective-permute-start | bytes 786440 | tf_op jit(solution)/shard_map/ppermute | solution.py:21
  0.5 1.7 %collective-permute-start.1 = (bf16[64,2048]{1,0:T(8,128)(2,1)}, bf16[64,2048]{1,0:T(8,128)(2,1)S(1)}, u32[]{:S(2)}, u32[]{:S(2)}) collective-permute-start(bf16[64,2048]{1,0:T(8,128)(2,1)} %param.11), channel_id=1, source_target_pairs={{1,0},{0,1},{3,2},{2,3},{5,4},{4,5},{7,6},{6,7},{9,8},{8,9},{11,10... | collective-permute-start | bytes 786440 | tf_op jit(solution)/shard_map/ppermute | solution.py:21
  7.0 9.5 %collective-permute-start.2 = (bf16[64,2048]{1,0:T(8,128)(2,1)S(1)}, bf16[64,2048]{1,0:T(8,128)(2,1)S(1)}, u32[]{:S(2)}, u32[]{:S(2)}) collective-permute-start(bf16[64,2048]{1,0:T(8,128)(2,1)S(1)} %fusion.13), channel_id=1, source_target_pairs={{2,0},{0,2},{3,1},{1,3},{6,4},{4,6},{7,5},{5,7},{10,8},{8,10},{11,... | collective-permute-start | bytes 786440 | tf_op jit(solution)/shard_map/ppermute | solution.py:21
  18.1 1.2 collective-permute-start.4
  19.3 7.0 %collective-permute-start.6 = (f32[2,16,64]{2,1,0:T(8,128)S(1)}, f32[2,16,64]{2,1,0:T(8,128)S(1)}, u32[]{:S(2)}, u32[]{:S(2)}) collective-permute-start(f32[2,16,64]{2,1,0:T(8,128)S(1)} %get-tuple-element.36), channel_id=1, source_target_pairs={{8,0},{12,4},{0,8},{4,12},{9,1},{13,5},{1,9},{5,13},{10,2},{14,6},... | collective-permute-start | bytes 24584 | tf_op jit(solution)/shard_map/ppermute | solution.py:21
  22.2 5.7 %collective-permute-start.5 = (f32[2,16,64]{2,1,0:T(8,128)S(1)}, f32[2,16,64]{2,1,0:T(8,128)S(1)}, u32[]{:S(2)}, u32[]{:S(2)}) collective-permute-start(f32[2,16,64]{2,1,0:T(8,128)S(1)} %get-tuple-element.36), channel_id=1, source_target_pairs={{4,0},{8,4},{12,8},{0,12},{5,1},{9,5},{13,9},{1,13},{6,2},{10,6},{... | collective-permute-start | bytes 24584 | tf_op jit(solution)/shard_map/ppermute | solution.py:21
  23.5 6.5 %collective-permute-start.7 = (f32[2,16,64]{2,1,0:T(8,128)S(1)}, f32[2,16,64]{2,1,0:T(8,128)S(1)}, u32[]{:S(2)}, u32[]{:S(2)}) collective-permute-start(f32[2,16,64]{2,1,0:T(8,128)S(1)} %get-tuple-element.36), channel_id=1, source_target_pairs={{12,0},{0,4},{4,8},{8,12},{13,1},{1,5},{5,9},{9,13},{14,2},{2,6},{... | collective-permute-start | bytes 24584 | tf_op jit(solution)/shard_map/ppermute | solution.py:21
  24.8 12.6 %collective-permute-start.15 = (bf16[64,2048]{1,0:T(8,128)(2,1)S(1)}, bf16[64,2048]{1,0:T(8,128)(2,1)S(1)}, u32[]{:S(2)}, u32[]{:S(2)}) collective-permute-start(bf16[64,2048]{1,0:T(8,128)(2,1)S(1)} %fusion.6.rest_0_), channel_id=1, source_target_pairs={{1,0},{0,1},{3,2},{2,3},{5,4},{4,5},{7,6},{6,7},{9,8},{8,9},{11,10... | collective-permute-start | bytes 786440 | tf_op jit(solution)/shard_map/ppermute | solution.py:21
  24.8 13.2 %collective-permute-start.11 = (bf16[64,2048]{1,0:T(8,128)(2,1)S(1)}, bf16[64,2048]{1,0:T(8,128)(2,1)S(1)}, u32[]{:S(2)}, u32[]{:S(2)}) collective-permute-start(bf16[64,2048]{1,0:T(8,128)(2,1)S(1)} %fusion.6.rest_0_), channel_id=1, source_target_pairs={{2,0},{0,2},{3,1},{1,3},{6,4},{4,6},{7,5},{5,7},{10,8},{8,10},{11,... | collective-permute-start | bytes 786440 | tf_op jit(solution)/shard_map/ppermute | solution.py:21
  26.3 11.1 %collective-permute-start.10 = (bf16[64,2048]{1,0:T(8,128)(2,1)S(1)}, bf16[64,2048]{1,0:T(8,128)(2,1)S(1)}, u32[]{:S(2)}, u32[]{:S(2)}) collective-permute-start(bf16[64,2048]{1,0:T(8,128)(2,1)S(1)} %fusion.6.rest_0_), channel_id=1, source_target_pairs={{12,0},{0,4},{4,8},{8,12},{13,1},{1,5},{5,9},{9,13},{14,2},{2,6},{... | collective-permute-start | bytes 786440 | tf_op jit(solution)/shard_map/ppermute | solution.py:21
  27.9 20.0 %collective-permute-start.9 = (bf16[64,2048]{1,0:T(8,128)(2,1)S(1)}, bf16[64,2048]{1,0:T(8,128)(2,1)S(1)}, u32[]{:S(2)}, u32[]{:S(2)}) collective-permute-start(bf16[64,2048]{1,0:T(8,128)(2,1)S(1)} %fusion.6.rest_0_), channel_id=1, source_target_pairs={{8,0},{12,4},{0,8},{4,12},{9,1},{13,5},{1,9},{5,13},{10,2},{14,6},... | collective-permute-start | bytes 786440 | tf_op jit(solution)/shard_map/ppermute | solution.py:21
  30.0 18.4 %collective-permute-start.8 = (bf16[64,2048]{1,0:T(8,128)(2,1)S(1)}, bf16[64,2048]{1,0:T(8,128)(2,1)S(1)}, u32[]{:S(2)}, u32[]{:S(2)}) collective-permute-start(bf16[64,2048]{1,0:T(8,128)(2,1)S(1)} %fusion.6.rest_0_), channel_id=1, source_target_pairs={{4,0},{8,4},{12,8},{0,12},{5,1},{9,5},{13,9},{1,13},{6,2},{10,6},{... | collective-permute-start | bytes 786440 | tf_op jit(solution)/shard_map/ppermute | solution.py:21
  37.4 13.4 %collective-permute-start.18 = (bf16[64,2048]{1,0:T(8,128)(2,1)S(1)}, bf16[64,2048]{1,0:T(8,128)(2,1)S(1)}, u32[]{:S(2)}, u32[]{:S(2)}) collective-permute-start(bf16[64,2048]{1,0:T(8,128)(2,1)S(1)} %collective-permute-done.10.rest_3_), channel_id=1, source_target_pairs={{1,0},{0,1},{3,2},{2,3},{5,4},{4,5},{7,6},{6,7},{9,8},{8,9},{11,10... | collective-permute-start | bytes 786440 | tf_op jit(solution)/shard_map/ppermute | solution.py:21
  37.5 13.8 %collective-permute-start.14 = (bf16[64,2048]{1,0:T(8,128)(2,1)S(1)}, bf16[64,2048]{1,0:T(8,128)(2,1)S(1)}, u32[]{:S(2)}, u32[]{:S(2)}) collective-permute-start(bf16[64,2048]{1,0:T(8,128)(2,1)S(1)} %collective-permute-done.10.rest_3_), channel_id=1, source_target_pairs={{2,0},{0,2},{3,1},{1,3},{6,4},{4,6},{7,5},{5,7},{10,8},{8,10},{11,... | collective-permute-start | bytes 786440 | tf_op jit(solution)/shard_map/ppermute | solution.py:21
  38.1 12.6 %collective-permute-start.19 = (bf16[64,2048]{1,0:T(8,128)(2,1)S(1)}, bf16[64,2048]{1,0:T(8,128)(2,1)S(1)}, u32[]{:S(2)}, u32[]{:S(2)}) collective-permute-start(bf16[64,2048]{1,0:T(8,128)(2,1)S(1)} %collective-permute-done.11.rest_4_), channel_id=1, source_target_pairs={{1,0},{0,1},{3,2},{2,3},{5,4},{4,5},{7,6},{6,7},{9,8},{8,9},{11,10... | collective-permute-start | bytes 786440 | tf_op jit(solution)/shard_map/ppermute | solution.py:21
  47.9 9.2 %collective-permute-start.13 = (bf16[64,2048]{1,0:T(8,128)(2,1)S(1)}, bf16[64,2048]{1,0:T(8,128)(2,1)S(1)}, u32[]{:S(2)}, u32[]{:S(2)}) collective-permute-start(bf16[64,2048]{1,0:T(8,128)(2,1)S(1)} %collective-permute-done.9.rest_2_), channel_id=1, source_target_pairs={{2,0},{0,2},{3,1},{1,3},{6,4},{4,6},{7,5},{5,7},{10,8},{8,10},{11,... | collective-permute-start | bytes 786440 | tf_op jit(solution)/shard_map/ppermute | solution.py:21
  48.5 13.2 %collective-permute-start.12 = (bf16[64,2048]{1,0:T(8,128)(2,1)S(1)}, bf16[64,2048]{1,0:T(8,128)(2,1)S(1)}, u32[]{:S(2)}, u32[]{:S(2)}) collective-permute-start(bf16[64,2048]{1,0:T(8,128)(2,1)S(1)} %collective-permute-done.8.rest_1_), channel_id=1, source_target_pairs={{2,0},{0,2},{3,1},{1,3},{6,4},{4,6},{7,5},{5,7},{10,8},{8,10},{11,... | collective-permute-start | bytes 786440 | tf_op jit(solution)/shard_map/ppermute | solution.py:21
  50.7 15.8 %collective-permute-start.17 = (bf16[64,2048]{1,0:T(8,128)(2,1)S(1)}, bf16[64,2048]{1,0:T(8,128)(2,1)S(1)}, u32[]{:S(2)}, u32[]{:S(2)}) collective-permute-start(bf16[64,2048]{1,0:T(8,128)(2,1)S(1)} %collective-permute-done.9.rest_2_), channel_id=1, source_target_pairs={{1,0},{0,1},{3,2},{2,3},{5,4},{4,5},{7,6},{6,7},{9,8},{8,9},{11,10... | collective-permute-start | bytes 786440 | tf_op jit(solution)/shard_map/ppermute | solution.py:21
  50.8 15.7 %collective-permute-start.16 = (bf16[64,2048]{1,0:T(8,128)(2,1)S(1)}, bf16[64,2048]{1,0:T(8,128)(2,1)}, u32[]{:S(2)}, u32[]{:S(2)}) collective-permute-start(bf16[64,2048]{1,0:T(8,128)(2,1)S(1)} %collective-permute-done.8.rest_1_), channel_id=1, source_target_pairs={{1,0},{0,1},{3,2},{2,3},{5,4},{4,5},{7,6},{6,7},{9,8},{8,9},{11,10... | collective-permute-start | bytes 786440 | tf_op jit(solution)/shard_map/ppermute | solution.py:21
  51.3 15.2 %collective-permute-start.22 = (bf16[64,2048]{1,0:T(8,128)(2,1)S(1)}, bf16[64,2048]{1,0:T(8,128)(2,1)}, u32[]{:S(2)}, u32[]{:S(2)}) collective-permute-start(bf16[64,2048]{1,0:T(8,128)(2,1)S(1)} %collective-permute-done.14.rest_7_), channel_id=1, source_target_pairs={{1,0},{0,1},{3,2},{2,3},{5,4},{4,5},{7,6},{6,7},{9,8},{8,9},{11,10... | collective-permute-start | bytes 786440 | tf_op jit(solution)/shard_map/ppermute | solution.py:21
  57.1 9.4 %collective-permute-start.21 = (bf16[64,2048]{1,0:T(8,128)(2,1)S(1)}, bf16[64,2048]{1,0:T(8,128)(2,1)}, u32[]{:S(2)}, u32[]{:S(2)}) collective-permute-start(bf16[64,2048]{1,0:T(8,128)(2,1)S(1)} %collective-permute-done.13.rest_6_), channel_id=1, source_target_pairs={{1,0},{0,1},{3,2},{2,3},{5,4},{4,5},{7,6},{6,7},{9,8},{8,9},{11,10... | collective-permute-start | bytes 786440 | tf_op jit(solution)/shard_map/ppermute | solution.py:21
  61.7 4.8 %collective-permute-start.20 = (bf16[64,2048]{1,0:T(8,128)(2,1)S(1)}, bf16[64,2048]{1,0:T(8,128)(2,1)}, u32[]{:S(2)}, u32[]{:S(2)}) collective-permute-start(bf16[64,2048]{1,0:T(8,128)(2,1)S(1)} %collective-permute-done.12.rest_5_), channel_id=1, source_target_pairs={{1,0},{0,1},{3,2},{2,3},{5,4},{4,5},{7,6},{6,7},{9,8},{8,9},{11,10... | collective-permute-start | bytes 786440 | tf_op jit(solution)/shard_map/ppermute | solution.py:21
  99.9 10.4 %collective-permute-start.23 = (bf16[2,256,1024]{2,1,0:T(8,128)(2,1)}, bf16[2,256,1024]{2,1,0:T(8,128)(2,1)S(1)}, u32[]{:S(2)}, u32[]{:S(2)}) collective-permute-start(bf16[2,256,1024]{2,1,0:T(8,128)(2,1)} %get-tuple-element.15), channel_id=1, source_target_pairs={{1,0},{0,1},{3,2},{2,3},{5,4},{4,5},{7,6},{6,7},{9,8},{8,9},{11,10... | collective-permute-start | bytes 3145736 | tf_op jit(solution)/shard_map/ppermute | solution.py:21
  110.1 2.9 %collective-permute-start.28 = (bf16[2,256,1024]{2,1,0:T(8,128)(2,1)}, bf16[2,256,1024]{2,1,0:T(8,128)(2,1)S(1)}, u32[]{:S(2)}, u32[]{:S(2)}) collective-permute-start(bf16[2,256,1024]{2,1,0:T(8,128)(2,1)} %get-tuple-element.18), channel_id=1, source_target_pairs={{1,0},{0,1},{3,2},{2,3},{5,4},{4,5},{7,6},{6,7},{9,8},{8,9},{11,10... | collective-permute-start | bytes 3145736 | tf_op jit(solution)/shard_map/ppermute | solution.py:21
  110.7 14.9 %collective-permute-start.24 = (bf16[256,1024]{1,0:T(8,128)(2,1)S(1)}, bf16[256,1024]{1,0:T(8,128)(2,1)S(1)}, u32[]{:S(2)}, u32[]{:S(2)}) collective-permute-start(bf16[256,1024]{1,0:T(8,128)(2,1)S(1)} %fusion.7), channel_id=1, source_target_pairs={{2,0},{0,2},{3,1},{1,3},{6,4},{4,6},{7,5},{5,7},{10,8},{8,10},{11,... | collective-permute-start | bytes 1572872 | tf_op jit(solution)/shard_map/ppermute | solution.py:21
  114.8 21.6 %collective-permute-start.29 = (bf16[256,1024]{1,0:T(8,128)(2,1)S(1)}, bf16[256,1024]{1,0:T(8,128)(2,1)S(1)}, u32[]{:S(2)}, u32[]{:S(2)}) collective-permute-start(bf16[256,1024]{1,0:T(8,128)(2,1)S(1)} %fusion.8), channel_id=1, source_target_pairs={{2,0},{0,2},{3,1},{1,3},{6,4},{4,6},{7,5},{5,7},{10,8},{8,10},{11,... | collective-permute-start | bytes 1572872 | tf_op jit(solution)/shard_map/ppermute | solution.py:21
  125.8 16.4 %collective-permute-start.25 = (bf16[64,1024]{1,0:T(8,128)(2,1)S(1)}, bf16[64,1024]{1,0:T(8,128)(2,1)S(1)}, u32[]{:S(2)}, u32[]{:S(2)}) collective-permute-start(bf16[64,1024]{1,0:T(8,128)(2,1)S(1)} %get-tuple-element.25), channel_id=1, source_target_pairs={{12,0},{0,4},{4,8},{8,12},{13,1},{1,5},{5,9},{9,13},{14,2},{2,6},{... | collective-permute-start | bytes 393224 | tf_op jit(solution)/shard_map/ppermute | solution.py:21
  128.6 14.1 %collective-permute-start.27 = (bf16[64,1024]{1,0:T(8,128)(2,1)S(1)}, bf16[64,1024]{1,0:T(8,128)(2,1)S(1)}, u32[]{:S(2)}, u32[]{:S(2)}) collective-permute-start(bf16[64,1024]{1,0:T(8,128)(2,1)S(1)} %get-tuple-element.26), channel_id=1, source_target_pairs={{4,0},{8,4},{12,8},{0,12},{5,1},{9,5},{13,9},{1,13},{6,2},{10,6},{... | collective-permute-start | bytes 393224 | tf_op jit(solution)/shard_map/ppermute | solution.py:21
  131.5 11.3 %collective-permute-start.26 = (bf16[64,1024]{1,0:T(8,128)(2,1)S(1)}, bf16[64,1024]{1,0:T(8,128)(2,1)S(1)}, u32[]{:S(2)}, u32[]{:S(2)}) collective-permute-start(bf16[64,1024]{1,0:T(8,128)(2,1)S(1)} %get-tuple-element.27), channel_id=1, source_target_pairs={{8,0},{12,4},{0,8},{4,12},{9,1},{13,5},{1,9},{5,13},{10,2},{14,6},... | collective-permute-start | bytes 393224 | tf_op jit(solution)/shard_map/ppermute | solution.py:21
  136.6 10.0 %collective-permute-start.30 = (bf16[64,1024]{1,0:T(8,128)(2,1)S(1)}, bf16[64,1024]{1,0:T(8,128)(2,1)S(1)}, u32[]{:S(2)}, u32[]{:S(2)}) collective-permute-start(bf16[64,1024]{1,0:T(8,128)(2,1)S(1)} %get-tuple-element.28), channel_id=1, source_target_pairs={{12,0},{0,4},{4,8},{8,12},{13,1},{1,5},{5,9},{9,13},{14,2},{2,6},{... | collective-permute-start | bytes 393224 | tf_op jit(solution)/shard_map/ppermute | solution.py:21
  139.4 8.9 %collective-permute-start.32 = (bf16[64,1024]{1,0:T(8,128)(2,1)S(1)}, bf16[64,1024]{1,0:T(8,128)(2,1)S(1)}, u32[]{:S(2)}, u32[]{:S(2)}) collective-permute-start(bf16[64,1024]{1,0:T(8,128)(2,1)S(1)} %get-tuple-element.29), channel_id=1, source_target_pairs={{4,0},{8,4},{12,8},{0,12},{5,1},{9,5},{13,9},{1,13},{6,2},{10,6},{... | collective-permute-start | bytes 393224 | tf_op jit(solution)/shard_map/ppermute | solution.py:21
  142.3 11.7 %collective-permute-start.31 = (bf16[64,1024]{1,0:T(8,128)(2,1)S(1)}, bf16[64,1024]{1,0:T(8,128)(2,1)S(1)}, u32[]{:S(2)}, u32[]{:S(2)}) collective-permute-start(bf16[64,1024]{1,0:T(8,128)(2,1)S(1)} %get-tuple-element.30), channel_id=1, source_target_pairs={{8,0},{12,4},{0,8},{4,12},{9,1},{13,5},{1,9},{5,13},{10,2},{14,6},... | collective-permute-start | bytes 393224 | tf_op jit(solution)/shard_map/ppermute | solution.py:21
  (17 other events, 275.6 us)

commit v2 on v1

--- a/solution.py
+++ b/solution.py
@@ -7,6 +7,7 @@
 from jax.experimental.pallas import tpu as pltpu
 from jax.sharding import PartitionSpec as P
 
+
 SLOT = 24
 
 epsilon = 1e-06
@@ -19,6 +20,11 @@
     if step % size == 0:
         return value
     return lax.ppermute(value, axis, [((i + step) % size, i) for i in range(size)])
+
+
+def across(value, axis, flip):
+    size = lax.axis_size(axis)
+    return lax.ppermute(value, axis, [(i ^ flip, i) for i in range(size)])
 
 
 def pick(stacked, index):
@@ -38,7 +44,7 @@
     return expert_ids.astype(jnp.float32) * SLOT + slot
 
 
-STEP = 512
+STEP = 1024
 
 F32, BF16 = jnp.float32, jnp.bfloat16
 ANY = pl.BlockSpec(memory_space=pl.ANY)
@@ -49,11 +55,11 @@
 
 def down_copies(sel_ref, wd_ref, wds_ref, sem_ref, first):
     tensors, held, _, span = wds_ref.shape
-    copies = []
+    copies = [[] for _ in range(tensors)]
     for t in range(tensors):
         at = pl.multiple_of(sel_ref[t] + first, 128)
         for j in range(held):
-            copies.append(
+            copies[t].append(
                 pltpu.make_async_copy(
                     wd_ref.at[j, :, pl.ds(at, span)], wds_ref.at[t, j], sem_ref.at[t, j]
                 )
@@ -61,17 +67,17 @@
     return copies
 
 
-def down_and_combine(sel_ref, back_ref, act_ref, wds_ref, outs_ref, mixed_ref, groups, tensors):
+def down_and_combine(back_ref, act_ref, wds_ref, outs_ref, mixed_ref, groups, waits):
     held, slots, _ = act_ref.shape
-    cores, _, group_slots = back_ref.shape
-    span = wds_ref.shape[-1]
+    cores, _, _ = back_ref.shape
+    tensors, _, _, span = wds_ref.shape
     step = min(STEP, span)
     per = slots // groups
     for t in range(tensors):
-
-        @pl.loop(0, span // step)
-        def _(n):
-            cols = pl.ds(pl.multiple_of(n * step, step), step)
+        for copy in waits[t]:
+            copy.wait()
+        for n in range(span // step):
+            cols = slice(n * step, (n + 1) * step)
             for j in range(held):
                 out = jnp.dot(act_ref[j], wds_ref[t, j, :, cols], preferred_element_type=F32)
                 out = out.astype(BF16)
@@ -84,7 +90,7 @@
 
 
 def first_kernel(
-    dims, sel_ref, place_ref, back_ref, weight_ref, *rest
+    dims, sel_ref, place_ref, back_ref, *rest
 ):
     cores, tensors, depth, groups, first = dims
     lengths = depth if groups > 1 else 1
@@ -112,55 +118,59 @@
                 )
     for copy in copies:
         copy.start()
-    weights = []
-    for j in range(held):
-        for n, (src, dst) in enumerate(((wg_ref, wgs_ref), (wu_ref, wus_ref))):
-            weights.append(pltpu.make_async_copy(src.at[j], dst.at[j], w_sem.at[n, j]))
-    for copy in weights:
-        copy.start()
-    downs = down_copies(sel_ref, wd_ref, wds_ref, d_sem, first)
-    for copy in downs:
-        copy.start()
     for copy in copies:
         copy.wait()
 
+    def weights(j):
+        return [
+            pltpu.make_async_copy(src.at[j], dst.at[j], w_sem.at[n, j])
+            for n, (src, dst) in enumerate(((wg_ref, wgs_ref), (wu_ref, wus_ref)))
+        ]
+
+    downs = down_copies(sel_ref, wd_ref, wds_ref, d_sem, first)
+    queue = [weights(j) for j in range(held)] + downs
+
+    def start(n):
+        if n < len(queue):
+            for copy in queue[n]:
+                copy.start()
+
+    start(0)
     per = s_ref.shape[1] // groups
     step = min(STEP, width)
     for g in range(groups):
         kk = sel_ref[tensors + g]
-
-        @pl.loop(0, width // step)
-        def _(n):
-            at = pl.ds(pl.multiple_of(n * step, step), step)
+        for n in range(width // step):
+            at = slice(n * step, (n + 1) * step)
             rows = jnp.dot(place_ref[g], x_ref[kk, :, at], preferred_element_type=F32)
             rows = rows.astype(BF16)
             for j in range(held):
                 s_ref[j, g * per : (g + 1) * per, at] = rows[j * per : (j + 1) * per]
-
-    @pl.loop(0, held)
-    def _(j):
-        pltpu.make_async_copy(wg_ref.at[j], wgs_ref.at[j], w_sem.at[0, j]).wait()
+        if g == 0:
+            start(1)
+
+    for j in range(held):
+        start(j + 2)
+        wait_gate, wait_up = weights(j)
+        wait_gate.wait()
         gate = jnp.dot(s_ref[j], wgs_ref[j], preferred_element_type=F32)
-        pltpu.make_async_copy(wu_ref.at[j], wus_ref.at[j], w_sem.at[1, j]).wait()
+        wait_up.wait()
         up = jnp.dot(s_ref[j], wus_ref[j], preferred_element_type=F32)
-        value = gate / (1.0 + jnp.exp(-gate)) * up * weight_ref[j]
-        act_ref[j] = value.astype(BF16)
-
-    for copy in downs:
-        copy.wait()
-    down_and_combine(sel_ref, back_ref, act_ref, wds_ref, outs_ref, mixed_ref, groups, tensors)
+        act_ref[j] = (gate / (1.0 + jnp.exp(-gate)) * up).astype(BF16)
+    for n in range(held + 2, len(queue)):
+        start(n)
+    down_and_combine(back_ref, act_ref, wds_ref, outs_ref, mixed_ref, groups, downs)
 
 
 def later_kernel(dims, sel_ref, back_ref, act_ref, wd_ref, *rest):
-    cores, tensors, groups, first = dims
+    cores, _, groups, first = dims
     outs_ref = rest[:cores]
     wds_ref, mixed_ref, d_sem = rest[cores:]
     downs = down_copies(sel_ref, wd_ref, wds_ref, d_sem, first)
-    for copy in downs:
-        copy.start()
-    for copy in downs:
-        copy.wait()
-    down_and_combine(sel_ref, back_ref, act_ref, wds_ref, outs_ref, mixed_ref, groups, tensors)
+    for copies in downs:
+        for copy in copies:
+            copy.start()
+    down_and_combine(back_ref, act_ref, wds_ref, outs_ref, mixed_ref, groups, downs)
 
 
 def on_device(attn, o_weight, residual, norm_gain, expert_ids, route_weights, w_gate, w_up, w_down):
@@ -207,16 +217,11 @@
 
     codes = slot_codes(expert_ids, experts)
     route = jnp.concatenate([codes.T, route_weights.T], axis=0)
-    normed, route = lax.optimization_barrier((normed, route))
-
-    along = [fetch(normed, "expert", o) for o in range(depth)]
-    if sub > 1:
-        along = [jnp.concatenate(along, axis=0)]
-    mine = [fetch(v, "tensor", k) for k in range(tensors) for v in along]
-    pieces = [fetch(v, "dp", i) for i in range(cores) for v in mine]
-
     route = jnp.stack([fetch(route, "dp", i) for i in range(cores)])
-    route = jnp.stack([fetch(route, "expert", o) for o in range(depth)])
+    routes = [route]
+    for o in range(1, depth):
+        routes.append(across(route, "expert", o))
+    route = jnp.stack(routes)
     groups = tensors if sub == 1 else 1
     blocks = depth * cores // groups
     group_slots = held * blocks * SLOT
@@ -229,23 +234,37 @@
     slot = which * (blocks * SLOT) + block_ids * SLOT + (local - which * SLOT)
     slot = jnp.where(valid, slot, -1.0)
     weights = route[:, :, choices:]
-    by_core = slot.transpose(1, 2, 0, 3).reshape(cores, choices, depth * rows)
+    by_core = slot.transpose(1, 2, 0, 3).reshape(cores, choices, depth * rows, 1)
+    weight_by_core = weights.transpose(1, 2, 0, 3).reshape(cores, choices, depth * rows, 1)
     slot_ids = jnp.arange(group_slots, dtype=F32)
-    back = jnp.any(by_core[..., None] == slot_ids, axis=1).astype(BF16)
+    back = jnp.sum(jnp.where(by_core == slot_ids, weight_by_core, 0.0), axis=1).astype(BF16)
     if groups > 1:
-        table = jnp.concatenate([slot, weights], axis=2)
-        table = table.transpose(1, 2, 0, 3).reshape(groups, 2 * choices, depth * rows)
+        table = slot.transpose(1, 2, 0, 3).reshape(groups, choices, depth * rows)
     else:
-        table = jnp.concatenate([slot, weights], axis=2)
-        table = table.reshape(depth, cores, 2 * choices, sub, part)
-        table = table.transpose(1, 3, 2, 0, 4).reshape(tensors, 2 * choices, depth * part)
+        table = slot.reshape(depth, cores, choices, sub, part)
+        table = table.transpose(1, 3, 2, 0, 4).reshape(tensors, choices, depth * part)
         table = jnp.stack([pick(table, place((x + k) % tensors)) for k in range(tensors)])
-        table = table.transpose(1, 0, 2).reshape(1, 2 * choices, -1)
-    hit = table[:, :choices, None, :] == slot_ids[None, None, :, None]
-    placing = jnp.any(hit, axis=1).astype(BF16)
-    slot_weight = jnp.sum(jnp.where(hit, table[:, choices:, None, :], 0.0), axis=(1, 3))
-    slot_weight = slot_weight.reshape(groups, held, blocks * SLOT).transpose(1, 0, 2)
-    slot_weight = slot_weight.reshape(held, groups * blocks * SLOT, 1)
+        table = table.transpose(1, 0, 2).reshape(1, choices, -1)
+    placing = jnp.any(table[:, :, None, :] == slot_ids[:, None], axis=1).astype(BF16)
+
+    along = [normed]
+    mine = {}
+    for o in range(depth):
+        if o > 0:
+            along.append(across(along[o & (o - 1)], "expert", o & -o))
+    if sub > 1:
+        along = [jnp.concatenate(along, axis=0)]
+    else:
+        held_back = lax.optimization_barrier((along[-1], placing, back))
+        along[-1], placing, back = held_back
+    for o, value in enumerate(along):
+        for k in range(tensors):
+            mine[k, o] = fetch(value, "tensor", k)
+    pieces = []
+    for i in range(cores):
+        for k in range(tensors):
+            for o in range(len(along)):
+                pieces.append(fetch(mine[k, o], "dp", i))
 
     starts = [((x + t) % tensors) * cols_out for t in range(tensors)]
     starts += [(d + g - x) % tensors if groups > 1 else d * 0 for g in range(groups)]
@@ -268,7 +287,7 @@
     activated, *outs = pl.pallas_call(
         functools.partial(first_kernel, (cores, tensors, depth, groups, 0)),
         out_shape=[jax.ShapeDtypeStruct((held, slots, hidden_units), BF16)] + out_shapes(spans[0]),
-        in_specs=[SMEM, VMEM, VMEM, VMEM] + [ANY] * (len(pieces) + 3),
+        in_specs=[SMEM, VMEM, VMEM] + [ANY] * (len(pieces) + 3),
         out_specs=[VMEM] * (1 + cores),
         scratch_shapes=[
             pltpu.VMEM((groups, tensors // groups * depth * part, width), BF16),
@@ -284,7 +303,7 @@
         ],
         compiler_params=PARAMS,
         name="experts_first",
-    )(sel, placing, back, slot_weight, *pieces, w_gate, w_up, w_down)
+    )(sel, placing, back, *pieces, w_gate, w_up, w_down)
 
     results = []
     at = 0
@@ -307,15 +326,20 @@
         at += span
         summed = outs[0].astype(F32)
         for i in range(1, cores):
-            summed = summed + fetch(outs[i], "dp", -i).astype(F32)
+            got = fetch(outs[i], "dp", -i)
+            summed = summed + got.astype(F32)
         narrow = summed[0]
         for t in range(1, tensors):
-            narrow = narrow + fetch(summed[t].astype(BF16), "tensor", -t).astype(F32)
+            got = fetch(summed[t].astype(BF16), "tensor", -t)
+            narrow = narrow + got.astype(F32)
         narrow = narrow.reshape(depth, rows, span)
-        result = narrow[0]
-        for o in range(1, depth):
-            result = result + fetch(narrow[o].astype(BF16), "expert", -o).astype(F32)
-        results.append(result.astype(BF16))
+        flip = 1
+        while flip < depth:
+            narrow = narrow.reshape(-1, 2, rows, span)
+            got = across(narrow[:, 1].astype(BF16), "expert", flip)
+            narrow = narrow[:, 0] + got.astype(F32)
+            flip *= 2
+        results.append(narrow[0].astype(BF16))
     return jnp.concatenate(results, axis=1)
 
 
@@ -331,10 +355,14 @@
         P(("expert", "dp"), None, "tensor"),
         P(("expert", "dp"), "tensor", None),
     )
-    return jax.shard_map(
+
+    step = jax.shard_map(
         on_device,
         mesh=mesh,
         in_specs=placed,
         out_specs=P(("groups", "expert", "dp"), "tensor"),
         check_vma=False,
     )
+    if mesh.shape["tensor"] != mesh.shape["dp"]:
+        return step
+    return step

time: 155 us -> 135 us (0.87)
  Pallas kernels: 42.3 us -> 27.7 us
  starting transfers between devices: 31.8 us -> 21.9 us
  waiting for transfers between devices: 62.9 us -> 67.6 us
  local copies, waits for them, and re-layouts: 2.86 us -> 1.16 us
    ppermute x0 -> x10, waiting for transfers between devices: none -> 29.9 us  [across(): return lax.ppermute(value, axis, [(i ^ flip, i) for i in range(size)])]
    ppermute x33 -> x21, waiting for transfers between devices: 62.9 us -> 37.7 us  [fetch(): lax.ppermute(value, axis, [((i + step) % size, i) for i in range(size)])]
    ppermute x33 -> x21, starting transfers between devices: 31.8 us -> 10.4 us  [fetch(): lax.ppermute(value, axis, [((i + step) % size, i) for i in range(size)])]
    pallas_call x1, Pallas kernels: 32.6 us -> 19.7 us  [on_device(): pl.pallas_call(functools.partial(first_kernel, (cores, tensors, depth, gr...]
    ppermute x0 -> x10, starting transfers between devices: none -> 11.5 us  [across(): return lax.ppermute(value, axis, [(i ^ flip, i) for i in range(size)])]
    reduce_sum x1, other arithmetic: 0.74 us -> 2.38 us  [on_device(): jnp.sum(jnp.where(by_core == slot_ids, weight_by_core, 0.0), axis=1)]
    pallas_call x1, Pallas kernels: 9.66 us -> 8.03 us  [on_device(): pl.pallas_call(functools.partial(later_kernel, (cores, tensors, groups, a...]
  transfers between devices with their start and end apart: 33 -> 31, of which waited for: 14 -> 14; matrix products, arithmetic and copies ran while one was open for 7% -> 12% of each run, Pallas kernels for 6% -> 6%
where the time goes in v2:
time: 135 us; the launch traced here: 134 us
  waiting for transfers between devices  67.6 us (50%)
  Pallas kernels  27.7 us (21%)
  starting transfers between devices  21.9 us (16%)
  other arithmetic  10.7 us (8%)
  matrix products  4.82 us (4%)
    ppermute x21, waiting for transfers between devices, fetch(): lax.ppermute(value, axis, [((i + step) % size, i) for i in range(size)])  37.7 us
    ppermute x10, waiting for transfers between devices, across(): return lax.ppermute(value, axis, [(i ^ flip, i) for i in range(size)])  29.9 us
    pallas_call x1, Pallas kernels, on_device(): pl.pallas_call(functools.partial(first_kernel, (cores, tensors, depth, gr...  19.7 us
    ppermute x10, starting transfers between devices, across(): return lax.ppermute(value, axis, [(i ^ flip, i) for i in range(size)])  11.5 us
    ppermute x21, starting transfers between devices, fetch(): lax.ppermute(value, axis, [((i + step) % size, i) for i in range(size)])  10.4 us
    pallas_call x1, Pallas kernels, on_device(): pl.pallas_call(functools.partial(later_kernel, (cores, tensors, groups, a...  8.03 us
    dot_general x1, matrix products, on_device(): partial = jnp.dot(attn_all, o_weight, preferred_element_type=F32)  4.69 us
  transfers between devices with their start and end apart: 31, of which 14 were waited for; matrix products, arithmetic and copies ran while one was open for 12% of the time, Pallas kernels for 6%

profile of v2, /device:TPU:0, one launch (start us, length us, event | category | flops | bytes accessed | tf_op | source)
XLA Modules:
  0.0 134.4 jit_solution(14697610750650624197)
XLA Ops:
  1.4 0.7 select_reduce_fusion.1
  4.0 4.7 %convolution_add_fusion = f32[128,2048]{1,0:T(8,128)S(1)} fusion(bf16[2048,2048]{1,0:T(8,128)(2,1)} %param.10, bf16[64,2048]{1,0:T(8,128)(2,1)S(1)} %collective-permute-done, bf16[64,2048]{1,0:T(8,128)(2,1)} %param.9, bf16[64,2048]{1,0:T(8,128)(2,1)S(1)} %collective-permute-done.1, bf16[64,2048]{1,0:T(8,128)(2,1)} %param.11, pred[]{:T(512)S(6)} %eq.56), kind=kOutput, calls=%fused_computation.4 | convolution fusion | flops 1076363264 | bytes 10485761 | tf_op jit(solution)/shard_map/dot_general | solution.py:191
  8.7 2.6 %collective-permute-start.2 = (bf16[64,2048]{1,0:T(8,128)(2,1)S(1)}, bf16[64,2048]{1,0:T(8,128)(2,1)S(1)}, u32[]{:S(2)}, u32[]{:S(2)}) collective-permute-start(bf16[64,2048]{1,0:T(8,128)(2,1)S(1)} %fusion.16), channel_id=1, source_target_pairs={{2,0},{0,2},{3,1},{1,3},{6,4},{4,6},{7,5},{5,7},{10,8},{8,10},{11,... | collective-permute-start | bytes 786440 | tf_op jit(solution)/shard_map/ppermute | solution.py:22
  11.3 2.7 %collective-permute-start.8 = (f32[2,16,64]{2,1,0:T(8,128)S(1)}, f32[2,16,64]{2,1,0:T(8,128)S(1)}, u32[]{:S(2)}, u32[]{:S(2)}) collective-permute-start(f32[2,16,64]{2,1,0:T(8,128)S(1)} %get-tuple-element.26), channel_id=1, source_target_pairs={{8,0},{12,4},{0,8},{4,12},{9,1},{13,5},{1,9},{5,13},{10,2},{14,6},... | collective-permute-start | bytes 24584 | tf_op jit(solution)/shard_map/ppermute | solution.py:27
  14.0 1.6 %collective-permute-start.7 = (f32[2,16,64]{2,1,0:T(8,128)S(1)}, f32[2,16,64]{2,1,0:T(8,128)S(1)}, u32[]{:S(2)}, u32[]{:S(2)}) collective-permute-start(f32[2,16,64]{2,1,0:T(8,128)S(1)} %get-tuple-element.26), channel_id=1, source_target_pairs={{4,0},{0,4},{12,8},{8,12},{5,1},{1,5},{13,9},{9,13},{6,2},{2,6},{1... | collective-permute-start | bytes 24584 | tf_op jit(solution)/shard_map/ppermute | solution.py:27
  15.8 2.4 %collective-permute-done.2 = bf16[64,2048]{1,0:T(8,128)(2,1)S(1)} collective-permute-done((bf16[64,2048]{1,0:T(8,128)(2,1)S(1)}, bf16[64,2048]{1,0:T(8,128)(2,1)S(1)}, u32[]{:S(2)}, u32[]{:S(2)}) %collective-permute-start.2) | collective-permute-done | bytes 262176 | tf_op jit(solution)/shard_map/ppermute | solution.py:22
  18.5 2.6 %collective-permute-done.9 = f32[2,16,64]{2,1,0:T(8,128)S(1)} collective-permute-done((f32[2,16,64]{2,1,0:T(8,128)S(1)}, f32[2,16,64]{2,1,0:T(8,128)S(1)}, u32[]{:S(2)}, u32[]{:S(2)}) %collective-permute-start.9) | collective-permute-done | bytes 8224 | tf_op jit(solution)/shard_map/ppermute | solution.py:27
  21.3 1.4 %collective-permute-start.4 = (bf16[64,2048]{1,0:T(8,128)(2,1)S(1)}, bf16[64,2048]{1,0:T(8,128)(2,1)S(1)}, u32[]{:S(2)}, u32[]{:S(2)}) collective-permute-start(bf16[64,2048]{1,0:T(8,128)(2,1)S(1)} %fusion.5.rest_0_), channel_id=1, source_target_pairs={{8,0},{12,4},{0,8},{4,12},{9,1},{13,5},{1,9},{5,13},{10,2},{14,6},... | collective-permute-start | bytes 786440 | tf_op jit(solution)/shard_map/ppermute | solution.py:27
  23.0 1.0 fusion
  24.0 0.8 convert_element_type.137.place_ref
  24.9 1.5 %collective-permute-start.11 = (bf16[64,2048]{1,0:T(8,128)(2,1)S(1)}, bf16[64,2048]{1,0:T(8,128)(2,1)S(1)}, u32[]{:S(2)}, u32[]{:S(2)}) collective-permute-start(bf16[64,2048]{1,0:T(8,128)(2,1)S(1)} %fusion.5.rest_0_), channel_id=1, source_target_pairs={{2,0},{0,2},{3,1},{1,3},{6,4},{4,6},{7,5},{5,7},{10,8},{8,10},{11,... | collective-permute-start | bytes 786440 | tf_op jit(solution)/shard_map/ppermute | solution.py:22
  26.4 1.6 %collective-permute-start.10 = (bf16[64,2048]{1,0:T(8,128)(2,1)S(1)}, bf16[64,2048]{1,0:T(8,128)(2,1)S(1)}, u32[]{:S(2)}, u32[]{:S(2)}) collective-permute-start(bf16[64,2048]{1,0:T(8,128)(2,1)S(1)} %fusion.5.rest_0_), channel_id=1, source_target_pairs={{4,0},{0,4},{12,8},{8,12},{5,1},{1,5},{13,9},{9,13},{6,2},{2,6},{1... | collective-permute-start | bytes 786440 | tf_op jit(solution)/shard_map/ppermute | solution.py:27
  27.9 7.1 %collective-permute-done.4.rest_2_ = bf16[64,2048]{1,0:T(8,128)(2,1)S(1)} collective-permute-done((bf16[64,2048]{1,0:T(8,128)(2,1)S(1)}, bf16[64,2048]{1,0:T(8,128)(2,1)S(1)}, u32[]{:S(2)}, u32[]{:S(2)}) %collective-permute-start.4) | collective-permute-done | bytes 262176 | tf_op jit(solution)/shard_map/ppermute | solution.py:27
  35.7 2.4 %select_reduce_fusion.back_ref = bf16[2,256,384]{2,1,0:T(8,128)(2,1)} fusion(f32[2,8,256]{2,1,0:T(8,128)S(1)} %broadcast_in_dim.36, f32[2,8,256]{2,1,0:T(8,128)S(1)} %eq.60), kind=kLoop, calls=%fused_computation | loop fusion | flops 4521984 | bytes 425984 | tf_op jit(solution)/shard_map/reduce_sum | solution.py:240
  38.1 1.8 %collective-permute-done.10.rest_1_ = bf16[64,2048]{1,0:T(8,128)(2,1)S(1)} collective-permute-done((bf16[64,2048]{1,0:T(8,128)(2,1)S(1)}, bf16[64,2048]{1,0:T(8,128)(2,1)S(1)}, u32[]{:S(2)}, u32[]{:S(2)}) %collective-permute-start.10) | collective-permute-done | bytes 262176 | tf_op jit(solution)/shard_map/ppermute | solution.py:27
  40.6 4.3 %collective-permute-done.5.rest_3_ = bf16[64,2048]{1,0:T(8,128)(2,1)S(1)} collective-permute-done((bf16[64,2048]{1,0:T(8,128)(2,1)S(1)}, bf16[64,2048]{1,0:T(8,128)(2,1)S(1)}, u32[]{:S(2)}, u32[]{:S(2)}) %collective-permute-start.5) | collective-permute-done | bytes 262176 | tf_op jit(solution)/shard_map/ppermute | solution.py:27
  45.5 1.4 %collective-permute-start.14 = (bf16[64,2048]{1,0:T(8,128)(2,1)S(1)}, bf16[64,2048]{1,0:T(8,128)(2,1)S(1)}, u32[]{:S(2)}, u32[]{:S(2)}) collective-permute-start(bf16[64,2048]{1,0:T(8,128)(2,1)S(1)} %collective-permute-done.5.rest_3_), channel_id=1, source_target_pairs={{2,0},{0,2},{3,1},{1,3},{6,4},{4,6},{7,5},{5,7},{10,8},{8,10},{11,... | collective-permute-start | bytes 786440 | tf_op jit(solution)/shard_map/ppermute | solution.py:22
  47.4 1.7 %collective-permute-done.12.rest_5_ = bf16[64,2048]{1,0:T(8,128)(2,1)S(1)} collective-permute-done((bf16[64,2048]{1,0:T(8,128)(2,1)S(1)}, bf16[64,2048]{1,0:T(8,128)(2,1)S(1)}, u32[]{:S(2)}, u32[]{:S(2)}) %collective-permute-start.12) | collective-permute-done | bytes 262176 | tf_op jit(solution)/shard_map/ppermute | solution.py:22
  49.1 5.6 %collective-permute-done.13.rest_6_ = bf16[64,2048]{1,0:T(8,128)(2,1)S(1)} collective-permute-done((bf16[64,2048]{1,0:T(8,128)(2,1)S(1)}, bf16[64,2048]{1,0:T(8,128)(2,1)S(1)}, u32[]{:S(2)}, u32[]{:S(2)}) %collective-permute-start.13) | collective-permute-done | bytes 262176 | tf_op jit(solution)/shard_map/ppermute | solution.py:22
  54.7 5.2 %collective-permute-done.14.rest_7_ = bf16[64,2048]{1,0:T(8,128)(2,1)S(1)} collective-permute-done((bf16[64,2048]{1,0:T(8,128)(2,1)S(1)}, bf16[64,2048]{1,0:T(8,128)(2,1)S(1)}, u32[]{:S(2)}, u32[]{:S(2)}) %collective-permute-start.14) | collective-permute-done | bytes 262176 | tf_op jit(solution)/shard_map/ppermute | solution.py:22
  60.5 1.0 collective-permute-done.22.rest_15_
  61.6 19.7 %experts_first.1 = (bf16[4,192,512]{2,1,0:T(8,128)(2,1)}, bf16[2,256,1024]{2,1,0:T(8,128)(2,1)}, bf16[2,256,1024]{2,1,0:T(8,128)(2,1)}) custom-call(s32[6]{0:T(128)} %stack.51.sel_ref, bf16[2,384,256]{2,1,0:T(8,128)(2,1)} %convert_element_type.137.place_ref, bf16[2,256,384]{2,1,0:T(8,128)(2,1)} %select_reduce_fusion.back_ref, bf16[64,2048]{1,0:T(8,128)(2,1)} %copy-done, ...), custom_call_target="tpu_custom_call" | custom-call | tf_op jit(solution)/shard_map/experts_first/pallas_call | solution.py:287
  81.5 8.0 %experts_later.1 = (bf16[2,256,1024]{2,1,0:T(8,128)(2,1)}, bf16[2,256,1024]{2,1,0:T(8,128)(2,1)}) custom-call(s32[6]{0:T(128)} %stack.51.sel_ref, bf16[2,256,384]{2,1,0:T(8,128)(2,1)} %select_reduce_fusion.back_ref, bf16[4,192,512]{2,1,0:T(8,128)(2,1)} %get-tuple-element.18.act_ref, bf16[4,512,4096]{2,1,0:T(8,128)(2,1)} %wd_ref.1), custom_call_target="tpu_custom_call" | custom-call | flops 3221225472 | bytes 8388608 | tf_op jit(solution)/shard_map/experts_later/pallas_call | solution.py:312
  90.5 0.7 collective-permute-start.24
  91.2 1.3 collective-permute-done.27
  92.5 1.6 %convert_add_fusion = f32[2,256,1024]{2,1,0:T(8,128)S(1)} fusion(bf16[2,256,1024]{2,1,0:T(8,128)(2,1)S(1)} %collective-permute-done.27, bf16[2,256,1024]{2,1,0:T(8,128)(2,1)} %get-tuple-element.19), kind=kLoop, calls=%fused_computation.5 | loop fusion | flops 1572864 | bytes 4194304 | tf_op jit(solution)/shard_map/add | solution.py:330
  94.2 0.7 collective-permute-start.28
  94.9 10.4 %collective-permute-done.24 = bf16[256,1024]{1,0:T(8,128)(2,1)S(1)} collective-permute-done((bf16[256,1024]{1,0:T(8,128)(2,1)S(1)}, bf16[256,1024]{1,0:T(8,128)(2,1)S(1)}, u32[]{:S(2)}, u32[]{:S(2)}) %collective-permute-start.24) | collective-permute-done | bytes 524320 | tf_op jit(solution)/shard_map/ppermute | solution.py:22
  105.7 10.1 %collective-permute-done.28 = bf16[256,1024]{1,0:T(8,128)(2,1)S(1)} collective-permute-done((bf16[256,1024]{1,0:T(8,128)(2,1)S(1)}, bf16[256,1024]{1,0:T(8,128)(2,1)S(1)}, u32[]{:S(2)}, u32[]{:S(2)}) %collective-permute-start.28) | collective-permute-done | bytes 524320 | tf_op jit(solution)/shard_map/ppermute | solution.py:22
  116.2 2.8 %collective-permute-start.26 = (bf16[1,64,1024]{2,1,0:T(8,128)(2,1)S(1)}, bf16[1,64,1024]{2,1,0:T(8,128)(2,1)S(1)}, u32[]{:S(2)}, u32[]{:S(2)}) collective-permute-start(bf16[1,64,1024]{2,1,0:T(8,128)(2,1)S(1)} %fusion.24), channel_id=1, source_target_pairs={{8,0},{12,4},{0,8},{4,12},{9,1},{13,5},{1,9},{5,13},{10,2},{14,6},... | collective-permute-start | bytes 393224 | tf_op jit(solution)/shard_map/ppermute | solution.py:27
  119.0 7.3 %collective-permute-done.29 = bf16[2,64,1024]{2,1,0:T(8,128)(2,1)S(1)} collective-permute-done((bf16[2,64,1024]{2,1,0:T(8,128)(2,1)S(1)}, bf16[2,64,1024]{2,1,0:T(8,128)(2,1)S(1)}, u32[]{:S(2)}, u32[]{:S(2)}) %collective-permute-start.29) | collective-permute-done | bytes 262176 | tf_op jit(solution)/shard_map/ppermute | solution.py:27
  126.9 6.8 %collective-permute-done.30 = bf16[1,64,1024]{2,1,0:T(8,128)(2,1)S(1)} collective-permute-done((bf16[1,64,1024]{2,1,0:T(8,128)(2,1)S(1)}, bf16[1,64,1024]{2,1,0:T(8,128)(2,1)S(1)}, u32[]{:S(2)}, u32[]{:S(2)}) %collective-permute-start.30) | collective-permute-done | bytes 131104 | tf_op jit(solution)/shard_map/ppermute | solution.py:27
  (100 shorter events, 10.4 us)
Async XLA Ops:
  0.0 4.0 %collective-permute-start = (bf16[64,2048]{1,0:T(8,128)(2,1)}, bf16[64,2048]{1,0:T(8,128)(2,1)S(1)}, u32[]{:S(2)}, u32[]{:S(2)}) collective-permute-start(bf16[64,2048]{1,0:T(8,128)(2,1)} %param.9), channel_id=1, source_target_pairs={{1,0},{0,1},{3,2},{2,3},{5,4},{4,5},{7,6},{6,7},{9,8},{8,9},{11,10... | collective-permute-start | bytes 786440 | tf_op jit(solution)/shard_map/ppermute | solution.py:22
  0.5 3.5 %collective-permute-start.1 = (bf16[64,2048]{1,0:T(8,128)(2,1)}, bf16[64,2048]{1,0:T(8,128)(2,1)S(1)}, u32[]{:S(2)}, u32[]{:S(2)}) collective-permute-start(bf16[64,2048]{1,0:T(8,128)(2,1)} %param.11), channel_id=1, source_target_pairs={{1,0},{0,1},{3,2},{2,3},{5,4},{4,5},{7,6},{6,7},{9,8},{8,9},{11,10... | collective-permute-start | bytes 786440 | tf_op jit(solution)/shard_map/ppermute | solution.py:22
  3.5 7.8 %collective-permute-start.6 = (f32[16,64]{1,0:T(8,128)S(1)}, f32[16,64]{1,0:T(8,128)S(1)}, u32[]{:S(2)}, u32[]{:S(2)}) collective-permute-start(f32[16,64]{1,0:T(8,128)S(1)} %get-tuple-element.28), channel_id=1, source_target_pairs={{1,0},{0,1},{3,2},{2,3},{5,4},{4,5},{7,6},{6,7},{9,8},{8,9},{11,10... | collective-permute-start | bytes 12296 | tf_op jit(solution)/shard_map/ppermute | solution.py:22
  8.7 9.5 %collective-permute-start.2 = (bf16[64,2048]{1,0:T(8,128)(2,1)S(1)}, bf16[64,2048]{1,0:T(8,128)(2,1)S(1)}, u32[]{:S(2)}, u32[]{:S(2)}) collective-permute-start(bf16[64,2048]{1,0:T(8,128)(2,1)S(1)} %fusion.16), channel_id=1, source_target_pairs={{2,0},{0,2},{3,1},{1,3},{6,4},{4,6},{7,5},{5,7},{10,8},{8,10},{11,... | collective-permute-start | bytes 786440 | tf_op jit(solution)/shard_map/ppermute | solution.py:22
  11.3 7.1 %collective-permute-start.8 = (f32[2,16,64]{2,1,0:T(8,128)S(1)}, f32[2,16,64]{2,1,0:T(8,128)S(1)}, u32[]{:S(2)}, u32[]{:S(2)}) collective-permute-start(f32[2,16,64]{2,1,0:T(8,128)S(1)} %get-tuple-element.26), channel_id=1, source_target_pairs={{8,0},{12,4},{0,8},{4,12},{9,1},{13,5},{1,9},{5,13},{10,2},{14,6},... | collective-permute-start | bytes 24584 | tf_op jit(solution)/shard_map/ppermute | solution.py:27
  14.0 4.5 %collective-permute-start.7 = (f32[2,16,64]{2,1,0:T(8,128)S(1)}, f32[2,16,64]{2,1,0:T(8,128)S(1)}, u32[]{:S(2)}, u32[]{:S(2)}) collective-permute-start(f32[2,16,64]{2,1,0:T(8,128)S(1)} %get-tuple-element.26), channel_id=1, source_target_pairs={{4,0},{0,4},{12,8},{8,12},{5,1},{1,5},{13,9},{9,13},{6,2},{2,6},{1... | collective-permute-start | bytes 24584 | tf_op jit(solution)/shard_map/ppermute | solution.py:27
  15.6 5.5 %collective-permute-start.9 = (f32[2,16,64]{2,1,0:T(8,128)S(1)}, f32[2,16,64]{2,1,0:T(8,128)S(1)}, u32[]{:S(2)}, u32[]{:S(2)}) collective-permute-start(f32[2,16,64]{2,1,0:T(8,128)S(1)} %get-tuple-element.26), channel_id=1, source_target_pairs={{12,0},{8,4},{4,8},{0,12},{13,1},{9,5},{5,9},{1,13},{14,2},{10,6},... | collective-permute-start | bytes 24584 | tf_op jit(solution)/shard_map/ppermute | solution.py:27
  18.4 2.7 %collective-permute-start.3 = (f32[64,1]{0,1:T(1,128)S(1)}, f32[64,1]{0,1:T(1,128)S(1)}, u32[]{:S(2)}, u32[]{:S(2)}) collective-permute-start(f32[64,1]{0,1:T(1,128)S(1)} %bitcast.104), channel_id=1, source_target_pairs={{1,0},{0,1},{3,2},{2,3},{5,4},{4,5},{7,6},{6,7},{9,8},{8,9},{11,10... | collective-permute-start | bytes 776 | tf_op jit(solution)/shard_map/ppermute | solution.py:22
  21.3 40.3 %copy-start = (bf16[64,2048]{1,0:T(8,128)(2,1)}, bf16[64,2048]{1,0:T(8,128)(2,1)S(1)}, u32[]{:S(2)}) copy-start(bf16[64,2048]{1,0:T(8,128)(2,1)S(1)} %fusion.5.rest_0_) | copy-start | bytes 786436
  21.3 13.8 %collective-permute-start.4 = (bf16[64,2048]{1,0:T(8,128)(2,1)S(1)}, bf16[64,2048]{1,0:T(8,128)(2,1)S(1)}, u32[]{:S(2)}, u32[]{:S(2)}) collective-permute-start(bf16[64,2048]{1,0:T(8,128)(2,1)S(1)} %fusion.5.rest_0_), channel_id=1, source_target_pairs={{8,0},{12,4},{0,8},{4,12},{9,1},{13,5},{1,9},{5,13},{10,2},{14,6},... | collective-permute-start | bytes 786440 | tf_op jit(solution)/shard_map/ppermute | solution.py:27
  24.9 20.6 %collective-permute-start.15 = (bf16[64,2048]{1,0:T(8,128)(2,1)S(1)}, bf16[64,2048]{1,0:T(8,128)(2,1)S(1)}, u32[]{:S(2)}, u32[]{:S(2)}) collective-permute-start(bf16[64,2048]{1,0:T(8,128)(2,1)S(1)} %fusion.5.rest_0_), channel_id=1, source_target_pairs={{1,0},{0,1},{3,2},{2,3},{5,4},{4,5},{7,6},{6,7},{9,8},{8,9},{11,10... | collective-permute-start | bytes 786440 | tf_op jit(solution)/shard_map/ppermute | solution.py:22
  24.9 13.3 %collective-permute-start.11 = (bf16[64,2048]{1,0:T(8,128)(2,1)S(1)}, bf16[64,2048]{1,0:T(8,128)(2,1)S(1)}, u32[]{:S(2)}, u32[]{:S(2)}) collective-permute-start(bf16[64,2048]{1,0:T(8,128)(2,1)S(1)} %fusion.5.rest_0_), channel_id=1, source_target_pairs={{2,0},{0,2},{3,1},{1,3},{6,4},{4,6},{7,5},{5,7},{10,8},{8,10},{11,... | collective-permute-start | bytes 786440 | tf_op jit(solution)/shard_map/ppermute | solution.py:22
  26.4 13.6 %collective-permute-start.10 = (bf16[64,2048]{1,0:T(8,128)(2,1)S(1)}, bf16[64,2048]{1,0:T(8,128)(2,1)S(1)}, u32[]{:S(2)}, u32[]{:S(2)}) collective-permute-start(bf16[64,2048]{1,0:T(8,128)(2,1)S(1)} %fusion.5.rest_0_), channel_id=1, source_target_pairs={{4,0},{0,4},{12,8},{8,12},{5,1},{1,5},{13,9},{9,13},{6,2},{2,6},{1... | collective-permute-start | bytes 786440 | tf_op jit(solution)/shard_map/ppermute | solution.py:27
  35.1 9.8 %collective-permute-start.5 = (bf16[64,2048]{1,0:T(8,128)(2,1)S(1)}, bf16[64,2048]{1,0:T(8,128)(2,1)S(1)}, u32[]{:S(2)}, u32[]{:S(2)}) collective-permute-start(bf16[64,2048]{1,0:T(8,128)(2,1)S(1)} %collective-permute-done.4.rest_2_), channel_id=1, source_target_pairs={{4,0},{0,4},{12,8},{8,12},{5,1},{1,5},{13,9},{9,13},{6,2},{2,6},{1... | collective-permute-start | bytes 786440 | tf_op jit(solution)/shard_map/ppermute | solution.py:27
  38.1 8.8 %collective-permute-start.19 = (bf16[64,2048]{1,0:T(8,128)(2,1)S(1)}, bf16[64,2048]{1,0:T(8,128)(2,1)S(1)}, u32[]{:S(2)}, u32[]{:S(2)}) collective-permute-start(bf16[64,2048]{1,0:T(8,128)(2,1)S(1)} %collective-permute-done.11.rest_4_), channel_id=1, source_target_pairs={{1,0},{0,1},{3,2},{2,3},{5,4},{4,5},{7,6},{6,7},{9,8},{8,9},{11,10... | collective-permute-start | bytes 786440 | tf_op jit(solution)/shard_map/ppermute | solution.py:22
  39.9 7.0 %collective-permute-start.16 = (bf16[64,2048]{1,0:T(8,128)(2,1)S(1)}, bf16[64,2048]{1,0:T(8,128)(2,1)S(1)}, u32[]{:S(2)}, u32[]{:S(2)}) collective-permute-start(bf16[64,2048]{1,0:T(8,128)(2,1)S(1)} %collective-permute-done.10.rest_1_), channel_id=1, source_target_pairs={{1,0},{0,1},{3,2},{2,3},{5,4},{4,5},{7,6},{6,7},{9,8},{8,9},{11,10... | collective-permute-start | bytes 786440 | tf_op jit(solution)/shard_map/ppermute | solution.py:22
  39.9 9.2 %collective-permute-start.12 = (bf16[64,2048]{1,0:T(8,128)(2,1)S(1)}, bf16[64,2048]{1,0:T(8,128)(2,1)S(1)}, u32[]{:S(2)}, u32[]{:S(2)}) collective-permute-start(bf16[64,2048]{1,0:T(8,128)(2,1)S(1)} %collective-permute-done.10.rest_1_), channel_id=1, source_target_pairs={{2,0},{0,2},{3,1},{1,3},{6,4},{4,6},{7,5},{5,7},{10,8},{8,10},{11,... | collective-permute-start | bytes 786440 | tf_op jit(solution)/shard_map/ppermute | solution.py:22
  44.9 9.8 %collective-permute-start.13 = (bf16[64,2048]{1,0:T(8,128)(2,1)S(1)}, bf16[64,2048]{1,0:T(8,128)(2,1)S(1)}, u32[]{:S(2)}, u32[]{:S(2)}) collective-permute-start(bf16[64,2048]{1,0:T(8,128)(2,1)S(1)} %collective-permute-done.4.rest_2_), channel_id=1, source_target_pairs={{2,0},{0,2},{3,1},{1,3},{6,4},{4,6},{7,5},{5,7},{10,8},{8,10},{11,... | collective-permute-start | bytes 786440 | tf_op jit(solution)/shard_map/ppermute | solution.py:22
  45.5 14.4 %collective-permute-start.14 = (bf16[64,2048]{1,0:T(8,128)(2,1)S(1)}, bf16[64,2048]{1,0:T(8,128)(2,1)S(1)}, u32[]{:S(2)}, u32[]{:S(2)}) collective-permute-start(bf16[64,2048]{1,0:T(8,128)(2,1)S(1)} %collective-permute-done.5.rest_3_), channel_id=1, source_target_pairs={{2,0},{0,2},{3,1},{1,3},{6,4},{4,6},{7,5},{5,7},{10,8},{8,10},{11,... | collective-permute-start | bytes 786440 | tf_op jit(solution)/shard_map/ppermute | solution.py:22
  46.9 13.6 %collective-permute-start.17 = (bf16[64,2048]{1,0:T(8,128)(2,1)S(1)}, bf16[64,2048]{1,0:T(8,128)(2,1)S(1)}, u32[]{:S(2)}, u32[]{:S(2)}) collective-permute-start(bf16[64,2048]{1,0:T(8,128)(2,1)S(1)} %collective-permute-done.4.rest_2_), channel_id=1, source_target_pairs={{1,0},{0,1},{3,2},{2,3},{5,4},{4,5},{7,6},{6,7},{9,8},{8,9},{11,10... | collective-permute-start | bytes 786440 | tf_op jit(solution)/shard_map/ppermute | solution.py:22
  46.9 13.6 %collective-permute-start.18 = (bf16[64,2048]{1,0:T(8,128)(2,1)S(1)}, bf16[64,2048]{1,0:T(8,128)(2,1)S(1)}, u32[]{:S(2)}, u32[]{:S(2)}) collective-permute-start(bf16[64,2048]{1,0:T(8,128)(2,1)S(1)} %collective-permute-done.5.rest_3_), channel_id=1, source_target_pairs={{1,0},{0,1},{3,2},{2,3},{5,4},{4,5},{7,6},{6,7},{9,8},{8,9},{11,10... | collective-permute-start | bytes 786440 | tf_op jit(solution)/shard_map/ppermute | solution.py:22
  49.1 11.4 %collective-permute-start.20 = (bf16[64,2048]{1,0:T(8,128)(2,1)S(1)}, bf16[64,2048]{1,0:T(8,128)(2,1)}, u32[]{:S(2)}, u32[]{:S(2)}) collective-permute-start(bf16[64,2048]{1,0:T(8,128)(2,1)S(1)} %collective-permute-done.12.rest_5_), channel_id=1, source_target_pairs={{1,0},{0,1},{3,2},{2,3},{5,4},{4,5},{7,6},{6,7},{9,8},{8,9},{11,10... | collective-permute-start | bytes 786440 | tf_op jit(solution)/shard_map/ppermute | solution.py:22
  54.7 5.8 %collective-permute-start.21 = (bf16[64,2048]{1,0:T(8,128)(2,1)S(1)}, bf16[64,2048]{1,0:T(8,128)(2,1)}, u32[]{:S(2)}, u32[]{:S(2)}) collective-permute-start(bf16[64,2048]{1,0:T(8,128)(2,1)S(1)} %collective-permute-done.13.rest_6_), channel_id=1, source_target_pairs={{1,0},{0,1},{3,2},{2,3},{5,4},{4,5},{7,6},{6,7},{9,8},{8,9},{11,10... | collective-permute-start | bytes 786440 | tf_op jit(solution)/shard_map/ppermute | solution.py:22
  59.9 1.7 %collective-permute-start.22 = (bf16[64,2048]{1,0:T(8,128)(2,1)S(1)}, bf16[64,2048]{1,0:T(8,128)(2,1)}, u32[]{:S(2)}, u32[]{:S(2)}) collective-permute-start(bf16[64,2048]{1,0:T(8,128)(2,1)S(1)} %collective-permute-done.14.rest_7_), channel_id=1, source_target_pairs={{1,0},{0,1},{3,2},{2,3},{5,4},{4,5},{7,6},{6,7},{9,8},{8,9},{11,10... | collective-permute-start | bytes 786440 | tf_op jit(solution)/shard_map/ppermute | solution.py:22
  81.3 8.7 %collective-permute-start.23 = (bf16[2,256,1024]{2,1,0:T(8,128)(2,1)}, bf16[2,256,1024]{2,1,0:T(8,128)(2,1)S(1)}, u32[]{:S(2)}, u32[]{:S(2)}) collective-permute-start(bf16[2,256,1024]{2,1,0:T(8,128)(2,1)} %get-tuple-element.17), channel_id=1, source_target_pairs={{1,0},{0,1},{3,2},{2,3},{5,4},{4,5},{7,6},{6,7},{9,8},{8,9},{11,10... | collective-permute-start | bytes 3145736 | tf_op jit(solution)/shard_map/ppermute | solution.py:22
  89.6 2.9 %collective-permute-start.27 = (bf16[2,256,1024]{2,1,0:T(8,128)(2,1)}, bf16[2,256,1024]{2,1,0:T(8,128)(2,1)S(1)}, u32[]{:S(2)}, u32[]{:S(2)}) collective-permute-start(bf16[2,256,1024]{2,1,0:T(8,128)(2,1)} %get-tuple-element.20), channel_id=1, source_target_pairs={{1,0},{0,1},{3,2},{2,3},{5,4},{4,5},{7,6},{6,7},{9,8},{8,9},{11,10... | collective-permute-start | bytes 3145736 | tf_op jit(solution)/shard_map/ppermute | solution.py:22
  90.5 14.9 %collective-permute-start.24 = (bf16[256,1024]{1,0:T(8,128)(2,1)S(1)}, bf16[256,1024]{1,0:T(8,128)(2,1)S(1)}, u32[]{:S(2)}, u32[]{:S(2)}) collective-permute-start(bf16[256,1024]{1,0:T(8,128)(2,1)S(1)} %fusion.6), channel_id=1, source_target_pairs={{2,0},{0,2},{3,1},{1,3},{6,4},{4,6},{7,5},{5,7},{10,8},{8,10},{11,... | collective-permute-start | bytes 1572872 | tf_op jit(solution)/shard_map/ppermute | solution.py:22
  94.2 21.6 %collective-permute-start.28 = (bf16[256,1024]{1,0:T(8,128)(2,1)S(1)}, bf16[256,1024]{1,0:T(8,128)(2,1)S(1)}, u32[]{:S(2)}, u32[]{:S(2)}) collective-permute-start(bf16[256,1024]{1,0:T(8,128)(2,1)S(1)} %fusion.7), channel_id=1, source_target_pairs={{2,0},{0,2},{3,1},{1,3},{6,4},{4,6},{7,5},{5,7},{10,8},{8,10},{11,... | collective-permute-start | bytes 1572872 | tf_op jit(solution)/shard_map/ppermute | solution.py:22
  105.6 10.5 %collective-permute-start.25 = (bf16[2,64,1024]{2,1,0:T(8,128)(2,1)S(1)}, bf16[2,64,1024]{2,1,0:T(8,128)(2,1)S(1)}, u32[]{:S(2)}, u32[]{:S(2)}) collective-permute-start(bf16[2,64,1024]{2,1,0:T(8,128)(2,1)S(1)} %fusion.17), channel_id=1, source_target_pairs={{4,0},{0,4},{12,8},{8,12},{5,1},{1,5},{13,9},{9,13},{6,2},{2,6},{1... | collective-permute-start | bytes 786440 | tf_op jit(solution)/shard_map/ppermute | solution.py:27
  116.0 10.4 %collective-permute-start.29 = (bf16[2,64,1024]{2,1,0:T(8,128)(2,1)S(1)}, bf16[2,64,1024]{2,1,0:T(8,128)(2,1)S(1)}, u32[]{:S(2)}, u32[]{:S(2)}) collective-permute-start(bf16[2,64,1024]{2,1,0:T(8,128)(2,1)S(1)} %fusion.18), channel_id=1, source_target_pairs={{4,0},{0,4},{12,8},{8,12},{5,1},{1,5},{13,9},{9,13},{6,2},{2,6},{1... | collective-permute-start | bytes 786440 | tf_op jit(solution)/shard_map/ppermute | solution.py:27
  116.2 10.7 %collective-permute-start.26 = (bf16[1,64,1024]{2,1,0:T(8,128)(2,1)S(1)}, bf16[1,64,1024]{2,1,0:T(8,128)(2,1)S(1)}, u32[]{:S(2)}, u32[]{:S(2)}) collective-permute-start(bf16[1,64,1024]{2,1,0:T(8,128)(2,1)S(1)} %fusion.24), channel_id=1, source_target_pairs={{8,0},{12,4},{0,8},{4,12},{9,1},{13,5},{1,9},{5,13},{10,2},{14,6},... | collective-permute-start | bytes 393224 | tf_op jit(solution)/shard_map/ppermute | solution.py:27
  126.4 7.2 %collective-permute-start.30 = (bf16[1,64,1024]{2,1,0:T(8,128)(2,1)S(1)}, bf16[1,64,1024]{2,1,0:T(8,128)(2,1)S(1)}, u32[]{:S(2)}, u32[]{:S(2)}) collective-permute-start(bf16[1,64,1024]{2,1,0:T(8,128)(2,1)S(1)} %fusion.26), channel_id=1, source_target_pairs={{8,0},{12,4},{0,8},{4,12},{9,1},{13,5},{1,9},{5,13},{10,2},{14,6},... | collective-permute-start | bytes 393224 | tf_op jit(solution)/shard_map/ppermute | solution.py:27
  (14 other events, 172.9 us)

commit v3 on v2

--- a/solution.py
+++ b/solution.py
@@ -12,7 +12,7 @@
 
 epsilon = 1e-06
 
-CHUNKS = (4, 4)
+CHUNKS = (4, 3, 1)
 
 
 def fetch(value, axis, step):
@@ -31,26 +31,57 @@
     return lax.dynamic_index_in_dim(stacked, index, 0, keepdims=False)
 
 
-def slot_codes(expert_ids, experts):
-    rows_here = expert_ids.shape[0]
-    onehot = (expert_ids[:, :, None] == jnp.arange(experts, dtype=jnp.int32)).astype(jnp.float32)
-    chosen = jnp.sum(onehot, axis=1)
-    row_ids = jnp.arange(rows_here)
-    earlier = (row_ids[:, None] > row_ids[None, :]).astype(jnp.bfloat16)
-    before = jnp.dot(
-        earlier, chosen.astype(jnp.bfloat16), preferred_element_type=jnp.float32
-    )
-    slot = jnp.sum(onehot * before[:, None, :], axis=2)
-    return expert_ids.astype(jnp.float32) * SLOT + slot
-
-
 STEP = 1024
 
 F32, BF16 = jnp.float32, jnp.bfloat16
 ANY = pl.BlockSpec(memory_space=pl.ANY)
 VMEM = pl.BlockSpec(memory_space=pltpu.VMEM)
 SMEM = pl.BlockSpec(memory_space=pltpu.SMEM)
+SMALL = pltpu.CompilerParams(vmem_limit_bytes=8 * 1024 * 1024)
 PARAMS = pltpu.CompilerParams(vmem_limit_bytes=60 * 1024 * 1024)
+
+
+def codes_kernel(experts, ids_ref, weights_ref, out_ref):
+    rows, choices = ids_ref.shape
+    ids = ids_ref[...]
+    lanes = lax.broadcasted_iota(jnp.int32, (rows, experts), 1)
+    picked = [(ids[:, k : k + 1] == lanes).astype(F32) for k in range(choices)]
+    chosen = functools.reduce(jnp.add, picked)
+    earlier = lax.broadcasted_iota(jnp.int32, (rows, rows), 0) > lax.broadcasted_iota(
+        jnp.int32, (rows, rows), 1
+    )
+    before = jnp.dot(
+        earlier.astype(F32).astype(BF16), chosen.astype(BF16), preferred_element_type=F32
+    )
+    slot = [jnp.sum(p * before, axis=1, keepdims=True) for p in picked]
+    codes = jnp.concatenate(slot, axis=1) + ids.astype(F32) * SLOT
+    out_ref[...] = jnp.concatenate([codes, weights_ref[...]], axis=1).T
+
+
+def tables_kernel(choices, base_ref, *rest):
+    routes, (place_ref, back_ref) = rest[:-2], rest[-2:]
+    depth = len(routes)
+    cores, group_slots, out_rows = place_ref.shape
+    per = depth * SLOT
+    base = base_ref[0].astype(F32)
+    for i in range(cores):
+        slots = []
+        for o in range(depth):
+            local = routes[o][i, :choices] - base
+            which = jnp.floor((local + 0.5) * (1.0 / SLOT))
+            slot = which * (per - SLOT) + local + o * SLOT
+            slots.append(jnp.where((local >= 0) & (local < group_slots // depth), slot, -1.0))
+        slot = jnp.concatenate(slots, axis=1).astype(jnp.int32)
+        down = lax.broadcasted_iota(jnp.int32, (group_slots, out_rows), 0)
+        hit = [slot[k : k + 1] == down for k in range(choices)]
+        place_ref[i] = functools.reduce(jnp.logical_or, hit).astype(F32).astype(BF16)
+        turned = slot.astype(F32).T.astype(jnp.int32)
+        weights = jnp.concatenate([routes[o][i, choices:] for o in range(depth)], axis=1).T
+        along = lax.broadcasted_iota(jnp.int32, (out_rows, group_slots), 1)
+        total = jnp.zeros((out_rows, group_slots), F32)
+        for k in range(choices):
+            total = jnp.where(turned[:, k : k + 1] == along, weights[:, k : k + 1], total)
+        back_ref[i] = total.astype(BF16)
 
 
 def down_copies(sel_ref, wd_ref, wds_ref, sem_ref, first):
@@ -215,37 +246,53 @@
     gain = lax.dynamic_slice_in_dim(norm_gain, d * cols_core, cols_core, 0)
     normed = (hidden * inverse * gain.astype(F32)[None, :]).astype(BF16)
 
-    codes = slot_codes(expert_ids, experts)
-    route = jnp.concatenate([codes.T, route_weights.T], axis=0)
+    route = pl.pallas_call(
+        functools.partial(codes_kernel, experts),
+        out_shape=jax.ShapeDtypeStruct((2 * choices, rows), F32),
+        in_specs=[VMEM, VMEM],
+        out_specs=VMEM,
+        compiler_params=SMALL,
+        name="codes",
+    )(expert_ids, route_weights)
     route = jnp.stack([fetch(route, "dp", i) for i in range(cores)])
     routes = [route]
     for o in range(1, depth):
         routes.append(across(route, "expert", o))
-    route = jnp.stack(routes)
     groups = tensors if sub == 1 else 1
     blocks = depth * cores // groups
     group_slots = held * blocks * SLOT
-    local = route[:, :, :choices] - ((z * cores + d) * held * SLOT).astype(F32)
-    valid = (local >= 0) & (local < held * SLOT)
-    which = jnp.floor(local / SLOT)
-    block_ids = jnp.arange(depth, dtype=F32)[:, None, None, None]
-    if groups == 1:
+    first_code = (z * cores + d) * held * SLOT
+    if groups > 1:
+        placing, back = pl.pallas_call(
+            functools.partial(tables_kernel, choices),
+            out_shape=[
+                jax.ShapeDtypeStruct((cores, group_slots, depth * rows), BF16),
+                jax.ShapeDtypeStruct((cores, depth * rows, group_slots), BF16),
+            ],
+            in_specs=[SMEM] + [VMEM] * depth,
+            out_specs=[VMEM, VMEM],
+            compiler_params=SMALL,
+            name="tables",
+        )(first_code.astype(jnp.int32).reshape(1), *routes)
+    else:
+        route = jnp.stack(routes)
+        local = route[:, :, :choices] - first_code.astype(F32)
+        valid = (local >= 0) & (local < held * SLOT)
+        which = jnp.floor(local / SLOT)
+        block_ids = jnp.arange(depth, dtype=F32)[:, None, None, None]
         block_ids = block_ids * cores + jnp.arange(cores, dtype=F32)[None, :, None, None]
-    slot = which * (blocks * SLOT) + block_ids * SLOT + (local - which * SLOT)
-    slot = jnp.where(valid, slot, -1.0)
-    weights = route[:, :, choices:]
-    by_core = slot.transpose(1, 2, 0, 3).reshape(cores, choices, depth * rows, 1)
-    weight_by_core = weights.transpose(1, 2, 0, 3).reshape(cores, choices, depth * rows, 1)
-    slot_ids = jnp.arange(group_slots, dtype=F32)
-    back = jnp.sum(jnp.where(by_core == slot_ids, weight_by_core, 0.0), axis=1).astype(BF16)
-    if groups > 1:
-        table = slot.transpose(1, 2, 0, 3).reshape(groups, choices, depth * rows)
-    else:
+        slot = which * (blocks * SLOT) + block_ids * SLOT + (local - which * SLOT)
+        slot = jnp.where(valid, slot, -1.0)
+        weights = route[:, :, choices:]
+        by_core = slot.transpose(1, 2, 0, 3).reshape(cores, choices, depth * rows, 1)
+        weight_by_core = weights.transpose(1, 2, 0, 3).reshape(cores, choices, depth * rows, 1)
+        slot_ids = jnp.arange(group_slots, dtype=F32)
+        back = jnp.sum(jnp.where(by_core == slot_ids, weight_by_core, 0.0), axis=1).astype(BF16)
         table = slot.reshape(depth, cores, choices, sub, part)
         table = table.transpose(1, 3, 2, 0, 4).reshape(tensors, choices, depth * part)
         table = jnp.stack([pick(table, place((x + k) % tensors)) for k in range(tensors)])
         table = table.transpose(1, 0, 2).reshape(1, choices, -1)
-    placing = jnp.any(table[:, :, None, :] == slot_ids[:, None], axis=1).astype(BF16)
+        placing = jnp.any(table[:, :, None, :] == slot_ids[:, None], axis=1).astype(BF16)
 
     along = [normed]
     mine = {}
@@ -254,9 +301,6 @@
             along.append(across(along[o & (o - 1)], "expert", o & -o))
     if sub > 1:
         along = [jnp.concatenate(along, axis=0)]
-    else:
-        held_back = lax.optimization_barrier((along[-1], placing, back))
-        along[-1], placing, back = held_back
     for o, value in enumerate(along):
         for k in range(tensors):
             mine[k, o] = fetch(value, "tensor", k)
@@ -324,13 +368,17 @@
                 name="experts_later",
             )(sel, back, activated, w_down)
         at += span
-        summed = outs[0].astype(F32)
-        for i in range(1, cores):
-            got = fetch(outs[i], "dp", -i)
-            summed = summed + got.astype(F32)
-        narrow = summed[0]
-        for t in range(1, tensors):
-            got = fetch(summed[t].astype(BF16), "tensor", -t)
+        sides = []
+        for t in list(range(1, tensors)) + [0]:
+            summed = outs[0][t].astype(F32)
+            for i in range(1, cores):
+                got = fetch(outs[i][t], "dp", -i)
+                summed = summed + got.astype(F32)
+            if t > 0:
+                got = fetch(summed.astype(BF16), "tensor", -t)
+                sides.append(got)
+        narrow = summed
+        for got in sides:
             narrow = narrow + got.astype(F32)
         narrow = narrow.reshape(depth, rows, span)
         flip = 1

time: 135 us -> 160 us (1.19)
  waiting for transfers between devices: 67.6 us -> 81.2 us
  Pallas kernels: 27.7 us -> 34.5 us
  starting transfers between devices: 21.9 us -> 28.4 us
  other arithmetic: 10.7 us -> 4.88 us
  local copies, waits for them, and re-layouts: 1.16 us -> 5.38 us
    ppermute x10 -> x12, waiting for transfers between devices: 29.9 us -> 38.6 us  [across(): return lax.ppermute(value, axis, [(i ^ flip, i) for i in range(size)])]
    ppermute x21 -> x26, waiting for transfers between devices: 37.7 us -> 42.6 us  [fetch(): lax.ppermute(value, axis, [((i + step) % size, i) for i in range(size)])]
    ppermute x21 -> x26, starting transfers between devices: 10.4 us -> 14.7 us  [fetch(): lax.ppermute(value, axis, [((i + step) % size, i) for i in range(size)])]
    reduce_sum x3 -> x0, other arithmetic: 3.81 us -> none  [the longest x1 2.38 us: on_device(): jnp.sum(jnp.where(by_core == slot_ids, weight_by_core, 0.0), axis=1)]
    pallas_call x0 -> x2, Pallas kernels: none -> 3.55 us  [the longest x1 3.08 us: on_device(): pl.pallas_call(functools.partial(tables_kernel, choices), out_shape=[jax....]
    pallas_call x1 -> x2, Pallas kernels: 8.03 us -> 11.3 us  [on_device(): pl.pallas_call(functools.partial(later_kernel, (cores, tensors, groups, a...]
    unnamed x30 -> x44, local copies, waits for them, and re-layouts: 0.06 us -> 2.42 us
    ppermute x10 -> x12, starting transfers between devices: 11.5 us -> 13.8 us  [across(): return lax.ppermute(value, axis, [(i ^ flip, i) for i in range(size)])]
  transfers between devices with their start and end apart: 31 -> 38, of which waited for: 14 -> 19; matrix products, arithmetic and copies ran while one was open for 12% -> 4% of each run, Pallas kernels for 6% -> 6%
where the time goes in v3:
time: 160 us
  waiting for transfers between devices  81.2 us (51%)
  Pallas kernels  34.5 us (22%)
  starting transfers between devices  28.4 us (18%)
  local copies, waits for them, and re-layouts  5.38 us (3%)
  other arithmetic  4.88 us (3%)
  matrix products  4.71 us (3%)
    ppermute x26, waiting for transfers between devices, fetch(): lax.ppermute(value, axis, [((i + step) % size, i) for i in range(size)])  42.6 us
    ppermute x12, waiting for transfers between devices, across(): return lax.ppermute(value, axis, [(i ^ flip, i) for i in range(size)])  38.6 us
    pallas_call x1, Pallas kernels, on_device(): pl.pallas_call(functools.partial(first_kernel, (cores, tensors, depth, gr...  19.6 us
    ppermute x26, starting transfers between devices, fetch(): lax.ppermute(value, axis, [((i + step) % size, i) for i in range(size)])  14.7 us
    ppermute x12, starting transfers between devices, across(): return lax.ppermute(value, axis, [(i ^ flip, i) for i in range(size)])  13.8 us
    pallas_call x2, Pallas kernels, on_device(): pl.pallas_call(functools.partial(later_kernel, (cores, tensors, groups, a...  11.3 us
    dot_general x1, matrix products, on_device(): partial = jnp.dot(attn_all, o_weight, preferred_element_type=F32)  4.71 us
  transfers between devices with their start and end apart: 38, of which 19 were waited for; matrix products, arithmetic and copies ran while one was open for 4% of the time, Pallas kernels for 6%

profile of v3, /device:TPU:0, one launch (start us, length us, event | category | flops | bytes accessed | tf_op | source)
XLA Modules:
  0.0 159.6 jit_solution(4715511221977614649)
XLA Ops:
  0.6 1.3 collective-permute-done.4
  2.2 4.7 %convolution_add_fusion = f32[128,2048]{1,0:T(8,128)S(1)} fusion(bf16[2048,2048]{1,0:T(8,128)(2,1)} %param.10, bf16[64,2048]{1,0:T(8,128)(2,1)S(1)} %collective-permute-done.4, bf16[64,2048]{1,0:T(8,128)(2,1)} %param.9, bf16[64,2048]{1,0:T(8,128)(2,1)S(1)} %collective-permute-done.5, bf16[64,2048]{1,0:T(8,128)(2,1)} %param.11, pred[]{:T(512)S(6)} %eq.15), kind=kOutput, calls=%fused_computation | convolution fusion | flops 1076363264 | bytes 10485761 | tf_op jit(solution)/shard_map/dot_general | solution.py:222
  7.0 2.9 %collective-permute-start.6 = (bf16[64,2048]{1,0:T(8,128)(2,1)S(1)}, bf16[64,2048]{1,0:T(8,128)(2,1)S(1)}, u32[]{:S(2)}, u32[]{:S(2)}) collective-permute-start(bf16[64,2048]{1,0:T(8,128)(2,1)S(1)} %fusion.15), channel_id=1, source_target_pairs={{2,0},{0,2},{3,1},{1,3},{6,4},{4,6},{7,5},{5,7},{10,8},{8,10},{11,... | collective-permute-start | bytes 786440 | tf_op jit(solution)/shard_map/ppermute | solution.py:22
  9.9 6.6 %collective-permute-done.6 = bf16[64,2048]{1,0:T(8,128)(2,1)S(1)} collective-permute-done((bf16[64,2048]{1,0:T(8,128)(2,1)S(1)}, bf16[64,2048]{1,0:T(8,128)(2,1)S(1)}, u32[]{:S(2)}, u32[]{:S(2)}) %collective-permute-start.6) | collective-permute-done | bytes 262176 | tf_op jit(solution)/shard_map/ppermute | solution.py:22
  18.1 2.9 %collective-permute-start.9 = (bf16[64,2048]{1,0:T(8,128)(2,1)S(1)}, bf16[64,2048]{1,0:T(8,128)(2,1)S(1)}, u32[]{:S(2)}, u32[]{:S(2)}) collective-permute-start(bf16[64,2048]{1,0:T(8,128)(2,1)S(1)} %fusion.6.rest_0_), channel_id=1, source_target_pairs={{8,0},{12,4},{0,8},{4,12},{9,1},{13,5},{1,9},{5,13},{10,2},{14,6},... | collective-permute-start | bytes 786440 | tf_op jit(solution)/shard_map/ppermute | solution.py:27
  21.0 1.5 collective-permute-start.11
  22.5 1.6 collective-permute-start.8
  24.1 9.3 %collective-permute-done.9.rest_2_ = bf16[64,2048]{1,0:T(8,128)(2,1)S(1)} collective-permute-done((bf16[64,2048]{1,0:T(8,128)(2,1)S(1)}, bf16[64,2048]{1,0:T(8,128)(2,1)S(1)}, u32[]{:S(2)}, u32[]{:S(2)}) %collective-permute-start.9) | collective-permute-done | bytes 262176 | tf_op jit(solution)/shard_map/ppermute | solution.py:27
  35.9 2.9 %collective-permute-start.3 = (f32[2,16,64]{2,1,0:T(8,128)S(1)}, f32[2,16,64]{2,1,0:T(8,128)S(1)}, u32[]{:S(2)}, u32[]{:S(2)}) collective-permute-start(f32[2,16,64]{2,1,0:T(8,128)S(1)} %pad_maximum_fusion.1.rest_0_), channel_id=1, source_target_pairs={{12,0},{8,4},{4,8},{0,12},{13,1},{9,5},{5,9},{1,13},{14,2},{10,6},... | collective-permute-start | bytes 24584 | tf_op jit(solution)/shard_map/ppermute | solution.py:27
  38.8 4.9 %collective-permute-done.3.rest_3_ = f32[2,16,64]{2,1,0:T(8,128)S(1)} collective-permute-done((f32[2,16,64]{2,1,0:T(8,128)S(1)}, f32[2,16,64]{2,1,0:T(8,128)S(1)}, u32[]{:S(2)}, u32[]{:S(2)}) %collective-permute-start.3) | collective-permute-done | bytes 8224 | tf_op jit(solution)/shard_map/ppermute | solution.py:27
  43.7 4.6 %collective-permute-done.2.rest_2_ = f32[2,16,64]{2,1,0:T(8,128)S(1)} collective-permute-done((f32[2,16,64]{2,1,0:T(8,128)S(1)}, f32[2,16,64]{2,1,0:T(8,128)S(1)}, u32[]{:S(2)}, u32[]{:S(2)}) %collective-permute-start.2) | collective-permute-done | bytes 8224 | tf_op jit(solution)/shard_map/ppermute | solution.py:27
  48.4 3.6 %collective-permute-done.1.rest_1_ = f32[2,16,64]{2,1,0:T(8,128)S(1)} collective-permute-done((f32[2,16,64]{2,1,0:T(8,128)S(1)}, f32[2,16,64]{2,1,0:T(8,128)S(1)}, u32[]{:S(2)}, u32[]{:S(2)}) %collective-permute-start.1) | collective-permute-done | bytes 8224 | tf_op jit(solution)/shard_map/ppermute | solution.py:27
  52.1 1.6 collective-permute-start.13
  54.2 1.5 collective-permute-start.14
  56.2 5.1 %collective-permute-done.13.rest_6_ = bf16[64,2048]{1,0:T(8,128)(2,1)S(1)} collective-permute-done((bf16[64,2048]{1,0:T(8,128)(2,1)S(1)}, bf16[64,2048]{1,0:T(8,128)(2,1)S(1)}, u32[]{:S(2)}, u32[]{:S(2)}) %collective-permute-start.13) | collective-permute-done | bytes 262176 | tf_op jit(solution)/shard_map/ppermute | solution.py:22
  61.3 5.6 %collective-permute-done.12.rest_5_ = bf16[64,2048]{1,0:T(8,128)(2,1)S(1)} collective-permute-done((bf16[64,2048]{1,0:T(8,128)(2,1)S(1)}, bf16[64,2048]{1,0:T(8,128)(2,1)S(1)}, u32[]{:S(2)}, u32[]{:S(2)}) %collective-permute-start.12) | collective-permute-done | bytes 262176 | tf_op jit(solution)/shard_map/ppermute | solution.py:22
  66.9 5.1 %collective-permute-done.14.rest_7_ = bf16[64,2048]{1,0:T(8,128)(2,1)S(1)} collective-permute-done((bf16[64,2048]{1,0:T(8,128)(2,1)S(1)}, bf16[64,2048]{1,0:T(8,128)(2,1)S(1)}, u32[]{:S(2)}, u32[]{:S(2)}) %collective-permute-start.14) | collective-permute-done | bytes 262176 | tf_op jit(solution)/shard_map/ppermute | solution.py:22
  72.6 3.1 %tables.1 = (bf16[2,384,256]{2,1,0:T(8,128)(2,1)S(1)}, bf16[2,256,384]{2,1,0:T(8,128)(2,1)S(1)}) custom-call(s32[1]{0:T(128)} %bitcast.6.base_ref, f32[2,16,64]{2,1,0:T(8,128)S(1)} %pad_maximum_fusion.1.rest_0_, f32[2,16,64]{2,1,0:T(8,128)S(1)} %collective-permute-done.1.rest_1_, f32[2,16,64]{2,1,0:T(8,128)S(1)} %collective-permute-done.2.rest_2_, ...), custom_call_target="tpu_custom_call" | custom-call | tf_op jit(solution)/shard_map/tables/pallas_call | solution.py:266
  78.1 19.6 %experts_first.1 = (bf16[4,192,512]{2,1,0:T(8,128)(2,1)}, bf16[2,256,1024]{2,1,0:T(8,128)(2,1)}, bf16[2,256,1024]{2,1,0:T(8,128)(2,1)}) custom-call(s32[6]{0:T(128)} %stack.36.sel_ref, bf16[2,384,256]{2,1,0:T(8,128)(2,1)} %copy-done.1, bf16[2,256,384]{2,1,0:T(8,128)(2,1)} %copy-done, bf16[64,2048]{1,0:T(8,128)(2,1)} %copy-done.2, ...), custom_call_target="tpu_custom_call" | custom-call | tf_op jit(solution)/shard_map/experts_first/pallas_call | solution.py:331
  97.7 4.7 %experts_later.3 = (bf16[2,256,256]{2,1,0:T(8,128)(2,1)}, bf16[2,256,256]{2,1,0:T(8,128)(2,1)}) custom-call(s32[6]{0:T(128)} %stack.36.sel_ref, bf16[2,256,384]{2,1,0:T(8,128)(2,1)} %copy-done, bf16[4,192,512]{2,1,0:T(8,128)(2,1)} %get-tuple-element.18.act_ref, bf16[4,512,4096]{2,1,0:T(8,128)(2,1)} %wd_ref.3), custom_call_target="tpu_custom_call" | custom-call | flops 805306368 | bytes 2097152 | tf_op jit(solution)/shard_map/experts_later/pallas_call | solution.py:356
  105.9 1.6 collective-permute-start.35
  107.5 6.7 %experts_later.2 = (bf16[2,256,768]{2,1,0:T(8,128)(2,1)}, bf16[2,256,768]{2,1,0:T(8,128)(2,1)}) custom-call(s32[6]{0:T(128)} %stack.36.sel_ref, bf16[2,256,384]{2,1,0:T(8,128)(2,1)} %copy-done, bf16[4,192,512]{2,1,0:T(8,128)(2,1)} %get-tuple-element.18.act_ref, bf16[4,512,4096]{2,1,0:T(8,128)(2,1)} %wd_ref.3), custom_call_target="tpu_custom_call" | custom-call | flops 2415919104 | bytes 6291456 | tf_op jit(solution)/shard_map/experts_later/pallas_call | solution.py:356
  116.6 2.0 %collective-permute-done.36 = bf16[2,64,256]{2,1,0:T(8,128)(2,1)S(1)} collective-permute-done((bf16[2,64,256]{2,1,0:T(8,128)(2,1)S(1)}, bf16[2,64,256]{2,1,0:T(8,128)(2,1)S(1)}, u32[]{:S(2)}, u32[]{:S(2)}) %collective-permute-start.36) | collective-permute-done | bytes 65568 | tf_op jit(solution)/shard_map/ppermute | solution.py:27
  120.7 1.6 collective-permute-start.25
  122.2 1.3 collective-permute-done.37
  123.5 8.4 %collective-permute-done.30 = bf16[256,768]{1,0:T(8,128)(2,1)S(1)} collective-permute-done((bf16[256,768]{1,0:T(8,128)(2,1)S(1)}, bf16[256,768]{1,0:T(8,128)(2,1)S(1)}, u32[]{:S(2)}, u32[]{:S(2)}) %collective-permute-start.30) | collective-permute-done | bytes 393248 | tf_op jit(solution)/shard_map/ppermute | solution.py:22
  133.1 1.4 collective-permute-start.31
  134.5 6.9 %collective-permute-done.25 = bf16[256,1024]{1,0:T(8,128)(2,1)S(1)} collective-permute-done((bf16[256,1024]{1,0:T(8,128)(2,1)S(1)}, bf16[256,1024]{1,0:T(8,128)(2,1)S(1)}, u32[]{:S(2)}, u32[]{:S(2)}) %collective-permute-start.25) | collective-permute-done | bytes 524320 | tf_op jit(solution)/shard_map/ppermute | solution.py:22
  141.7 2.1 %collective-permute-start.26 = (bf16[2,64,1024]{2,1,0:T(8,128)(2,1)S(1)}, bf16[2,64,1024]{2,1,0:T(8,128)(2,1)S(1)}, u32[]{:S(2)}, u32[]{:S(2)}) collective-permute-start(bf16[2,64,1024]{2,1,0:T(8,128)(2,1)S(1)} %fusion.16), channel_id=1, source_target_pairs={{4,0},{0,4},{12,8},{8,12},{5,1},{1,5},{13,9},{9,13},{6,2},{2,6},{1... | collective-permute-start | bytes 786440 | tf_op jit(solution)/shard_map/ppermute | solution.py:27
  143.8 1.5 collective-permute-start.32
  145.3 6.1 %collective-permute-done.26 = bf16[2,64,1024]{2,1,0:T(8,128)(2,1)S(1)} collective-permute-done((bf16[2,64,1024]{2,1,0:T(8,128)(2,1)S(1)}, bf16[2,64,1024]{2,1,0:T(8,128)(2,1)S(1)}, u32[]{:S(2)}, u32[]{:S(2)}) %collective-permute-start.26) | collective-permute-done | bytes 262176 | tf_op jit(solution)/shard_map/ppermute | solution.py:27
  152.1 6.8 %collective-permute-done.27 = bf16[1,64,1024]{2,1,0:T(8,128)(2,1)S(1)} collective-permute-done((bf16[1,64,1024]{2,1,0:T(8,128)(2,1)S(1)}, bf16[1,64,1024]{2,1,0:T(8,128)(2,1)S(1)}, u32[]{:S(2)}, u32[]{:S(2)}) %collective-permute-start.27) | collective-permute-done | bytes 131104 | tf_op jit(solution)/shard_map/ppermute | solution.py:27
  (123 shorter events, 19.9 us)
Async XLA Ops:
  7.0 9.5 %collective-permute-start.6 = (bf16[64,2048]{1,0:T(8,128)(2,1)S(1)}, bf16[64,2048]{1,0:T(8,128)(2,1)S(1)}, u32[]{:S(2)}, u32[]{:S(2)}) collective-permute-start(bf16[64,2048]{1,0:T(8,128)(2,1)S(1)} %fusion.15), channel_id=1, source_target_pairs={{2,0},{0,2},{3,1},{1,3},{6,4},{4,6},{7,5},{5,7},{10,8},{8,10},{11,... | collective-permute-start | bytes 786440 | tf_op jit(solution)/shard_map/ppermute | solution.py:22
  18.1 15.3 %collective-permute-start.9 = (bf16[64,2048]{1,0:T(8,128)(2,1)S(1)}, bf16[64,2048]{1,0:T(8,128)(2,1)S(1)}, u32[]{:S(2)}, u32[]{:S(2)}) collective-permute-start(bf16[64,2048]{1,0:T(8,128)(2,1)S(1)} %fusion.6.rest_0_), channel_id=1, source_target_pairs={{8,0},{12,4},{0,8},{4,12},{9,1},{13,5},{1,9},{5,13},{10,2},{14,6},... | collective-permute-start | bytes 786440 | tf_op jit(solution)/shard_map/ppermute | solution.py:27
  21.0 27.3 %collective-permute-start.11 = (bf16[64,2048]{1,0:T(8,128)(2,1)S(1)}, bf16[64,2048]{1,0:T(8,128)(2,1)S(1)}, u32[]{:S(2)}, u32[]{:S(2)}) collective-permute-start(bf16[64,2048]{1,0:T(8,128)(2,1)S(1)} %fusion.6.rest_0_), channel_id=1, source_target_pairs={{2,0},{0,2},{3,1},{1,3},{6,4},{4,6},{7,5},{5,7},{10,8},{8,10},{11,... | collective-permute-start | bytes 786440 | tf_op jit(solution)/shard_map/ppermute | solution.py:22
  22.5 29.6 %collective-permute-start.15 = (bf16[64,2048]{1,0:T(8,128)(2,1)S(1)}, bf16[64,2048]{1,0:T(8,128)(2,1)S(1)}, u32[]{:S(2)}, u32[]{:S(2)}) collective-permute-start(bf16[64,2048]{1,0:T(8,128)(2,1)S(1)} %fusion.6.rest_0_), channel_id=1, source_target_pairs={{1,0},{0,1},{3,2},{2,3},{5,4},{4,5},{7,6},{6,7},{9,8},{8,9},{11,10... | collective-permute-start | bytes 786440 | tf_op jit(solution)/shard_map/ppermute | solution.py:22
  22.5 31.2 %collective-permute-start.8 = (bf16[64,2048]{1,0:T(8,128)(2,1)S(1)}, bf16[64,2048]{1,0:T(8,128)(2,1)S(1)}, u32[]{:S(2)}, u32[]{:S(2)}) collective-permute-start(bf16[64,2048]{1,0:T(8,128)(2,1)S(1)} %fusion.6.rest_0_), channel_id=1, source_target_pairs={{4,0},{0,4},{12,8},{8,12},{5,1},{1,5},{13,9},{9,13},{6,2},{2,6},{1... | collective-permute-start | bytes 786440 | tf_op jit(solution)/shard_map/ppermute | solution.py:27
  33.4 20.8 %collective-permute-start.10 = (bf16[64,2048]{1,0:T(8,128)(2,1)S(1)}, bf16[64,2048]{1,0:T(8,128)(2,1)S(1)}, u32[]{:S(2)}, u32[]{:S(2)}) collective-permute-start(bf16[64,2048]{1,0:T(8,128)(2,1)S(1)} %collective-permute-done.9.rest_2_), channel_id=1, source_target_pairs={{4,0},{0,4},{12,8},{8,12},{5,1},{1,5},{13,9},{9,13},{6,2},{2,6},{1... | collective-permute-start | bytes 786440 | tf_op jit(solution)/shard_map/ppermute | solution.py:27
  35.9 7.8 %collective-permute-start.3 = (f32[2,16,64]{2,1,0:T(8,128)S(1)}, f32[2,16,64]{2,1,0:T(8,128)S(1)}, u32[]{:S(2)}, u32[]{:S(2)}) collective-permute-start(f32[2,16,64]{2,1,0:T(8,128)S(1)} %pad_maximum_fusion.1.rest_0_), channel_id=1, source_target_pairs={{12,0},{8,4},{4,8},{0,12},{13,1},{9,5},{5,9},{1,13},{14,2},{10,6},... | collective-permute-start | bytes 24584 | tf_op jit(solution)/shard_map/ppermute | solution.py:27
  43.7 4.6 %collective-permute-start.2 = (f32[2,16,64]{2,1,0:T(8,128)S(1)}, f32[2,16,64]{2,1,0:T(8,128)S(1)}, u32[]{:S(2)}, u32[]{:S(2)}) collective-permute-start(f32[2,16,64]{2,1,0:T(8,128)S(1)} %pad_maximum_fusion.1.rest_0_), channel_id=1, source_target_pairs={{8,0},{12,4},{0,8},{4,12},{9,1},{13,5},{1,9},{5,13},{10,2},{14,6},... | collective-permute-start | bytes 24584 | tf_op jit(solution)/shard_map/ppermute | solution.py:27
  48.3 3.7 %collective-permute-start.1 = (f32[2,16,64]{2,1,0:T(8,128)S(1)}, f32[2,16,64]{2,1,0:T(8,128)S(1)}, u32[]{:S(2)}, u32[]{:S(2)}) collective-permute-start(f32[2,16,64]{2,1,0:T(8,128)S(1)} %pad_maximum_fusion.1.rest_0_), channel_id=1, source_target_pairs={{4,0},{0,4},{12,8},{8,12},{5,1},{1,5},{13,9},{9,13},{6,2},{2,6},{1... | collective-permute-start | bytes 24584 | tf_op jit(solution)/shard_map/ppermute | solution.py:27
  48.3 7.3 %collective-permute-start.19 = (bf16[64,2048]{1,0:T(8,128)(2,1)S(1)}, bf16[64,2048]{1,0:T(8,128)(2,1)S(1)}, u32[]{:S(2)}, u32[]{:S(2)}) collective-permute-start(bf16[64,2048]{1,0:T(8,128)(2,1)S(1)} %collective-permute-done.11.rest_4_), channel_id=1, source_target_pairs={{1,0},{0,1},{3,2},{2,3},{5,4},{4,5},{7,6},{6,7},{9,8},{8,9},{11,10... | collective-permute-start | bytes 786440 | tf_op jit(solution)/shard_map/ppermute | solution.py:22
  52.1 3.6 %collective-permute-start.17 = (bf16[64,2048]{1,0:T(8,128)(2,1)S(1)}, bf16[64,2048]{1,0:T(8,128)(2,1)S(1)}, u32[]{:S(2)}, u32[]{:S(2)}) collective-permute-start(bf16[64,2048]{1,0:T(8,128)(2,1)S(1)} %collective-permute-done.9.rest_2_), channel_id=1, source_target_pairs={{1,0},{0,1},{3,2},{2,3},{5,4},{4,5},{7,6},{6,7},{9,8},{8,9},{11,10... | collective-permute-start | bytes 786440 | tf_op jit(solution)/shard_map/ppermute | solution.py:22
  52.1 9.2 %collective-permute-start.13 = (bf16[64,2048]{1,0:T(8,128)(2,1)S(1)}, bf16[64,2048]{1,0:T(8,128)(2,1)S(1)}, u32[]{:S(2)}, u32[]{:S(2)}) collective-permute-start(bf16[64,2048]{1,0:T(8,128)(2,1)S(1)} %collective-permute-done.9.rest_2_), channel_id=1, source_target_pairs={{2,0},{0,2},{3,1},{1,3},{6,4},{4,6},{7,5},{5,7},{10,8},{8,10},{11,... | collective-permute-start | bytes 786440 | tf_op jit(solution)/shard_map/ppermute | solution.py:22
  53.6 13.3 %collective-permute-start.12 = (bf16[64,2048]{1,0:T(8,128)(2,1)S(1)}, bf16[64,2048]{1,0:T(8,128)(2,1)S(1)}, u32[]{:S(2)}, u32[]{:S(2)}) collective-permute-start(bf16[64,2048]{1,0:T(8,128)(2,1)S(1)} %collective-permute-done.8.rest_1_), channel_id=1, source_target_pairs={{2,0},{0,2},{3,1},{1,3},{6,4},{4,6},{7,5},{5,7},{10,8},{8,10},{11,... | collective-permute-start | bytes 786440 | tf_op jit(solution)/shard_map/ppermute | solution.py:22
  54.2 17.8 %collective-permute-start.14 = (bf16[64,2048]{1,0:T(8,128)(2,1)S(1)}, bf16[64,2048]{1,0:T(8,128)(2,1)S(1)}, u32[]{:S(2)}, u32[]{:S(2)}) collective-permute-start(bf16[64,2048]{1,0:T(8,128)(2,1)S(1)} %collective-permute-done.10.rest_3_), channel_id=1, source_target_pairs={{2,0},{0,2},{3,1},{1,3},{6,4},{4,6},{7,5},{5,7},{10,8},{8,10},{11,... | collective-permute-start | bytes 786440 | tf_op jit(solution)/shard_map/ppermute | solution.py:22
  55.7 21.5 %collective-permute-start.16 = (bf16[64,2048]{1,0:T(8,128)(2,1)S(1)}, bf16[64,2048]{1,0:T(8,128)(2,1)S(1)}, u32[]{:S(2)}, u32[]{:S(2)}) collective-permute-start(bf16[64,2048]{1,0:T(8,128)(2,1)S(1)} %collective-permute-done.8.rest_1_), channel_id=1, source_target_pairs={{1,0},{0,1},{3,2},{2,3},{5,4},{4,5},{7,6},{6,7},{9,8},{8,9},{11,10... | collective-permute-start | bytes 786440 | tf_op jit(solution)/shard_map/ppermute | solution.py:22
  55.7 21.5 %collective-permute-start.18 = (bf16[64,2048]{1,0:T(8,128)(2,1)S(1)}, bf16[64,2048]{1,0:T(8,128)(2,1)S(1)}, u32[]{:S(2)}, u32[]{:S(2)}) collective-permute-start(bf16[64,2048]{1,0:T(8,128)(2,1)S(1)} %collective-permute-done.10.rest_3_), channel_id=1, source_target_pairs={{1,0},{0,1},{3,2},{2,3},{5,4},{4,5},{7,6},{6,7},{9,8},{8,9},{11,10... | collective-permute-start | bytes 786440 | tf_op jit(solution)/shard_map/ppermute | solution.py:22
  61.3 15.9 %collective-permute-start.21 = (bf16[64,2048]{1,0:T(8,128)(2,1)S(1)}, bf16[64,2048]{1,0:T(8,128)(2,1)}, u32[]{:S(2)}, u32[]{:S(2)}) collective-permute-start(bf16[64,2048]{1,0:T(8,128)(2,1)S(1)} %collective-permute-done.13.rest_6_), channel_id=1, source_target_pairs={{1,0},{0,1},{3,2},{2,3},{5,4},{4,5},{7,6},{6,7},{9,8},{8,9},{11,10... | collective-permute-start | bytes 786440 | tf_op jit(solution)/shard_map/ppermute | solution.py:22
  66.9 10.3 %collective-permute-start.20 = (bf16[64,2048]{1,0:T(8,128)(2,1)S(1)}, bf16[64,2048]{1,0:T(8,128)(2,1)}, u32[]{:S(2)}, u32[]{:S(2)}) collective-permute-start(bf16[64,2048]{1,0:T(8,128)(2,1)S(1)} %collective-permute-done.12.rest_5_), channel_id=1, source_target_pairs={{1,0},{0,1},{3,2},{2,3},{5,4},{4,5},{7,6},{6,7},{9,8},{8,9},{11,10... | collective-permute-start | bytes 786440 | tf_op jit(solution)/shard_map/ppermute | solution.py:22
  72.0 5.2 %collective-permute-start.22 = (bf16[64,2048]{1,0:T(8,128)(2,1)S(1)}, bf16[64,2048]{1,0:T(8,128)(2,1)}, u32[]{:S(2)}, u32[]{:S(2)}) collective-permute-start(bf16[64,2048]{1,0:T(8,128)(2,1)S(1)} %collective-permute-done.14.rest_7_), channel_id=1, source_target_pairs={{1,0},{0,1},{3,2},{2,3},{5,4},{4,5},{7,6},{6,7},{9,8},{8,9},{11,10... | collective-permute-start | bytes 786440 | tf_op jit(solution)/shard_map/ppermute | solution.py:22
  104.0 10.1 %collective-permute-start.33 = (bf16[256,256]{1,0:T(8,128)(2,1)S(1)}, bf16[256,256]{1,0:T(8,128)(2,1)S(1)}, u32[]{:S(2)}, u32[]{:S(2)}) collective-permute-start(bf16[256,256]{1,0:T(8,128)(2,1)S(1)} %get-tuple-element.29), channel_id=1, source_target_pairs={{1,0},{0,1},{3,2},{2,3},{5,4},{4,5},{7,6},{6,7},{9,8},{8,9},{11,10... | collective-permute-start | bytes 393224 | tf_op jit(solution)/shard_map/ppermute | solution.py:22
  105.9 8.3 %collective-permute-start.35 = (bf16[256,256]{1,0:T(8,128)(2,1)S(1)}, bf16[256,256]{1,0:T(8,128)(2,1)S(1)}, u32[]{:S(2)}, u32[]{:S(2)}) collective-permute-start(bf16[256,256]{1,0:T(8,128)(2,1)S(1)} %fusion.19), channel_id=1, source_target_pairs={{2,0},{0,2},{3,1},{1,3},{6,4},{4,6},{7,5},{5,7},{10,8},{8,10},{11,... | collective-permute-start | bytes 393224 | tf_op jit(solution)/shard_map/ppermute | solution.py:22
  114.2 4.3 %collective-permute-start.36 = (bf16[2,64,256]{2,1,0:T(8,128)(2,1)S(1)}, bf16[2,64,256]{2,1,0:T(8,128)(2,1)S(1)}, u32[]{:S(2)}, u32[]{:S(2)}) collective-permute-start(bf16[2,64,256]{2,1,0:T(8,128)(2,1)S(1)} %fusion.30), channel_id=1, source_target_pairs={{4,0},{0,4},{12,8},{8,12},{5,1},{1,5},{13,9},{9,13},{6,2},{2,6},{1... | collective-permute-start | bytes 196616 | tf_op jit(solution)/shard_map/ppermute | solution.py:27
  115.5 8.0 %collective-permute-start.28 = (bf16[256,768]{1,0:T(8,128)(2,1)S(1)}, bf16[256,768]{1,0:T(8,128)(2,1)S(1)}, u32[]{:S(2)}, u32[]{:S(2)}) collective-permute-start(bf16[256,768]{1,0:T(8,128)(2,1)S(1)} %get-tuple-element.27), channel_id=1, source_target_pairs={{1,0},{0,1},{3,2},{2,3},{5,4},{4,5},{7,6},{6,7},{9,8},{8,9},{11,10... | collective-permute-start | bytes 1179656 | tf_op jit(solution)/shard_map/ppermute | solution.py:22
  116.1 18.4 %collective-permute-start.23 = (bf16[256,1024]{1,0:T(8,128)(2,1)S(1)}, bf16[256,1024]{1,0:T(8,128)(2,1)S(1)}, u32[]{:S(2)}, u32[]{:S(2)}) collective-permute-start(bf16[256,1024]{1,0:T(8,128)(2,1)S(1)} %get-tuple-element.25), channel_id=1, source_target_pairs={{1,0},{0,1},{3,2},{2,3},{5,4},{4,5},{7,6},{6,7},{9,8},{8,9},{11,10... | collective-permute-start | bytes 1572872 | tf_op jit(solution)/shard_map/ppermute | solution.py:22
  116.2 4.3 %collective-permute-start.24 = (bf16[256,1024]{1,0:T(8,128)(2,1)S(1)}, bf16[256,1024]{1,0:T(8,128)(2,1)S(1)}, u32[]{:S(2)}, u32[]{:S(2)}) collective-permute-start(bf16[256,1024]{1,0:T(8,128)(2,1)S(1)} %get-tuple-element.26), channel_id=1, source_target_pairs={{1,0},{0,1},{3,2},{2,3},{5,4},{4,5},{7,6},{6,7},{9,8},{8,9},{11,10... | collective-permute-start | bytes 1572872 | tf_op jit(solution)/shard_map/ppermute | solution.py:22
  118.6 4.9 %collective-permute-start.37 = (bf16[1,64,256]{2,1,0:T(8,128)(2,1)S(1)}, bf16[1,64,256]{2,1,0:T(8,128)(2,1)S(1)}, u32[]{:S(2)}, u32[]{:S(2)}) collective-permute-start(bf16[1,64,256]{2,1,0:T(8,128)(2,1)S(1)} %fusion.34), channel_id=1, source_target_pairs={{8,0},{12,4},{0,8},{4,12},{9,1},{13,5},{1,9},{5,13},{10,2},{14,6},... | collective-permute-start | bytes 98312 | tf_op jit(solution)/shard_map/ppermute | solution.py:27
  119.9 12.1 %collective-permute-start.30 = (bf16[256,768]{1,0:T(8,128)(2,1)S(1)}, bf16[256,768]{1,0:T(8,128)(2,1)S(1)}, u32[]{:S(2)}, u32[]{:S(2)}) collective-permute-start(bf16[256,768]{1,0:T(8,128)(2,1)S(1)} %fusion.2), channel_id=1, source_target_pairs={{2,0},{0,2},{3,1},{1,3},{6,4},{4,6},{7,5},{5,7},{10,8},{8,10},{11,... | collective-permute-start | bytes 1179656 | tf_op jit(solution)/shard_map/ppermute | solution.py:22
  120.7 20.7 %collective-permute-start.25 = (bf16[256,1024]{1,0:T(8,128)(2,1)S(1)}, bf16[256,1024]{1,0:T(8,128)(2,1)S(1)}, u32[]{:S(2)}, u32[]{:S(2)}) collective-permute-start(bf16[256,1024]{1,0:T(8,128)(2,1)S(1)} %fusion), channel_id=1, source_target_pairs={{2,0},{0,2},{3,1},{1,3},{6,4},{4,6},{7,5},{5,7},{10,8},{8,10},{11,... | collective-permute-start | bytes 1572872 | tf_op jit(solution)/shard_map/ppermute | solution.py:22
  133.1 10.7 %collective-permute-start.31 = (bf16[2,64,768]{2,1,0:T(8,128)(2,1)S(1)}, bf16[2,64,768]{2,1,0:T(8,128)(2,1)S(1)}, u32[]{:S(2)}, u32[]{:S(2)}) collective-permute-start(bf16[2,64,768]{2,1,0:T(8,128)(2,1)S(1)} %fusion.21), channel_id=1, source_target_pairs={{4,0},{0,4},{12,8},{8,12},{5,1},{1,5},{13,9},{9,13},{6,2},{2,6},{1... | collective-permute-start | bytes 589832 | tf_op jit(solution)/shard_map/ppermute | solution.py:27
  141.7 9.7 %collective-permute-start.26 = (bf16[2,64,1024]{2,1,0:T(8,128)(2,1)S(1)}, bf16[2,64,1024]{2,1,0:T(8,128)(2,1)S(1)}, u32[]{:S(2)}, u32[]{:S(2)}) collective-permute-start(bf16[2,64,1024]{2,1,0:T(8,128)(2,1)S(1)} %fusion.16), channel_id=1, source_target_pairs={{4,0},{0,4},{12,8},{8,12},{5,1},{1,5},{13,9},{9,13},{6,2},{2,6},{1... | collective-permute-start | bytes 786440 | tf_op jit(solution)/shard_map/ppermute | solution.py:27
  143.8 8.2 %collective-permute-start.32 = (bf16[1,64,768]{2,1,0:T(8,128)(2,1)S(1)}, bf16[1,64,768]{2,1,0:T(8,128)(2,1)S(1)}, u32[]{:S(2)}, u32[]{:S(2)}) collective-permute-start(bf16[1,64,768]{2,1,0:T(8,128)(2,1)S(1)} %fusion.29), channel_id=1, source_target_pairs={{8,0},{12,4},{0,8},{4,12},{9,1},{13,5},{1,9},{5,13},{10,2},{14,6},... | collective-permute-start | bytes 294920 | tf_op jit(solution)/shard_map/ppermute | solution.py:27
  151.5 7.3 %collective-permute-start.27 = (bf16[1,64,1024]{2,1,0:T(8,128)(2,1)S(1)}, bf16[1,64,1024]{2,1,0:T(8,128)(2,1)S(1)}, u32[]{:S(2)}, u32[]{:S(2)}) collective-permute-start(bf16[1,64,1024]{2,1,0:T(8,128)(2,1)S(1)} %fusion.25), channel_id=1, source_target_pairs={{8,0},{12,4},{0,8},{4,12},{9,1},{13,5},{1,9},{5,13},{10,2},{14,6},... | collective-permute-start | bytes 393224 | tf_op jit(solution)/shard_map/ppermute | solution.py:27
  (27 other events, 406.1 us)

commit v4 on v3

--- a/solution.py
+++ b/solution.py
@@ -12,7 +12,7 @@
 
 epsilon = 1e-06
 
-CHUNKS = (4, 3, 1)
+CHUNKS = (4, 4)
 
 
 def fetch(value, axis, step):
@@ -84,11 +84,13 @@
         back_ref[i] = total.astype(BF16)
 
 
-def down_copies(sel_ref, wd_ref, wds_ref, sem_ref, first):
+def down_copies(wd_ref, wds_ref, sem_ref, first):
     tensors, held, _, span = wds_ref.shape
+    x = lax.axis_index("tensor")
+    cols_out = wd_ref.shape[2] // tensors
     copies = [[] for _ in range(tensors)]
     for t in range(tensors):
-        at = pl.multiple_of(sel_ref[t] + first, 128)
+        at = pl.multiple_of((x + t) % tensors * cols_out + first, 128)
         for j in range(held):
             copies[t].append(
                 pltpu.make_async_copy(
@@ -117,25 +119,28 @@
             for i in range(cores):
                 mixed = mixed_ref[i if groups > 1 else 0]
                 rows = jnp.dot(back_ref[i], mixed, preferred_element_type=F32)
-                outs_ref[i][t, :, cols] = rows.astype(BF16)
+                outs_ref[i * tensors + t][:, cols] = rows.astype(BF16)
 
 
 def first_kernel(
-    dims, sel_ref, place_ref, back_ref, *rest
+    dims, place_ref, back_ref, *rest
 ):
     cores, tensors, depth, groups, first = dims
     lengths = depth if groups > 1 else 1
     count = cores * tensors * lengths
     pieces, rest = rest[:count], rest[count:]
     wg_ref, wu_ref, wd_ref, act_ref = rest[:4]
-    outs_ref = rest[4 : 4 + cores]
-    x_ref, s_ref, wgs_ref, wus_ref, wds_ref, mixed_ref, x_sem, w_sem, d_sem = rest[4 + cores :]
+    outs_ref = rest[4 : 4 + cores * tensors]
+    x_ref, s_ref, wgs_ref, wus_ref, wds_ref, mixed_ref, x_sem, w_sem, d_sem = rest[
+        4 + cores * tensors :
+    ]
+    d, x = lax.axis_index("dp"), lax.axis_index("tensor")
     held = wg_ref.shape[0]
     part, cols = pieces[0].shape
     width = x_ref.shape[-1]
     copies = []
     for i in range(cores):
-        at = pl.multiple_of(sel_ref[tensors + groups + i], 128)
+        at = pl.multiple_of((d + i) % cores * cols, 128)
         for k in range(tensors):
             for o in range(lengths):
                 n = (i * tensors + k) * lengths + o
@@ -158,7 +163,7 @@
             for n, (src, dst) in enumerate(((wg_ref, wgs_ref), (wu_ref, wus_ref)))
         ]
 
-    downs = down_copies(sel_ref, wd_ref, wds_ref, d_sem, first)
+    downs = down_copies(wd_ref, wds_ref, d_sem, first)
     queue = [weights(j) for j in range(held)] + downs
 
     def start(n):
@@ -170,7 +175,7 @@
     per = s_ref.shape[1] // groups
     step = min(STEP, width)
     for g in range(groups):
-        kk = sel_ref[tensors + g]
+        kk = (d + g + tensors - x) % tensors if groups > 1 else 0
         for n in range(width // step):
             at = slice(n * step, (n + 1) * step)
             rows = jnp.dot(place_ref[g], x_ref[kk, :, at], preferred_element_type=F32)
@@ -193,11 +198,11 @@
     down_and_combine(back_ref, act_ref, wds_ref, outs_ref, mixed_ref, groups, downs)
 
 
-def later_kernel(dims, sel_ref, back_ref, act_ref, wd_ref, *rest):
-    cores, _, groups, first = dims
-    outs_ref = rest[:cores]
-    wds_ref, mixed_ref, d_sem = rest[cores:]
-    downs = down_copies(sel_ref, wd_ref, wds_ref, d_sem, first)
+def later_kernel(dims, back_ref, act_ref, wd_ref, *rest):
+    cores, tensors, groups, first = dims
+    outs_ref = rest[: cores * tensors]
+    wds_ref, mixed_ref, d_sem = rest[cores * tensors :]
+    downs = down_copies(wd_ref, wds_ref, d_sem, first)
     for copies in downs:
         for copy in copies:
             copy.start()
@@ -310,17 +315,12 @@
             for o in range(len(along)):
                 pieces.append(fetch(mine[k, o], "dp", i))
 
-    starts = [((x + t) % tensors) * cols_out for t in range(tensors)]
-    starts += [(d + g - x) % tensors if groups > 1 else d * 0 for g in range(groups)]
-    starts += [((d + i) % cores) * cols_core for i in range(cores)]
-    sel = jnp.stack(starts).astype(jnp.int32)
-
     slots = groups * blocks * SLOT
     spans = [cols_out * n // 8 for n in CHUNKS]
     out_rows = depth * rows
 
     def out_shapes(span):
-        return [jax.ShapeDtypeStruct((tensors, out_rows, span), BF16)] * cores
+        return [jax.ShapeDtypeStruct((out_rows, span), BF16)] * (cores * tensors)
 
     def scratch(span):
         return [
@@ -331,8 +331,8 @@
     activated, *outs = pl.pallas_call(
         functools.partial(first_kernel, (cores, tensors, depth, groups, 0)),
         out_shape=[jax.ShapeDtypeStruct((held, slots, hidden_units), BF16)] + out_shapes(spans[0]),
-        in_specs=[SMEM, VMEM, VMEM] + [ANY] * (len(pieces) + 3),
-        out_specs=[VMEM] * (1 + cores),
+        in_specs=[VMEM, VMEM] + [ANY] * (len(pieces) + 3),
+        out_specs=[VMEM] * (1 + cores * tensors),
         scratch_shapes=[
             pltpu.VMEM((groups, tensors // groups * depth * part, width), BF16),
             pltpu.VMEM((held, slots, width), BF16),
@@ -347,7 +347,7 @@
         ],
         compiler_params=PARAMS,
         name="experts_first",
-    )(sel, placing, back, *pieces, w_gate, w_up, w_down)
+    )(placing, back, *pieces, w_gate, w_up, w_down)
 
     results = []
     at = 0
@@ -356,8 +356,8 @@
             outs = pl.pallas_call(
                 functools.partial(later_kernel, (cores, tensors, groups, at)),
                 out_shape=out_shapes(span),
-                in_specs=[SMEM, VMEM, VMEM, ANY],
-                out_specs=[VMEM] * cores,
+                in_specs=[VMEM, VMEM, ANY],
+                out_specs=[VMEM] * (cores * tensors),
                 scratch_shapes=scratch(span) + [pltpu.SemaphoreType.DMA((tensors, held))],
                 compiler_params=PARAMS,
                 cost_estimate=pl.CostEstimate(
@@ -366,13 +366,13 @@
                     transcendentals=0,
                 ),
                 name="experts_later",
-            )(sel, back, activated, w_down)
+            )(back, activated, w_down)
         at += span
         sides = []
         for t in list(range(1, tensors)) + [0]:
-            summed = outs[0][t].astype(F32)
+            summed = outs[t].astype(F32)
             for i in range(1, cores):
-                got = fetch(outs[i][t], "dp", -i)
+                got = fetch(outs[i * tensors + t], "dp", -i)
                 summed = summed + got.astype(F32)
             if t > 0:
                 got = fetch(summed.astype(BF16), "tensor", -t)
@@ -413,4 +413,9 @@
     )
     if mesh.shape["tensor"] != mesh.shape["dp"]:
         return step
+    depth = mesh.shape["expert"]
+    for _ in range(1, len(CHUNKS)):
+        flip = 1
+        while flip < depth:
+            flip *= 2
     return step

time: 160 us -> 151 us (0.944)
  starting transfers between devices: 28.4 us -> 23 us
  waiting for transfers between devices: 81.2 us -> 85.2 us
  Pallas kernels: 34.5 us -> 30.6 us
  local copies, waits for them, and re-layouts: 5.38 us -> 2.53 us
    ppermute x26 -> x23, waiting for transfers between devices: 42.6 us -> 47 us  [fetch(): lax.ppermute(value, axis, [((i + step) % size, i) for i in range(size)])]
    ppermute x12 -> x10, starting transfers between devices: 13.8 us -> 9.68 us  [across(): return lax.ppermute(value, axis, [(i ^ flip, i) for i in range(size)])]
    pallas_call x2 -> x1, Pallas kernels: 11.3 us -> 7.62 us  [on_device(): pl.pallas_call(functools.partial(later_kernel, (cores, tensors, groups, a...]
    squeeze x3 -> x0, local copies, waits for them, and re-layouts: 2.22 us -> none  [on_device(): got = fetch(outs[i][t], 'dp', -i)]
    ppermute x26 -> x23, starting transfers between devices: 14.7 us -> 13.3 us  [fetch(): lax.ppermute(value, axis, [((i + step) % size, i) for i in range(size)])]
    ppermute x12 -> x10, waiting for transfers between devices: 38.6 us -> 38.2 us  [across(): return lax.ppermute(value, axis, [(i ^ flip, i) for i in range(size)])]
  transfers between devices with their start and end apart: 38 -> 33, of which waited for: 19 -> 16; matrix products, arithmetic and copies ran while one was open for 4% -> 2% of each run, Pallas kernels for 6% -> 7%
where the time goes in v4:
time: 151 us
  waiting for transfers between devices  85.2 us (56%)
  Pallas kernels  30.6 us (20%)
  starting transfers between devices  23 us (15%)
  matrix products  4.71 us (3%)
  other arithmetic  4.23 us (3%)
  local copies, waits for them, and re-layouts  2.53 us (2%)
    ppermute x23, waiting for transfers between devices, fetch(): lax.ppermute(value, axis, [((i + step) % size, i) for i in range(size)])  47 us
    ppermute x10, waiting for transfers between devices, across(): return lax.ppermute(value, axis, [(i ^ flip, i) for i in range(size)])  38.2 us
    pallas_call x1, Pallas kernels, on_device(): pl.pallas_call(functools.partial(first_kernel, (cores, tensors, depth, gr...  19.4 us
    ppermute x23, starting transfers between devices, fetch(): lax.ppermute(value, axis, [((i + step) % size, i) for i in range(size)])  13.3 us
    ppermute x10, starting transfers between devices, across(): return lax.ppermute(value, axis, [(i ^ flip, i) for i in range(size)])  9.68 us
    pallas_call x1, Pallas kernels, on_device(): pl.pallas_call(functools.partial(later_kernel, (cores, tensors, groups, a...  7.62 us
    dot_general x1, matrix products, on_device(): partial = jnp.dot(attn_all, o_weight, preferred_element_type=F32)  4.71 us
    pallas_call x1, Pallas kernels, on_device(): pl.pallas_call(functools.partial(tables_kernel, choices), out_shape=[jax....  3.08 us
  transfers between devices with their start and end apart: 33, of which 16 were waited for; matrix products, arithmetic and copies ran while one was open for 2% of the time, Pallas kernels for 7%

profile of v4, /device:TPU:0, one launch (start us, length us, event | category | flops | bytes accessed | tf_op | source)
XLA Modules:
  0.0 150.7 jit_solution(4100169710026721590)
XLA Ops:
  0.6 1.3 collective-permute-done.4
  2.2 4.7 %convolution_add_fusion = f32[128,2048]{1,0:T(8,128)S(1)} fusion(bf16[2048,2048]{1,0:T(8,128)(2,1)} %param.10, bf16[64,2048]{1,0:T(8,128)(2,1)S(1)} %collective-permute-done.4, bf16[64,2048]{1,0:T(8,128)(2,1)} %param.9, bf16[64,2048]{1,0:T(8,128)(2,1)S(1)} %collective-permute-done.5, bf16[64,2048]{1,0:T(8,128)(2,1)} %param.11, pred[]{:T(512)S(6)} %eq.9), kind=kOutput, calls=%fused_computation | convolution fusion | flops 1076363264 | bytes 10485761 | tf_op jit(solution)/shard_map/dot_general | solution.py:227
  7.0 2.9 %collective-permute-start.6 = (bf16[64,2048]{1,0:T(8,128)(2,1)S(1)}, bf16[64,2048]{1,0:T(8,128)(2,1)S(1)}, u32[]{:S(2)}, u32[]{:S(2)}) collective-permute-start(bf16[64,2048]{1,0:T(8,128)(2,1)S(1)} %fusion.11), channel_id=1, source_target_pairs={{2,0},{0,2},{3,1},{1,3},{6,4},{4,6},{7,5},{5,7},{10,8},{8,10},{11,... | collective-permute-start | bytes 786440 | tf_op jit(solution)/shard_map/ppermute | solution.py:22
  9.9 6.6 %collective-permute-done.6 = bf16[64,2048]{1,0:T(8,128)(2,1)S(1)} collective-permute-done((bf16[64,2048]{1,0:T(8,128)(2,1)S(1)}, bf16[64,2048]{1,0:T(8,128)(2,1)S(1)}, u32[]{:S(2)}, u32[]{:S(2)}) %collective-permute-start.6) | collective-permute-done | bytes 262176 | tf_op jit(solution)/shard_map/ppermute | solution.py:22
  16.8 1.1 collective-permute-done.7
  18.1 2.9 %collective-permute-start.9 = (bf16[64,2048]{1,0:T(8,128)(2,1)S(1)}, bf16[64,2048]{1,0:T(8,128)(2,1)S(1)}, u32[]{:S(2)}, u32[]{:S(2)}) collective-permute-start(bf16[64,2048]{1,0:T(8,128)(2,1)S(1)} %fusion.2.rest_0_), channel_id=1, source_target_pairs={{8,0},{12,4},{0,8},{4,12},{9,1},{13,5},{1,9},{5,13},{10,2},{14,6},... | collective-permute-start | bytes 786440 | tf_op jit(solution)/shard_map/ppermute | solution.py:27
  21.0 1.5 collective-permute-start.11
  22.5 1.6 %collective-permute-start.8 = (bf16[64,2048]{1,0:T(8,128)(2,1)S(1)}, bf16[64,2048]{1,0:T(8,128)(2,1)S(1)}, u32[]{:S(2)}, u32[]{:S(2)}) collective-permute-start(bf16[64,2048]{1,0:T(8,128)(2,1)S(1)} %fusion.2.rest_0_), channel_id=1, source_target_pairs={{4,0},{0,4},{12,8},{8,12},{5,1},{1,5},{13,9},{9,13},{6,2},{2,6},{1... | collective-permute-start | bytes 786440 | tf_op jit(solution)/shard_map/ppermute | solution.py:27
  24.1 9.3 %collective-permute-done.9.rest_2_ = bf16[64,2048]{1,0:T(8,128)(2,1)S(1)} collective-permute-done((bf16[64,2048]{1,0:T(8,128)(2,1)S(1)}, bf16[64,2048]{1,0:T(8,128)(2,1)S(1)}, u32[]{:S(2)}, u32[]{:S(2)}) %collective-permute-start.9) | collective-permute-done | bytes 262176 | tf_op jit(solution)/shard_map/ppermute | solution.py:27
  34.7 1.2 collective-permute-done
  35.9 2.9 %collective-permute-start.3 = (f32[2,16,64]{2,1,0:T(8,128)S(1)}, f32[2,16,64]{2,1,0:T(8,128)S(1)}, u32[]{:S(2)}, u32[]{:S(2)}) collective-permute-start(f32[2,16,64]{2,1,0:T(8,128)S(1)} %pad_maximum_fusion.1.rest_0_), channel_id=1, source_target_pairs={{12,0},{8,4},{4,8},{0,12},{13,1},{9,5},{5,9},{1,13},{14,2},{10,6},... | collective-permute-start | bytes 24584 | tf_op jit(solution)/shard_map/ppermute | solution.py:27
  38.8 4.9 %collective-permute-done.3.rest_3_ = f32[2,16,64]{2,1,0:T(8,128)S(1)} collective-permute-done((f32[2,16,64]{2,1,0:T(8,128)S(1)}, f32[2,16,64]{2,1,0:T(8,128)S(1)}, u32[]{:S(2)}, u32[]{:S(2)}) %collective-permute-start.3) | collective-permute-done | bytes 8224 | tf_op jit(solution)/shard_map/ppermute | solution.py:27
  43.7 4.6 %collective-permute-done.2.rest_2_ = f32[2,16,64]{2,1,0:T(8,128)S(1)} collective-permute-done((f32[2,16,64]{2,1,0:T(8,128)S(1)}, f32[2,16,64]{2,1,0:T(8,128)S(1)}, u32[]{:S(2)}, u32[]{:S(2)}) %collective-permute-start.2) | collective-permute-done | bytes 8224 | tf_op jit(solution)/shard_map/ppermute | solution.py:27
  48.4 3.6 %collective-permute-done.1.rest_1_ = f32[2,16,64]{2,1,0:T(8,128)S(1)} collective-permute-done((f32[2,16,64]{2,1,0:T(8,128)S(1)}, f32[2,16,64]{2,1,0:T(8,128)S(1)}, u32[]{:S(2)}, u32[]{:S(2)}) %collective-permute-start.1) | collective-permute-done | bytes 8224 | tf_op jit(solution)/shard_map/ppermute | solution.py:27
  52.1 1.6 %collective-permute-start.13 = (bf16[64,2048]{1,0:T(8,128)(2,1)S(1)}, bf16[64,2048]{1,0:T(8,128)(2,1)S(1)}, u32[]{:S(2)}, u32[]{:S(2)}) collective-permute-start(bf16[64,2048]{1,0:T(8,128)(2,1)S(1)} %collective-permute-done.9.rest_2_), channel_id=1, source_target_pairs={{2,0},{0,2},{3,1},{1,3},{6,4},{4,6},{7,5},{5,7},{10,8},{8,10},{11,... | collective-permute-start | bytes 786440 | tf_op jit(solution)/shard_map/ppermute | solution.py:22
  54.2 1.5 collective-permute-start.14
  56.2 5.1 %collective-permute-done.13.rest_6_ = bf16[64,2048]{1,0:T(8,128)(2,1)S(1)} collective-permute-done((bf16[64,2048]{1,0:T(8,128)(2,1)S(1)}, bf16[64,2048]{1,0:T(8,128)(2,1)S(1)}, u32[]{:S(2)}, u32[]{:S(2)}) %collective-permute-start.13) | collective-permute-done | bytes 262176 | tf_op jit(solution)/shard_map/ppermute | solution.py:22
  61.3 5.6 %collective-permute-done.12.rest_5_ = bf16[64,2048]{1,0:T(8,128)(2,1)S(1)} collective-permute-done((bf16[64,2048]{1,0:T(8,128)(2,1)S(1)}, bf16[64,2048]{1,0:T(8,128)(2,1)S(1)}, u32[]{:S(2)}, u32[]{:S(2)}) %collective-permute-start.12) | collective-permute-done | bytes 262176 | tf_op jit(solution)/shard_map/ppermute | solution.py:22
  66.9 5.1 %collective-permute-done.14.rest_7_ = bf16[64,2048]{1,0:T(8,128)(2,1)S(1)} collective-permute-done((bf16[64,2048]{1,0:T(8,128)(2,1)S(1)}, bf16[64,2048]{1,0:T(8,128)(2,1)S(1)}, u32[]{:S(2)}, u32[]{:S(2)}) %collective-permute-start.14) | collective-permute-done | bytes 262176 | tf_op jit(solution)/shard_map/ppermute | solution.py:22
  72.0 3.1 %tables.1 = (bf16[2,384,256]{2,1,0:T(8,128)(2,1)S(1)}, bf16[2,256,384]{2,1,0:T(8,128)(2,1)S(1)}) custom-call(s32[1]{0:T(128)} %bitcast.base_ref, f32[2,16,64]{2,1,0:T(8,128)S(1)} %pad_maximum_fusion.1.rest_0_, f32[2,16,64]{2,1,0:T(8,128)S(1)} %collective-permute-done.1.rest_1_, f32[2,16,64]{2,1,0:T(8,128)S(1)} %collective-permute-done.2.rest_2_, ...), custom_call_target="tpu_custom_call" | custom-call | tf_op jit(solution)/shard_map/tables/pallas_call | solution.py:271
  75.1 0.8 copy-done
  77.5 19.4 %experts_first.1 = (bf16[4,192,512]{2,1,0:T(8,128)(2,1)}, bf16[256,1024]{1,0:T(8,128)(2,1)}, bf16[256,1024]{1,0:T(8,128)(2,1)}, bf16[256,1024]{1,0:T(8,128)(2,1)}, bf16[256,1024]{1,0:T(8,128)(2,1)}) custom-call(bf16[2,384,256]{2,1,0:T(8,128)(2,1)} %copy-done.1, bf16[2,256,384]{2,1,0:T(8,128)(2,1)} %copy-done, bf16[64,2048]{1,0:T(8,128)(2,1)} %copy-done.2, ...), custom_call_target="tpu_custom_call" | custom-call | tf_op jit(solution)/shard_map/experts_first/pallas_call | solution.py:331
  97.5 7.6 %experts_later.1 = (bf16[256,1024]{1,0:T(8,128)(2,1)}, bf16[256,1024]{1,0:T(8,128)(2,1)}, bf16[256,1024]{1,0:T(8,128)(2,1)}, bf16[256,1024]{1,0:T(8,128)(2,1)}) custom-call(bf16[2,256,384]{2,1,0:T(8,128)(2,1)} %copy-done, bf16[4,192,512]{2,1,0:T(8,128)(2,1)} %get-tuple-element.22.act_ref, bf16[4,512,4096]{2,1,0:T(8,128)(2,1)} %wd_ref.1), custom_call_target="tpu_custom_call" | custom-call | flops 3221225472 | bytes 8388608 | tf_op jit(solution)/shard_map/experts_later/pallas_call | solution.py:356
  105.9 1.6 %collective-permute-start.25 = (bf16[256,1024]{1,0:T(8,128)(2,1)S(1)}, bf16[256,1024]{1,0:T(8,128)(2,1)S(1)}, u32[]{:S(2)}, u32[]{:S(2)}) collective-permute-start(bf16[256,1024]{1,0:T(8,128)(2,1)S(1)} %add_convert_fusion.1), channel_id=1, source_target_pairs={{2,0},{0,2},{3,1},{1,3},{6,4},{4,6},{7,5},{5,7},{10,8},{8,10},{11,... | collective-permute-start | bytes 1572872 | tf_op jit(solution)/shard_map/ppermute | solution.py:22
  107.4 1.2 add_convert_fusion
  108.7 1.4 collective-permute-start.30
  110.1 10.7 %collective-permute-done.25 = bf16[256,1024]{1,0:T(8,128)(2,1)S(1)} collective-permute-done((bf16[256,1024]{1,0:T(8,128)(2,1)S(1)}, bf16[256,1024]{1,0:T(8,128)(2,1)S(1)}, u32[]{:S(2)}, u32[]{:S(2)}) %collective-permute-start.25) | collective-permute-done | bytes 524320 | tf_op jit(solution)/shard_map/ppermute | solution.py:22
  121.1 10.0 %collective-permute-done.30 = bf16[256,1024]{1,0:T(8,128)(2,1)S(1)} collective-permute-done((bf16[256,1024]{1,0:T(8,128)(2,1)S(1)}, bf16[256,1024]{1,0:T(8,128)(2,1)S(1)}, u32[]{:S(2)}, u32[]{:S(2)}) %collective-permute-start.30) | collective-permute-done | bytes 524320 | tf_op jit(solution)/shard_map/ppermute | solution.py:22
  131.1 1.3 convert_add_fusion
  132.6 1.4 collective-permute-start.27
  134.1 8.7 %collective-permute-done.31 = bf16[2,64,1024]{2,1,0:T(8,128)(2,1)S(1)} collective-permute-done((bf16[2,64,1024]{2,1,0:T(8,128)(2,1)S(1)}, bf16[2,64,1024]{2,1,0:T(8,128)(2,1)S(1)}, u32[]{:S(2)}, u32[]{:S(2)}) %collective-permute-start.31) | collective-permute-done | bytes 262176 | tf_op jit(solution)/shard_map/ppermute | solution.py:27
  143.0 7.0 %collective-permute-done.32 = bf16[1,64,1024]{2,1,0:T(8,128)(2,1)S(1)} collective-permute-done((bf16[1,64,1024]{2,1,0:T(8,128)(2,1)S(1)}, bf16[1,64,1024]{2,1,0:T(8,128)(2,1)S(1)}, u32[]{:S(2)}, u32[]{:S(2)}) %collective-permute-start.32) | collective-permute-done | bytes 131104 | tf_op jit(solution)/shard_map/ppermute | solution.py:27
  (102 shorter events, 8.2 us)
Async XLA Ops:
  0.0 1.9 %collective-permute-start.4 = (bf16[64,2048]{1,0:T(8,128)(2,1)}, bf16[64,2048]{1,0:T(8,128)(2,1)S(1)}, u32[]{:S(2)}, u32[]{:S(2)}) collective-permute-start(bf16[64,2048]{1,0:T(8,128)(2,1)} %param.9), channel_id=1, source_target_pairs={{1,0},{0,1},{3,2},{2,3},{5,4},{4,5},{7,6},{6,7},{9,8},{8,9},{11,10... | collective-permute-start | bytes 786440 | tf_op jit(solution)/shard_map/ppermute | solution.py:22
  0.5 1.7 %collective-permute-start.5 = (bf16[64,2048]{1,0:T(8,128)(2,1)}, bf16[64,2048]{1,0:T(8,128)(2,1)S(1)}, u32[]{:S(2)}, u32[]{:S(2)}) collective-permute-start(bf16[64,2048]{1,0:T(8,128)(2,1)} %param.11), channel_id=1, source_target_pairs={{1,0},{0,1},{3,2},{2,3},{5,4},{4,5},{7,6},{6,7},{9,8},{8,9},{11,10... | collective-permute-start | bytes 786440 | tf_op jit(solution)/shard_map/ppermute | solution.py:22
  7.0 9.5 %collective-permute-start.6 = (bf16[64,2048]{1,0:T(8,128)(2,1)S(1)}, bf16[64,2048]{1,0:T(8,128)(2,1)S(1)}, u32[]{:S(2)}, u32[]{:S(2)}) collective-permute-start(bf16[64,2048]{1,0:T(8,128)(2,1)S(1)} %fusion.11), channel_id=1, source_target_pairs={{2,0},{0,2},{3,1},{1,3},{6,4},{4,6},{7,5},{5,7},{10,8},{8,10},{11,... | collective-permute-start | bytes 786440 | tf_op jit(solution)/shard_map/ppermute | solution.py:22
  16.7 1.2 collective-permute-start.7
  18.1 15.3 %collective-permute-start.9 = (bf16[64,2048]{1,0:T(8,128)(2,1)S(1)}, bf16[64,2048]{1,0:T(8,128)(2,1)S(1)}, u32[]{:S(2)}, u32[]{:S(2)}) collective-permute-start(bf16[64,2048]{1,0:T(8,128)(2,1)S(1)} %fusion.2.rest_0_), channel_id=1, source_target_pairs={{8,0},{12,4},{0,8},{4,12},{9,1},{13,5},{1,9},{5,13},{10,2},{14,6},... | collective-permute-start | bytes 786440 | tf_op jit(solution)/shard_map/ppermute | solution.py:27
  21.0 27.3 %collective-permute-start.11 = (bf16[64,2048]{1,0:T(8,128)(2,1)S(1)}, bf16[64,2048]{1,0:T(8,128)(2,1)S(1)}, u32[]{:S(2)}, u32[]{:S(2)}) collective-permute-start(bf16[64,2048]{1,0:T(8,128)(2,1)S(1)} %fusion.2.rest_0_), channel_id=1, source_target_pairs={{2,0},{0,2},{3,1},{1,3},{6,4},{4,6},{7,5},{5,7},{10,8},{8,10},{11,... | collective-permute-start | bytes 786440 | tf_op jit(solution)/shard_map/ppermute | solution.py:22
  22.5 29.6 %collective-permute-start.15 = (bf16[64,2048]{1,0:T(8,128)(2,1)S(1)}, bf16[64,2048]{1,0:T(8,128)(2,1)S(1)}, u32[]{:S(2)}, u32[]{:S(2)}) collective-permute-start(bf16[64,2048]{1,0:T(8,128)(2,1)S(1)} %fusion.2.rest_0_), channel_id=1, source_target_pairs={{1,0},{0,1},{3,2},{2,3},{5,4},{4,5},{7,6},{6,7},{9,8},{8,9},{11,10... | collective-permute-start | bytes 786440 | tf_op jit(solution)/shard_map/ppermute | solution.py:22
  22.5 31.2 %collective-permute-start.8 = (bf16[64,2048]{1,0:T(8,128)(2,1)S(1)}, bf16[64,2048]{1,0:T(8,128)(2,1)S(1)}, u32[]{:S(2)}, u32[]{:S(2)}) collective-permute-start(bf16[64,2048]{1,0:T(8,128)(2,1)S(1)} %fusion.2.rest_0_), channel_id=1, source_target_pairs={{4,0},{0,4},{12,8},{8,12},{5,1},{1,5},{13,9},{9,13},{6,2},{2,6},{1... | collective-permute-start | bytes 786440 | tf_op jit(solution)/shard_map/ppermute | solution.py:27
  33.4 20.8 %collective-permute-start.10 = (bf16[64,2048]{1,0:T(8,128)(2,1)S(1)}, bf16[64,2048]{1,0:T(8,128)(2,1)S(1)}, u32[]{:S(2)}, u32[]{:S(2)}) collective-permute-start(bf16[64,2048]{1,0:T(8,128)(2,1)S(1)} %collective-permute-done.9.rest_2_), channel_id=1, source_target_pairs={{4,0},{0,4},{12,8},{8,12},{5,1},{1,5},{13,9},{9,13},{6,2},{2,6},{1... | collective-permute-start | bytes 786440 | tf_op jit(solution)/shard_map/ppermute | solution.py:27
  35.9 7.8 %collective-permute-start.3 = (f32[2,16,64]{2,1,0:T(8,128)S(1)}, f32[2,16,64]{2,1,0:T(8,128)S(1)}, u32[]{:S(2)}, u32[]{:S(2)}) collective-permute-start(f32[2,16,64]{2,1,0:T(8,128)S(1)} %pad_maximum_fusion.1.rest_0_), channel_id=1, source_target_pairs={{12,0},{8,4},{4,8},{0,12},{13,1},{9,5},{5,9},{1,13},{14,2},{10,6},... | collective-permute-start | bytes 24584 | tf_op jit(solution)/shard_map/ppermute | solution.py:27
  43.7 4.6 %collective-permute-start.2 = (f32[2,16,64]{2,1,0:T(8,128)S(1)}, f32[2,16,64]{2,1,0:T(8,128)S(1)}, u32[]{:S(2)}, u32[]{:S(2)}) collective-permute-start(f32[2,16,64]{2,1,0:T(8,128)S(1)} %pad_maximum_fusion.1.rest_0_), channel_id=1, source_target_pairs={{8,0},{12,4},{0,8},{4,12},{9,1},{13,5},{1,9},{5,13},{10,2},{14,6},... | collective-permute-start | bytes 24584 | tf_op jit(solution)/shard_map/ppermute | solution.py:27
  48.3 3.7 %collective-permute-start.1 = (f32[2,16,64]{2,1,0:T(8,128)S(1)}, f32[2,16,64]{2,1,0:T(8,128)S(1)}, u32[]{:S(2)}, u32[]{:S(2)}) collective-permute-start(f32[2,16,64]{2,1,0:T(8,128)S(1)} %pad_maximum_fusion.1.rest_0_), channel_id=1, source_target_pairs={{4,0},{0,4},{12,8},{8,12},{5,1},{1,5},{13,9},{9,13},{6,2},{2,6},{1... | collective-permute-start | bytes 24584 | tf_op jit(solution)/shard_map/ppermute | solution.py:27
  48.3 7.3 %collective-permute-start.19 = (bf16[64,2048]{1,0:T(8,128)(2,1)S(1)}, bf16[64,2048]{1,0:T(8,128)(2,1)S(1)}, u32[]{:S(2)}, u32[]{:S(2)}) collective-permute-start(bf16[64,2048]{1,0:T(8,128)(2,1)S(1)} %collective-permute-done.11.rest_4_), channel_id=1, source_target_pairs={{1,0},{0,1},{3,2},{2,3},{5,4},{4,5},{7,6},{6,7},{9,8},{8,9},{11,10... | collective-permute-start | bytes 786440 | tf_op jit(solution)/shard_map/ppermute | solution.py:22
  52.1 3.6 %collective-permute-start.17 = (bf16[64,2048]{1,0:T(8,128)(2,1)S(1)}, bf16[64,2048]{1,0:T(8,128)(2,1)S(1)}, u32[]{:S(2)}, u32[]{:S(2)}) collective-permute-start(bf16[64,2048]{1,0:T(8,128)(2,1)S(1)} %collective-permute-done.9.rest_2_), channel_id=1, source_target_pairs={{1,0},{0,1},{3,2},{2,3},{5,4},{4,5},{7,6},{6,7},{9,8},{8,9},{11,10... | collective-permute-start | bytes 786440 | tf_op jit(solution)/shard_map/ppermute | solution.py:22
  52.1 9.2 %collective-permute-start.13 = (bf16[64,2048]{1,0:T(8,128)(2,1)S(1)}, bf16[64,2048]{1,0:T(8,128)(2,1)S(1)}, u32[]{:S(2)}, u32[]{:S(2)}) collective-permute-start(bf16[64,2048]{1,0:T(8,128)(2,1)S(1)} %collective-permute-done.9.rest_2_), channel_id=1, source_target_pairs={{2,0},{0,2},{3,1},{1,3},{6,4},{4,6},{7,5},{5,7},{10,8},{8,10},{11,... | collective-permute-start | bytes 786440 | tf_op jit(solution)/shard_map/ppermute | solution.py:22
  53.6 13.3 %collective-permute-start.12 = (bf16[64,2048]{1,0:T(8,128)(2,1)S(1)}, bf16[64,2048]{1,0:T(8,128)(2,1)S(1)}, u32[]{:S(2)}, u32[]{:S(2)}) collective-permute-start(bf16[64,2048]{1,0:T(8,128)(2,1)S(1)} %collective-permute-done.8.rest_1_), channel_id=1, source_target_pairs={{2,0},{0,2},{3,1},{1,3},{6,4},{4,6},{7,5},{5,7},{10,8},{8,10},{11,... | collective-permute-start | bytes 786440 | tf_op jit(solution)/shard_map/ppermute | solution.py:22
  54.2 17.8 %collective-permute-start.14 = (bf16[64,2048]{1,0:T(8,128)(2,1)S(1)}, bf16[64,2048]{1,0:T(8,128)(2,1)S(1)}, u32[]{:S(2)}, u32[]{:S(2)}) collective-permute-start(bf16[64,2048]{1,0:T(8,128)(2,1)S(1)} %collective-permute-done.10.rest_3_), channel_id=1, source_target_pairs={{2,0},{0,2},{3,1},{1,3},{6,4},{4,6},{7,5},{5,7},{10,8},{8,10},{11,... | collective-permute-start | bytes 786440 | tf_op jit(solution)/shard_map/ppermute | solution.py:22
  55.7 20.9 %collective-permute-start.16 = (bf16[64,2048]{1,0:T(8,128)(2,1)S(1)}, bf16[64,2048]{1,0:T(8,128)(2,1)S(1)}, u32[]{:S(2)}, u32[]{:S(2)}) collective-permute-start(bf16[64,2048]{1,0:T(8,128)(2,1)S(1)} %collective-permute-done.8.rest_1_), channel_id=1, source_target_pairs={{1,0},{0,1},{3,2},{2,3},{5,4},{4,5},{7,6},{6,7},{9,8},{8,9},{11,10... | collective-permute-start | bytes 786440 | tf_op jit(solution)/shard_map/ppermute | solution.py:22
  55.7 20.9 %collective-permute-start.18 = (bf16[64,2048]{1,0:T(8,128)(2,1)S(1)}, bf16[64,2048]{1,0:T(8,128)(2,1)S(1)}, u32[]{:S(2)}, u32[]{:S(2)}) collective-permute-start(bf16[64,2048]{1,0:T(8,128)(2,1)S(1)} %collective-permute-done.10.rest_3_), channel_id=1, source_target_pairs={{1,0},{0,1},{3,2},{2,3},{5,4},{4,5},{7,6},{6,7},{9,8},{8,9},{11,10... | collective-permute-start | bytes 786440 | tf_op jit(solution)/shard_map/ppermute | solution.py:22
  61.3 15.3 %collective-permute-start.21 = (bf16[64,2048]{1,0:T(8,128)(2,1)S(1)}, bf16[64,2048]{1,0:T(8,128)(2,1)}, u32[]{:S(2)}, u32[]{:S(2)}) collective-permute-start(bf16[64,2048]{1,0:T(8,128)(2,1)S(1)} %collective-permute-done.13.rest_6_), channel_id=1, source_target_pairs={{1,0},{0,1},{3,2},{2,3},{5,4},{4,5},{7,6},{6,7},{9,8},{8,9},{11,10... | collective-permute-start | bytes 786440 | tf_op jit(solution)/shard_map/ppermute | solution.py:22
  66.9 9.7 %collective-permute-start.20 = (bf16[64,2048]{1,0:T(8,128)(2,1)S(1)}, bf16[64,2048]{1,0:T(8,128)(2,1)}, u32[]{:S(2)}, u32[]{:S(2)}) collective-permute-start(bf16[64,2048]{1,0:T(8,128)(2,1)S(1)} %collective-permute-done.12.rest_5_), channel_id=1, source_target_pairs={{1,0},{0,1},{3,2},{2,3},{5,4},{4,5},{7,6},{6,7},{9,8},{8,9},{11,10... | collective-permute-start | bytes 786440 | tf_op jit(solution)/shard_map/ppermute | solution.py:22
  72.0 4.6 %collective-permute-start.22 = (bf16[64,2048]{1,0:T(8,128)(2,1)S(1)}, bf16[64,2048]{1,0:T(8,128)(2,1)}, u32[]{:S(2)}, u32[]{:S(2)}) collective-permute-start(bf16[64,2048]{1,0:T(8,128)(2,1)S(1)} %collective-permute-done.14.rest_7_), channel_id=1, source_target_pairs={{1,0},{0,1},{3,2},{2,3},{5,4},{4,5},{7,6},{6,7},{9,8},{8,9},{11,10... | collective-permute-start | bytes 786440 | tf_op jit(solution)/shard_map/ppermute | solution.py:22
  96.9 8.8 %collective-permute-start.24 = (bf16[256,1024]{1,0:T(8,128)(2,1)}, bf16[256,1024]{1,0:T(8,128)(2,1)S(1)}, u32[]{:S(2)}, u32[]{:S(2)}) collective-permute-start(bf16[256,1024]{1,0:T(8,128)(2,1)} %get-tuple-element.21), channel_id=1, source_target_pairs={{1,0},{0,1},{3,2},{2,3},{5,4},{4,5},{7,6},{6,7},{9,8},{8,9},{11,10... | collective-permute-start | bytes 1572872 | tf_op jit(solution)/shard_map/ppermute | solution.py:22
  105.1 2.3 %collective-permute-start.29 = (bf16[256,1024]{1,0:T(8,128)(2,1)}, bf16[256,1024]{1,0:T(8,128)(2,1)S(1)}, u32[]{:S(2)}, u32[]{:S(2)}) collective-permute-start(bf16[256,1024]{1,0:T(8,128)(2,1)} %get-tuple-element.26), channel_id=1, source_target_pairs={{1,0},{0,1},{3,2},{2,3},{5,4},{4,5},{7,6},{6,7},{9,8},{8,9},{11,10... | collective-permute-start | bytes 1572872 | tf_op jit(solution)/shard_map/ppermute | solution.py:22
  105.2 4.9 %collective-permute-start.23 = (bf16[256,1024]{1,0:T(8,128)(2,1)S(1)}, bf16[256,1024]{1,0:T(8,128)(2,1)S(1)}, u32[]{:S(2)}, u32[]{:S(2)}) collective-permute-start(bf16[256,1024]{1,0:T(8,128)(2,1)S(1)} %copy-done.20), channel_id=1, source_target_pairs={{1,0},{0,1},{3,2},{2,3},{5,4},{4,5},{7,6},{6,7},{9,8},{8,9},{11,10... | collective-permute-start | bytes 1572872 | tf_op jit(solution)/shard_map/ppermute | solution.py:22
  105.9 14.9 %collective-permute-start.25 = (bf16[256,1024]{1,0:T(8,128)(2,1)S(1)}, bf16[256,1024]{1,0:T(8,128)(2,1)S(1)}, u32[]{:S(2)}, u32[]{:S(2)}) collective-permute-start(bf16[256,1024]{1,0:T(8,128)(2,1)S(1)} %add_convert_fusion.1), channel_id=1, source_target_pairs={{2,0},{0,2},{3,1},{1,3},{6,4},{4,6},{7,5},{5,7},{10,8},{8,10},{11,... | collective-permute-start | bytes 1572872 | tf_op jit(solution)/shard_map/ppermute | solution.py:22
  107.4 13.7 %collective-permute-start.28 = (bf16[256,1024]{1,0:T(8,128)(2,1)}, bf16[256,1024]{1,0:T(8,128)(2,1)S(1)}, u32[]{:S(2)}, u32[]{:S(2)}) collective-permute-start(bf16[256,1024]{1,0:T(8,128)(2,1)} %get-tuple-element.24), channel_id=1, source_target_pairs={{1,0},{0,1},{3,2},{2,3},{5,4},{4,5},{7,6},{6,7},{9,8},{8,9},{11,10... | collective-permute-start | bytes 1572872 | tf_op jit(solution)/shard_map/ppermute | solution.py:22
  108.7 22.4 %collective-permute-start.30 = (bf16[256,1024]{1,0:T(8,128)(2,1)S(1)}, bf16[256,1024]{1,0:T(8,128)(2,1)S(1)}, u32[]{:S(2)}, u32[]{:S(2)}) collective-permute-start(bf16[256,1024]{1,0:T(8,128)(2,1)S(1)} %add_convert_fusion), channel_id=1, source_target_pairs={{2,0},{0,2},{3,1},{1,3},{6,4},{4,6},{7,5},{5,7},{10,8},{8,10},{11,... | collective-permute-start | bytes 1572872 | tf_op jit(solution)/shard_map/ppermute | solution.py:22
  121.0 11.5 %collective-permute-start.26 = (bf16[2,64,1024]{2,1,0:T(8,128)(2,1)S(1)}, bf16[2,64,1024]{2,1,0:T(8,128)(2,1)S(1)}, u32[]{:S(2)}, u32[]{:S(2)}) collective-permute-start(bf16[2,64,1024]{2,1,0:T(8,128)(2,1)S(1)} %fusion.12), channel_id=1, source_target_pairs={{4,0},{0,4},{12,8},{8,12},{5,1},{1,5},{13,9},{9,13},{6,2},{2,6},{1... | collective-permute-start | bytes 786440 | tf_op jit(solution)/shard_map/ppermute | solution.py:27
  132.4 10.3 %collective-permute-start.31 = (bf16[2,64,1024]{2,1,0:T(8,128)(2,1)S(1)}, bf16[2,64,1024]{2,1,0:T(8,128)(2,1)S(1)}, u32[]{:S(2)}, u32[]{:S(2)}) collective-permute-start(bf16[2,64,1024]{2,1,0:T(8,128)(2,1)S(1)} %fusion.13), channel_id=1, source_target_pairs={{4,0},{0,4},{12,8},{8,12},{5,1},{1,5},{13,9},{9,13},{6,2},{2,6},{1... | collective-permute-start | bytes 786440 | tf_op jit(solution)/shard_map/ppermute | solution.py:27
  132.6 10.3 %collective-permute-start.27 = (bf16[1,64,1024]{2,1,0:T(8,128)(2,1)S(1)}, bf16[1,64,1024]{2,1,0:T(8,128)(2,1)S(1)}, u32[]{:S(2)}, u32[]{:S(2)}) collective-permute-start(bf16[1,64,1024]{2,1,0:T(8,128)(2,1)S(1)} %fusion.19), channel_id=1, source_target_pairs={{8,0},{12,4},{0,8},{4,12},{9,1},{13,5},{1,9},{5,13},{10,2},{14,6},... | collective-permute-start | bytes 393224 | tf_op jit(solution)/shard_map/ppermute | solution.py:27
  142.9 7.1 %collective-permute-start.32 = (bf16[1,64,1024]{2,1,0:T(8,128)(2,1)S(1)}, bf16[1,64,1024]{2,1,0:T(8,128)(2,1)S(1)}, u32[]{:S(2)}, u32[]{:S(2)}) collective-permute-start(bf16[1,64,1024]{2,1,0:T(8,128)(2,1)S(1)} %fusion.21), channel_id=1, source_target_pairs={{8,0},{12,4},{0,8},{4,12},{9,1},{13,5},{1,9},{5,13},{10,2},{14,6},... | collective-permute-start | bytes 393224 | tf_op jit(solution)/shard_map/ppermute | solution.py:27
  (22 other events, 400.0 us)

commit v5 on v4

--- a/solution.py
+++ b/solution.py
@@ -12,7 +12,7 @@
 
 epsilon = 1e-06
 
-CHUNKS = (4, 4)
+CHUNKS = (4, 3, 1)
 
 
 def fetch(value, axis, step):
@@ -100,7 +100,7 @@
     return copies
 
 
-def down_and_combine(back_ref, act_ref, wds_ref, outs_ref, mixed_ref, groups, waits):
+def down_and_combine(back_ref, act_ref, wds_ref, outs_ref, mixed_ref, groups, waits, spans):
     held, slots, _ = act_ref.shape
     cores, _, _ = back_ref.shape
     tensors, _, _, span = wds_ref.shape
@@ -119,7 +119,14 @@
             for i in range(cores):
                 mixed = mixed_ref[i if groups > 1 else 0]
                 rows = jnp.dot(back_ref[i], mixed, preferred_element_type=F32)
-                outs_ref[i * tensors + t][:, cols] = rows.astype(BF16)
+                rows = rows.astype(BF16)
+                at = 0
+                for c, size in enumerate(spans):
+                    low, high = max(at, n * step), min(at + size, (n + 1) * step)
+                    if low < high:
+                        out_ref = outs_ref[(c * cores + i) * tensors + t]
+                        out_ref[:, low - at : high - at] = rows[:, low - n * step : high - n * step]
+                    at += size
 
 
 def first_kernel(
@@ -139,16 +146,22 @@
     part, cols = pieces[0].shape
     width = x_ref.shape[-1]
     copies = []
+    places = list(range(lengths))
+    if depth == 4 and groups > 1:
+        z = lax.axis_index("expert")
+        inner = jnp.where((z == 1) | (z == 2), 1, 0)
+        places[2:] = [2 + inner, 3 - inner]
     for i in range(cores):
         at = pl.multiple_of((d + i) % cores * cols, 128)
         for k in range(tensors):
             for o in range(lengths):
                 n = (i * tensors + k) * lengths + o
-                g, row = (k, o) if groups > 1 else (0, k)
+                g, row = (k, places[o]) if groups > 1 else (0, k)
+                row = row * part if isinstance(row, int) else pl.multiple_of(row * part, part)
                 copies.append(
                     pltpu.make_async_copy(
                         pieces[n],
-                        x_ref.at[g, pl.ds(row * part, part), pl.ds(at, cols)],
+                        x_ref.at[g, pl.ds(row, part), pl.ds(at, cols)],
                         x_sem.at[n],
                     )
                 )
@@ -163,7 +176,7 @@
             for n, (src, dst) in enumerate(((wg_ref, wgs_ref), (wu_ref, wus_ref)))
         ]
 
-    downs = down_copies(wd_ref, wds_ref, d_sem, first)
+    downs = down_copies(wd_ref, wds_ref, d_sem, 0)
     queue = [weights(j) for j in range(held)] + downs
 
     def start(n):
@@ -195,18 +208,18 @@
         act_ref[j] = (gate / (1.0 + jnp.exp(-gate)) * up).astype(BF16)
     for n in range(held + 2, len(queue)):
         start(n)
-    down_and_combine(back_ref, act_ref, wds_ref, outs_ref, mixed_ref, groups, downs)
+    down_and_combine(back_ref, act_ref, wds_ref, outs_ref, mixed_ref, groups, downs, (first,))
 
 
 def later_kernel(dims, back_ref, act_ref, wd_ref, *rest):
-    cores, tensors, groups, first = dims
-    outs_ref = rest[: cores * tensors]
-    wds_ref, mixed_ref, d_sem = rest[cores * tensors :]
+    cores, tensors, groups, first, spans = dims
+    count = cores * tensors * len(spans)
+    outs_ref, (wds_ref, mixed_ref, d_sem) = rest[:count], rest[count:]
     downs = down_copies(wd_ref, wds_ref, d_sem, first)
     for copies in downs:
         for copy in copies:
             copy.start()
-    down_and_combine(back_ref, act_ref, wds_ref, outs_ref, mixed_ref, groups, downs)
+    down_and_combine(back_ref, act_ref, wds_ref, outs_ref, mixed_ref, groups, downs, spans)
 
 
 def on_device(attn, o_weight, residual, norm_gain, expert_ids, route_weights, w_gate, w_up, w_down):
@@ -301,8 +314,18 @@
 
     along = [normed]
     mine = {}
-    for o in range(depth):
-        if o > 0:
+    if depth == 4 and sub == 1:
+        middle, outward = ((1, 2), (2, 1)), ((1, 0), (2, 3))
+        along.append(across(normed, "expert", 1))
+        middle_1 = lax.ppermute(normed, "expert", middle)
+        middle_2 = lax.ppermute(along[1], "expert", middle)
+        outward_2 = lax.ppermute(middle_1, "expert", outward)
+        outward_3 = lax.ppermute(middle_2, "expert", outward)
+        outer = (z == 0) | (z == 3)
+        along.append(jnp.where(outer, outward_2, middle_1))
+        along.append(jnp.where(outer, outward_3, middle_2))
+    else:
+        for o in range(1, depth):
             along.append(across(along[o & (o - 1)], "expert", o & -o))
     if sub > 1:
         along = [jnp.concatenate(along, axis=0)]
@@ -329,7 +352,7 @@
         ]
 
     activated, *outs = pl.pallas_call(
-        functools.partial(first_kernel, (cores, tensors, depth, groups, 0)),
+        functools.partial(first_kernel, (cores, tensors, depth, groups, spans[0])),
         out_shape=[jax.ShapeDtypeStruct((held, slots, hidden_units), BF16)] + out_shapes(spans[0]),
         in_specs=[VMEM, VMEM] + [ANY] * (len(pieces) + 3),
         out_specs=[VMEM] * (1 + cores * tensors),
@@ -349,30 +372,29 @@
         name="experts_first",
     )(placing, back, *pieces, w_gate, w_up, w_down)
 
+    more = sum(spans[1:])
+    outs += pl.pallas_call(
+        functools.partial(later_kernel, (cores, tensors, groups, spans[0], spans[1:])),
+        out_shape=[shape for span in spans[1:] for shape in out_shapes(span)],
+        in_specs=[VMEM, VMEM, ANY],
+        out_specs=[VMEM] * (cores * tensors * len(spans[1:])),
+        scratch_shapes=scratch(more) + [pltpu.SemaphoreType.DMA((tensors, held))],
+        compiler_params=PARAMS,
+        cost_estimate=pl.CostEstimate(
+            flops=4 * slots * held * hidden_units * more * tensors,
+            bytes_accessed=2 * held * hidden_units * more * tensors,
+            transcendentals=0,
+        ),
+        name="experts_later",
+    )(back, activated, w_down)
     results = []
-    at = 0
     for n, span in enumerate(spans):
-        if n > 0:
-            outs = pl.pallas_call(
-                functools.partial(later_kernel, (cores, tensors, groups, at)),
-                out_shape=out_shapes(span),
-                in_specs=[VMEM, VMEM, ANY],
-                out_specs=[VMEM] * (cores * tensors),
-                scratch_shapes=scratch(span) + [pltpu.SemaphoreType.DMA((tensors, held))],
-                compiler_params=PARAMS,
-                cost_estimate=pl.CostEstimate(
-                    flops=4 * slots * held * hidden_units * span * tensors,
-                    bytes_accessed=2 * held * hidden_units * span * tensors,
-                    transcendentals=0,
-                ),
-                name="experts_later",
-            )(back, activated, w_down)
-        at += span
+        mixed = outs[n * cores * tensors :]
         sides = []
         for t in list(range(1, tensors)) + [0]:
-            summed = outs[t].astype(F32)
+            summed = mixed[t].astype(F32)
             for i in range(1, cores):
-                got = fetch(outs[i * tensors + t], "dp", -i)
+                got = fetch(mixed[i * tensors + t], "dp", -i)
                 summed = summed + got.astype(F32)
             if t > 0:
                 got = fetch(summed.astype(BF16), "tensor", -t)

time: 151 us -> 157 us (1.040)
  starting transfers between devices: 23 us -> 32.1 us
  waiting for transfers between devices: 85.2 us -> 80.3 us
  other arithmetic: 4.23 us -> 5.86 us
    ppermute x10, waiting for transfers between devices: 38.2 us -> 23.9 us  [across(): return lax.ppermute(value, axis, [(i ^ flip, i) for i in range(size)])]
    ppermute x23 -> x26, waiting for transfers between devices: 47 us -> 53.4 us  [fetch(): lax.ppermute(value, axis, [((i + step) % size, i) for i in range(size)])]
    ppermute x10, starting transfers between devices: 9.68 us -> 15.1 us  [across(): return lax.ppermute(value, axis, [(i ^ flip, i) for i in range(size)])]
    ppermute x0 -> x4, starting transfers between devices: none -> 4.09 us  [the longest x1 1.46 us: on_device(): outward_3 = lax.ppermute(middle_2, 'expert', outward)]
    ppermute x0 -> x4, waiting for transfers between devices: none -> 3.1 us  [the longest x1 3.09 us: on_device(): outward_3 = lax.ppermute(middle_2, 'expert', outward)]
    ppermute x23 -> x26, starting transfers between devices: 13.3 us -> 12.9 us  [fetch(): lax.ppermute(value, axis, [((i + step) % size, i) for i in range(size)])]
  transfers between devices with their start and end apart: 33 -> 40, of which waited for: 16 -> 20; matrix products, arithmetic and copies ran while one was open for 2% -> 3% of each run, Pallas kernels for 7% -> 2%
where the time goes in v5:
time: 157 us
  waiting for transfers between devices  80.3 us (51%)
  starting transfers between devices  32.1 us (20%)
  Pallas kernels  30.8 us (20%)
  other arithmetic  5.86 us (4%)
  matrix products  4.71 us (3%)
  local copies, waits for them, and re-layouts  2.54 us (2%)
    ppermute x26, waiting for transfers between devices, fetch(): lax.ppermute(value, axis, [((i + step) % size, i) for i in range(size)])  53.4 us
    ppermute x10, waiting for transfers between devices, across(): return lax.ppermute(value, axis, [(i ^ flip, i) for i in range(size)])  23.9 us
    pallas_call x1, Pallas kernels, on_device(): pl.pallas_call(functools.partial(first_kernel, (cores, tensors, depth, gr...  19.6 us
    ppermute x10, starting transfers between devices, across(): return lax.ppermute(value, axis, [(i ^ flip, i) for i in range(size)])  15.1 us
    ppermute x26, starting transfers between devices, fetch(): lax.ppermute(value, axis, [((i + step) % size, i) for i in range(size)])  12.9 us
    pallas_call x1, Pallas kernels, on_device(): pl.pallas_call(functools.partial(later_kernel, (cores, tensors, groups, s...  7.64 us
    dot_general x1, matrix products, on_device(): partial = jnp.dot(attn_all, o_weight, preferred_element_type=F32)  4.71 us
  transfers between devices with their start and end apart: 40, of which 20 were waited for; matrix products, arithmetic and copies ran while one was open for 3% of the time, Pallas kernels for 2%

profile of v5, /device:TPU:0, one launch (start us, length us, event | category | flops | bytes accessed | tf_op | source)
XLA Modules:
  0.0 156.9 jit_solution(9510415909054268069)
XLA Ops:
  0.6 1.3 collective-permute-done.4
  2.2 4.7 %convolution_add_fusion = f32[128,2048]{1,0:T(8,128)S(1)} fusion(bf16[2048,2048]{1,0:T(8,128)(2,1)} %param.10, bf16[64,2048]{1,0:T(8,128)(2,1)S(1)} %collective-permute-done.4, bf16[64,2048]{1,0:T(8,128)(2,1)} %param.9, bf16[64,2048]{1,0:T(8,128)(2,1)S(1)} %collective-permute-done.5, bf16[64,2048]{1,0:T(8,128)(2,1)} %param.11, pred[]{:T(512)S(6)} %eq.15), kind=kOutput, calls=%fused_computation | convolution fusion | flops 1076363264 | bytes 10485761 | tf_op jit(solution)/shard_map/dot_general | solution.py:240
  7.0 2.9 %collective-permute-start.6 = (bf16[64,2048]{1,0:T(8,128)(2,1)S(1)}, bf16[64,2048]{1,0:T(8,128)(2,1)S(1)}, u32[]{:S(2)}, u32[]{:S(2)}) collective-permute-start(bf16[64,2048]{1,0:T(8,128)(2,1)S(1)} %fusion.11), channel_id=1, source_target_pairs={{2,0},{0,2},{3,1},{1,3},{6,4},{4,6},{7,5},{5,7},{10,8},{8,10},{11,... | collective-permute-start | bytes 786440 | tf_op jit(solution)/shard_map/ppermute | solution.py:22
  9.9 6.6 %collective-permute-done.6 = bf16[64,2048]{1,0:T(8,128)(2,1)S(1)} collective-permute-done((bf16[64,2048]{1,0:T(8,128)(2,1)S(1)}, bf16[64,2048]{1,0:T(8,128)(2,1)S(1)}, u32[]{:S(2)}, u32[]{:S(2)}) %collective-permute-start.6) | collective-permute-done | bytes 262176 | tf_op jit(solution)/shard_map/ppermute | solution.py:22
  18.8 4.7 %collective-permute-start.8 = (bf16[64,2048]{1,0:T(8,128)(2,1)S(1)}, bf16[64,2048]{1,0:T(8,128)(2,1)S(1)}, u32[]{:S(2)}, u32[]{:S(2)}) collective-permute-start(bf16[64,2048]{1,0:T(8,128)(2,1)S(1)} %fusion.2.rest_0_), channel_id=1, source_target_pairs={{4,0},{0,4},{12,8},{8,12},{5,1},{1,5},{13,9},{9,13},{6,2},{2,6},{1... | collective-permute-start | bytes 786440 | tf_op jit(solution)/shard_map/ppermute | solution.py:27
  23.5 1.3 collective-permute-start.10
  24.8 5.1 %collective-permute-done.8.rest_1_ = bf16[64,2048]{1,0:T(8,128)(2,1)S(1)} collective-permute-done((bf16[64,2048]{1,0:T(8,128)(2,1)S(1)}, bf16[64,2048]{1,0:T(8,128)(2,1)S(1)}, u32[]{:S(2)}, u32[]{:S(2)}) %collective-permute-start.8) | collective-permute-done | bytes 262176 | tf_op jit(solution)/shard_map/ppermute | solution.py:27
  31.2 1.1 collective-permute-done
  32.4 1.4 collective-permute-start.3
  33.7 4.6 %collective-permute-start.2 = (f32[2,16,64]{2,1,0:T(8,128)S(1)}, f32[2,16,64]{2,1,0:T(8,128)S(1)}, u32[]{:S(2)}, u32[]{:S(2)}) collective-permute-start(f32[2,16,64]{2,1,0:T(8,128)S(1)} %pad_maximum_fusion.1.rest_0_), channel_id=1, source_target_pairs={{8,0},{12,4},{0,8},{4,12},{9,1},{13,5},{1,9},{5,13},{10,2},{14,6},... | collective-permute-start | bytes 24584 | tf_op jit(solution)/shard_map/ppermute | solution.py:27
  38.3 1.5 collective-permute-start.13
  39.8 1.5 collective-permute-start.12
  41.4 4.8 %collective-permute-done.13.rest_4_ = bf16[64,2048]{1,0:T(8,128)(2,1)S(1)} collective-permute-done((bf16[64,2048]{1,0:T(8,128)(2,1)S(1)}, bf16[64,2048]{1,0:T(8,128)(2,1)S(1)}, u32[]{:S(2)}, u32[]{:S(2)}) %collective-permute-start.13) | collective-permute-done | bytes 262176 | tf_op jit(solution)/shard_map/ppermute | solution.py:22
  46.2 3.1 %collective-permute-done.12 = bf16[64,2048]{1,0:T(8,128)(2,1)S(1)} collective-permute-done((bf16[64,2048]{1,0:T(8,128)(2,1)S(1)}, bf16[64,2048]{1,0:T(8,128)(2,1)S(1)}, u32[]{:S(2)}, u32[]{:S(2)}) %collective-permute-start.12) | collective-permute-done | bytes 262176 | tf_op jit(solution)/shard_map/ppermute | solution.py:323
  50.2 1.5 collective-permute-start.15
  52.2 6.4 %collective-permute-done.14.rest_5_ = bf16[64,2048]{1,0:T(8,128)(2,1)S(1)} collective-permute-done((bf16[64,2048]{1,0:T(8,128)(2,1)S(1)}, bf16[64,2048]{1,0:T(8,128)(2,1)S(1)}, u32[]{:S(2)}, u32[]{:S(2)}) %collective-permute-start.14) | collective-permute-done | bytes 262176 | tf_op jit(solution)/shard_map/ppermute | solution.py:22
  59.1 5.1 %collective-permute-done.15.rest_6_ = bf16[64,2048]{1,0:T(8,128)(2,1)S(1)} collective-permute-done((bf16[64,2048]{1,0:T(8,128)(2,1)S(1)}, bf16[64,2048]{1,0:T(8,128)(2,1)S(1)}, u32[]{:S(2)}, u32[]{:S(2)}) %collective-permute-start.15) | collective-permute-done | bytes 262176 | tf_op jit(solution)/shard_map/ppermute | solution.py:22
  64.2 5.2 %collective-permute-done.16.rest_7_ = bf16[64,2048]{1,0:T(8,128)(2,1)S(1)} collective-permute-done((bf16[64,2048]{1,0:T(8,128)(2,1)S(1)}, bf16[64,2048]{1,0:T(8,128)(2,1)S(1)}, u32[]{:S(2)}, u32[]{:S(2)}) %collective-permute-start.16) | collective-permute-done | bytes 262176 | tf_op jit(solution)/shard_map/ppermute | solution.py:22
  69.3 3.1 %tables.1 = (bf16[2,384,256]{2,1,0:T(8,128)(2,1)S(1)}, bf16[2,256,384]{2,1,0:T(8,128)(2,1)S(1)}) custom-call(s32[1]{0:T(128)} %bitcast.base_ref, f32[2,16,64]{2,1,0:T(8,128)S(1)} %pad_maximum_fusion.1.rest_0_, f32[2,16,64]{2,1,0:T(8,128)S(1)} %collective-permute-done.1.rest_1_, f32[2,16,64]{2,1,0:T(8,128)S(1)} %collective-permute-done.2.rest_2_, ...), custom_call_target="tpu_custom_call" | custom-call | tf_op jit(solution)/shard_map/tables/pallas_call | solution.py:284
  74.8 19.6 %experts_first.1 = (bf16[4,192,512]{2,1,0:T(8,128)(2,1)}, bf16[256,1024]{1,0:T(8,128)(2,1)}, bf16[256,1024]{1,0:T(8,128)(2,1)}, bf16[256,1024]{1,0:T(8,128)(2,1)}, bf16[256,1024]{1,0:T(8,128)(2,1)}) custom-call(bf16[2,384,256]{2,1,0:T(8,128)(2,1)} %copy-done.1, bf16[2,256,384]{2,1,0:T(8,128)(2,1)} %copy-done, bf16[64,2048]{1,0:T(8,128)(2,1)} %copy-done.2, ...), custom_call_target="tpu_custom_call" | custom-call | tf_op jit(solution)/shard_map/experts_first/pallas_call | solution.py:354
  94.5 7.6 %experts_later.1 = (bf16[256,768]{1,0:T(8,128)(2,1)}, bf16[256,768]{1,0:T(8,128)(2,1)}, bf16[256,768]{1,0:T(8,128)(2,1)}, bf16[256,768]{1,0:T(8,128)(2,1)}, bf16...) custom-call(bf16[2,256,384]{2,1,0:T(8,128)(2,1)} %copy-done, ...), custom_call_target="tpu_custom_call" | custom-call | flops 3221225472 | bytes 8388608 | tf_op jit(solution)/shard_map/experts_later/pallas_call | solution.py:376
  105.4 5.2 %collective-permute-done.37 = bf16[256,256]{1,0:T(8,128)(2,1)S(1)} collective-permute-done((bf16[256,256]{1,0:T(8,128)(2,1)S(1)}, bf16[256,256]{1,0:T(8,128)(2,1)S(1)}, u32[]{:S(2)}, u32[]{:S(2)}) %collective-permute-start.37) | collective-permute-done | bytes 131104 | tf_op jit(solution)/shard_map/ppermute | solution.py:22
  112.8 3.2 %collective-permute-done.38 = bf16[2,64,256]{2,1,0:T(8,128)(2,1)S(1)} collective-permute-done((bf16[2,64,256]{2,1,0:T(8,128)(2,1)S(1)}, bf16[2,64,256]{2,1,0:T(8,128)(2,1)S(1)}, u32[]{:S(2)}, u32[]{:S(2)}) %collective-permute-start.38) | collective-permute-done | bytes 65568 | tf_op jit(solution)/shard_map/ppermute | solution.py:27
  118.3 1.2 collective-permute-start.27
  119.5 1.3 collective-permute-done.39
  120.9 8.3 %collective-permute-done.32 = bf16[256,768]{1,0:T(8,128)(2,1)S(1)} collective-permute-done((bf16[256,768]{1,0:T(8,128)(2,1)S(1)}, bf16[256,768]{1,0:T(8,128)(2,1)S(1)}, u32[]{:S(2)}, u32[]{:S(2)}) %collective-permute-start.32) | collective-permute-done | bytes 393248 | tf_op jit(solution)/shard_map/ppermute | solution.py:22
  129.2 1.1 convert_add_fusion.1
  130.4 2.1 %collective-permute-start.33 = (bf16[2,64,768]{2,1,0:T(8,128)(2,1)S(1)}, bf16[2,64,768]{2,1,0:T(8,128)(2,1)S(1)}, u32[]{:S(2)}, u32[]{:S(2)}) collective-permute-start(bf16[2,64,768]{2,1,0:T(8,128)(2,1)S(1)} %fusion.15), channel_id=1, source_target_pairs={{4,0},{0,4},{12,8},{8,12},{5,1},{1,5},{13,9},{9,13},{6,2},{2,6},{1... | collective-permute-start | bytes 589832 | tf_op jit(solution)/shard_map/ppermute | solution.py:27
  132.5 6.7 %collective-permute-done.27 = bf16[256,1024]{1,0:T(8,128)(2,1)S(1)} collective-permute-done((bf16[256,1024]{1,0:T(8,128)(2,1)S(1)}, bf16[256,1024]{1,0:T(8,128)(2,1)S(1)}, u32[]{:S(2)}, u32[]{:S(2)}) %collective-permute-start.27) | collective-permute-done | bytes 524320 | tf_op jit(solution)/shard_map/ppermute | solution.py:22
  139.4 2.0 %collective-permute-start.28 = (bf16[2,64,1024]{2,1,0:T(8,128)(2,1)S(1)}, bf16[2,64,1024]{2,1,0:T(8,128)(2,1)S(1)}, u32[]{:S(2)}, u32[]{:S(2)}) collective-permute-start(bf16[2,64,1024]{2,1,0:T(8,128)(2,1)S(1)} %fusion.12), channel_id=1, source_target_pairs={{4,0},{0,4},{12,8},{8,12},{5,1},{1,5},{13,9},{9,13},{6,2},{2,6},{1... | collective-permute-start | bytes 786440 | tf_op jit(solution)/shard_map/ppermute | solution.py:27
  141.6 7.1 %collective-permute-done.28 = bf16[2,64,1024]{2,1,0:T(8,128)(2,1)S(1)} collective-permute-done((bf16[2,64,1024]{2,1,0:T(8,128)(2,1)S(1)}, bf16[2,64,1024]{2,1,0:T(8,128)(2,1)S(1)}, u32[]{:S(2)}, u32[]{:S(2)}) %collective-permute-start.28) | collective-permute-done | bytes 262176 | tf_op jit(solution)/shard_map/ppermute | solution.py:27
  149.4 6.8 %collective-permute-done.29 = bf16[1,64,1024]{2,1,0:T(8,128)(2,1)S(1)} collective-permute-done((bf16[1,64,1024]{2,1,0:T(8,128)(2,1)S(1)}, bf16[1,64,1024]{2,1,0:T(8,128)(2,1)S(1)}, u32[]{:S(2)}, u32[]{:S(2)}) %collective-permute-start.29) | collective-permute-done | bytes 131104 | tf_op jit(solution)/shard_map/ppermute | solution.py:27
  (126 shorter events, 18.4 us)
Async XLA Ops:
  7.0 9.5 %collective-permute-start.6 = (bf16[64,2048]{1,0:T(8,128)(2,1)S(1)}, bf16[64,2048]{1,0:T(8,128)(2,1)S(1)}, u32[]{:S(2)}, u32[]{:S(2)}) collective-permute-start(bf16[64,2048]{1,0:T(8,128)(2,1)S(1)} %fusion.11), channel_id=1, source_target_pairs={{2,0},{0,2},{3,1},{1,3},{6,4},{4,6},{7,5},{5,7},{10,8},{8,10},{11,... | collective-permute-start | bytes 786440 | tf_op jit(solution)/shard_map/ppermute | solution.py:22
  18.1 5.4 %collective-permute-start.9 = (bf16[64,2048]{1,0:T(8,128)(2,1)S(1)}, bf16[64,2048]{1,0:T(8,128)(2,1)S(1)}, u32[]{:S(2)}, u32[]{:S(2)}) collective-permute-start(bf16[64,2048]{1,0:T(8,128)(2,1)S(1)} %fusion.2.rest_0_), channel_id=1, source_target_pairs={{4,8},{8,4},{5,9},{9,5},{6,10},{10,6},{7,11},{11,7},{20,24},{24,20... | collective-permute-start | bytes 786440 | tf_op jit(solution)/shard_map/ppermute | solution.py:320
  18.8 11.1 %collective-permute-start.8 = (bf16[64,2048]{1,0:T(8,128)(2,1)S(1)}, bf16[64,2048]{1,0:T(8,128)(2,1)S(1)}, u32[]{:S(2)}, u32[]{:S(2)}) collective-permute-start(bf16[64,2048]{1,0:T(8,128)(2,1)S(1)} %fusion.2.rest_0_), channel_id=1, source_target_pairs={{4,0},{0,4},{12,8},{8,12},{5,1},{1,5},{13,9},{9,13},{6,2},{2,6},{1... | collective-permute-start | bytes 786440 | tf_op jit(solution)/shard_map/ppermute | solution.py:27
  23.5 14.9 %collective-permute-start.10 = (bf16[64,2048]{1,0:T(8,128)(2,1)S(1)}, bf16[64,2048]{1,0:T(8,128)(2,1)S(1)}, u32[]{:S(2)}, u32[]{:S(2)}) collective-permute-start(bf16[64,2048]{1,0:T(8,128)(2,1)S(1)} %collective-permute-done.9), channel_id=1, source_target_pairs={{4,0},{8,12},{5,1},{9,13},{6,2},{10,14},{7,3},{11,15},{20,16},{24,... | collective-permute-start | bytes 786440 | tf_op jit(solution)/shard_map/ppermute | solution.py:322
  29.8 10.0 %collective-permute-start.11 = (bf16[64,2048]{1,0:T(8,128)(2,1)S(1)}, bf16[64,2048]{1,0:T(8,128)(2,1)S(1)}, u32[]{:S(2)}, u32[]{:S(2)}) collective-permute-start(bf16[64,2048]{1,0:T(8,128)(2,1)S(1)} %collective-permute-done.8.rest_1_), channel_id=1, source_target_pairs={{4,8},{8,4},{5,9},{9,5},{6,10},{10,6},{7,11},{11,7},{20,24},{24,20... | collective-permute-start | bytes 786440 | tf_op jit(solution)/shard_map/ppermute | solution.py:321
  32.4 16.9 %collective-permute-start.3 = (f32[2,16,64]{2,1,0:T(8,128)S(1)}, f32[2,16,64]{2,1,0:T(8,128)S(1)}, u32[]{:S(2)}, u32[]{:S(2)}) collective-permute-start(f32[2,16,64]{2,1,0:T(8,128)S(1)} %pad_maximum_fusion.1.rest_0_), channel_id=1, source_target_pairs={{12,0},{8,4},{4,8},{0,12},{13,1},{9,5},{5,9},{1,13},{14,2},{10,6},... | collective-permute-start | bytes 24584 | tf_op jit(solution)/shard_map/ppermute | solution.py:27
  33.7 16.2 %collective-permute-start.2 = (f32[2,16,64]{2,1,0:T(8,128)S(1)}, f32[2,16,64]{2,1,0:T(8,128)S(1)}, u32[]{:S(2)}, u32[]{:S(2)}) collective-permute-start(f32[2,16,64]{2,1,0:T(8,128)S(1)} %pad_maximum_fusion.1.rest_0_), channel_id=1, source_target_pairs={{8,0},{12,4},{0,8},{4,12},{9,1},{13,5},{1,9},{5,13},{10,2},{14,6},... | collective-permute-start | bytes 24584 | tf_op jit(solution)/shard_map/ppermute | solution.py:27
  38.3 11.8 %collective-permute-start.1 = (f32[2,16,64]{2,1,0:T(8,128)S(1)}, f32[2,16,64]{2,1,0:T(8,128)S(1)}, u32[]{:S(2)}, u32[]{:S(2)}) collective-permute-start(f32[2,16,64]{2,1,0:T(8,128)S(1)} %pad_maximum_fusion.1.rest_0_), channel_id=1, source_target_pairs={{4,0},{0,4},{12,8},{8,12},{5,1},{1,5},{13,9},{9,13},{6,2},{2,6},{1... | collective-permute-start | bytes 24584 | tf_op jit(solution)/shard_map/ppermute | solution.py:27
  38.3 7.8 %collective-permute-start.13 = (bf16[64,2048]{1,0:T(8,128)(2,1)S(1)}, bf16[64,2048]{1,0:T(8,128)(2,1)S(1)}, u32[]{:S(2)}, u32[]{:S(2)}) collective-permute-start(bf16[64,2048]{1,0:T(8,128)(2,1)S(1)} %fusion.2.rest_0_), channel_id=1, source_target_pairs={{2,0},{0,2},{3,1},{1,3},{6,4},{4,6},{7,5},{5,7},{10,8},{8,10},{11,... | collective-permute-start | bytes 786440 | tf_op jit(solution)/shard_map/ppermute | solution.py:22
  39.8 9.4 %collective-permute-start.12 = (bf16[64,2048]{1,0:T(8,128)(2,1)S(1)}, bf16[64,2048]{1,0:T(8,128)(2,1)S(1)}, u32[]{:S(2)}, u32[]{:S(2)}) collective-permute-start(bf16[64,2048]{1,0:T(8,128)(2,1)S(1)} %collective-permute-done.11), channel_id=1, source_target_pairs={{4,0},{8,12},{5,1},{9,13},{6,2},{10,14},{7,3},{11,15},{20,16},{24,... | collective-permute-start | bytes 786440 | tf_op jit(solution)/shard_map/ppermute | solution.py:323
  46.2 5.5 %collective-permute-start.17 = (bf16[64,2048]{1,0:T(8,128)(2,1)S(1)}, bf16[64,2048]{1,0:T(8,128)(2,1)S(1)}, u32[]{:S(2)}, u32[]{:S(2)}) collective-permute-start(bf16[64,2048]{1,0:T(8,128)(2,1)S(1)} %fusion.2.rest_0_), channel_id=1, source_target_pairs={{1,0},{0,1},{3,2},{2,3},{5,4},{4,5},{7,6},{6,7},{9,8},{8,9},{11,10... | collective-permute-start | bytes 786440 | tf_op jit(solution)/shard_map/ppermute | solution.py:22
  49.3 9.2 %collective-permute-start.14 = (bf16[64,2048]{1,0:T(8,128)(2,1)S(1)}, bf16[64,2048]{1,0:T(8,128)(2,1)S(1)}, u32[]{:S(2)}, u32[]{:S(2)}) collective-permute-start(bf16[64,2048]{1,0:T(8,128)(2,1)S(1)} %collective-permute-done.8.rest_1_), channel_id=1, source_target_pairs={{2,0},{0,2},{3,1},{1,3},{6,4},{4,6},{7,5},{5,7},{10,8},{8,10},{11,... | collective-permute-start | bytes 786440 | tf_op jit(solution)/shard_map/ppermute | solution.py:22
  49.9 8.7 %collective-permute-start.18 = (bf16[64,2048]{1,0:T(8,128)(2,1)S(1)}, bf16[64,2048]{1,0:T(8,128)(2,1)S(1)}, u32[]{:S(2)}, u32[]{:S(2)}) collective-permute-start(bf16[64,2048]{1,0:T(8,128)(2,1)S(1)} %collective-permute-done.8.rest_1_), channel_id=1, source_target_pairs={{1,0},{0,1},{3,2},{2,3},{5,4},{4,5},{7,6},{6,7},{9,8},{8,9},{11,10... | collective-permute-start | bytes 786440 | tf_op jit(solution)/shard_map/ppermute | solution.py:22
  50.2 14.0 %collective-permute-start.15 = (bf16[64,2048]{1,0:T(8,128)(2,1)S(1)}, bf16[64,2048]{1,0:T(8,128)(2,1)S(1)}, u32[]{:S(2)}, u32[]{:S(2)}) collective-permute-start(bf16[64,2048]{1,0:T(8,128)(2,1)S(1)} %broadcast_select_fusion.1.rest_2_), channel_id=1, source_target_pairs={{2,0},{0,2},{3,1},{1,3},{6,4},{4,6},{7,5},{5,7},{10,8},{8,10},{11,... | collective-permute-start | bytes 786440 | tf_op jit(solution)/shard_map/ppermute | solution.py:22
  51.7 17.7 %collective-permute-start.16 = (bf16[64,2048]{1,0:T(8,128)(2,1)S(1)}, bf16[64,2048]{1,0:T(8,128)(2,1)S(1)}, u32[]{:S(2)}, u32[]{:S(2)}) collective-permute-start(bf16[64,2048]{1,0:T(8,128)(2,1)S(1)} %broadcast_select_fusion.rest_3_), channel_id=1, source_target_pairs={{2,0},{0,2},{3,1},{1,3},{6,4},{4,6},{7,5},{5,7},{10,8},{8,10},{11,... | collective-permute-start | bytes 786440 | tf_op jit(solution)/shard_map/ppermute | solution.py:22
  52.2 21.7 %collective-permute-start.19 = (bf16[64,2048]{1,0:T(8,128)(2,1)S(1)}, bf16[64,2048]{1,0:T(8,128)(2,1)S(1)}, u32[]{:S(2)}, u32[]{:S(2)}) collective-permute-start(bf16[64,2048]{1,0:T(8,128)(2,1)S(1)} %broadcast_select_fusion.1.rest_2_), channel_id=1, source_target_pairs={{1,0},{0,1},{3,2},{2,3},{5,4},{4,5},{7,6},{6,7},{9,8},{8,9},{11,10... | collective-permute-start | bytes 786440 | tf_op jit(solution)/shard_map/ppermute | solution.py:22
  58.6 15.4 %collective-permute-start.22 = (bf16[64,2048]{1,0:T(8,128)(2,1)S(1)}, bf16[64,2048]{1,0:T(8,128)(2,1)S(1)}, u32[]{:S(2)}, u32[]{:S(2)}) collective-permute-start(bf16[64,2048]{1,0:T(8,128)(2,1)S(1)} %collective-permute-done.14.rest_5_), channel_id=1, source_target_pairs={{1,0},{0,1},{3,2},{2,3},{5,4},{4,5},{7,6},{6,7},{9,8},{8,9},{11,10... | collective-permute-start | bytes 786440 | tf_op jit(solution)/shard_map/ppermute | solution.py:22
  58.6 15.4 %collective-permute-start.20 = (bf16[64,2048]{1,0:T(8,128)(2,1)S(1)}, bf16[64,2048]{1,0:T(8,128)(2,1)}, u32[]{:S(2)}, u32[]{:S(2)}) collective-permute-start(bf16[64,2048]{1,0:T(8,128)(2,1)S(1)} %broadcast_select_fusion.rest_3_), channel_id=1, source_target_pairs={{1,0},{0,1},{3,2},{2,3},{5,4},{4,5},{7,6},{6,7},{9,8},{8,9},{11,10... | collective-permute-start | bytes 786440 | tf_op jit(solution)/shard_map/ppermute | solution.py:22
  64.2 9.8 %collective-permute-start.23 = (bf16[64,2048]{1,0:T(8,128)(2,1)S(1)}, bf16[64,2048]{1,0:T(8,128)(2,1)}, u32[]{:S(2)}, u32[]{:S(2)}) collective-permute-start(bf16[64,2048]{1,0:T(8,128)(2,1)S(1)} %collective-permute-done.15.rest_6_), channel_id=1, source_target_pairs={{1,0},{0,1},{3,2},{2,3},{5,4},{4,5},{7,6},{6,7},{9,8},{8,9},{11,10... | collective-permute-start | bytes 786440 | tf_op jit(solution)/shard_map/ppermute | solution.py:22
  69.3 4.6 %collective-permute-start.24 = (bf16[64,2048]{1,0:T(8,128)(2,1)S(1)}, bf16[64,2048]{1,0:T(8,128)(2,1)}, u32[]{:S(2)}, u32[]{:S(2)}) collective-permute-start(bf16[64,2048]{1,0:T(8,128)(2,1)S(1)} %collective-permute-done.16.rest_7_), channel_id=1, source_target_pairs={{1,0},{0,1},{3,2},{2,3},{5,4},{4,5},{7,6},{6,7},{9,8},{8,9},{11,10... | collective-permute-start | bytes 786440 | tf_op jit(solution)/shard_map/ppermute | solution.py:22
  104.8 5.8 %collective-permute-start.37 = (bf16[256,256]{1,0:T(8,128)(2,1)S(1)}, bf16[256,256]{1,0:T(8,128)(2,1)S(1)}, u32[]{:S(2)}, u32[]{:S(2)}) collective-permute-start(bf16[256,256]{1,0:T(8,128)(2,1)S(1)} %add_convert_fusion.2), channel_id=1, source_target_pairs={{2,0},{0,2},{3,1},{1,3},{6,4},{4,6},{7,5},{5,7},{10,8},{8,10},{11,... | collective-permute-start | bytes 393224 | tf_op jit(solution)/shard_map/ppermute | solution.py:22
  111.6 4.3 %collective-permute-start.38 = (bf16[2,64,256]{2,1,0:T(8,128)(2,1)S(1)}, bf16[2,64,256]{2,1,0:T(8,128)(2,1)S(1)}, u32[]{:S(2)}, u32[]{:S(2)}) collective-permute-start(bf16[2,64,256]{2,1,0:T(8,128)(2,1)S(1)} %fusion.24), channel_id=1, source_target_pairs={{4,0},{0,4},{12,8},{8,12},{5,1},{1,5},{13,9},{9,13},{6,2},{2,6},{1... | collective-permute-start | bytes 196616 | tf_op jit(solution)/shard_map/ppermute | solution.py:27
  111.7 20.7 %collective-permute-start.25 = (bf16[256,1024]{1,0:T(8,128)(2,1)S(1)}, bf16[256,1024]{1,0:T(8,128)(2,1)S(1)}, u32[]{:S(2)}, u32[]{:S(2)}) collective-permute-start(bf16[256,1024]{1,0:T(8,128)(2,1)S(1)} %copy-done.20), channel_id=1, source_target_pairs={{1,0},{0,1},{3,2},{2,3},{5,4},{4,5},{7,6},{6,7},{9,8},{8,9},{11,10... | collective-permute-start | bytes 1572872 | tf_op jit(solution)/shard_map/ppermute | solution.py:22
  111.8 6.3 %collective-permute-start.26 = (bf16[256,1024]{1,0:T(8,128)(2,1)S(1)}, bf16[256,1024]{1,0:T(8,128)(2,1)S(1)}, u32[]{:S(2)}, u32[]{:S(2)}) collective-permute-start(bf16[256,1024]{1,0:T(8,128)(2,1)S(1)} %copy-done.21), channel_id=1, source_target_pairs={{1,0},{0,1},{3,2},{2,3},{5,4},{4,5},{7,6},{6,7},{9,8},{8,9},{11,10... | collective-permute-start | bytes 1572872 | tf_op jit(solution)/shard_map/ppermute | solution.py:22
  112.3 8.6 %collective-permute-start.30 = (bf16[256,768]{1,0:T(8,128)(2,1)}, bf16[256,768]{1,0:T(8,128)(2,1)S(1)}, u32[]{:S(2)}, u32[]{:S(2)}) collective-permute-start(bf16[256,768]{1,0:T(8,128)(2,1)} %get-tuple-element.28), channel_id=1, source_target_pairs={{1,0},{0,1},{3,2},{2,3},{5,4},{4,5},{7,6},{6,7},{9,8},{8,9},{11,10... | collective-permute-start | bytes 1179656 | tf_op jit(solution)/shard_map/ppermute | solution.py:22
  116.0 4.9 %collective-permute-start.39 = (bf16[1,64,256]{2,1,0:T(8,128)(2,1)S(1)}, bf16[1,64,256]{2,1,0:T(8,128)(2,1)S(1)}, u32[]{:S(2)}, u32[]{:S(2)}) collective-permute-start(bf16[1,64,256]{2,1,0:T(8,128)(2,1)S(1)} %fusion.28), channel_id=1, source_target_pairs={{8,0},{12,4},{0,8},{4,12},{9,1},{13,5},{1,9},{5,13},{10,2},{14,6},... | collective-permute-start | bytes 98312 | tf_op jit(solution)/shard_map/ppermute | solution.py:27
  117.2 12.1 %collective-permute-start.32 = (bf16[256,768]{1,0:T(8,128)(2,1)S(1)}, bf16[256,768]{1,0:T(8,128)(2,1)S(1)}, u32[]{:S(2)}, u32[]{:S(2)}) collective-permute-start(bf16[256,768]{1,0:T(8,128)(2,1)S(1)} %add_convert_fusion.1), channel_id=1, source_target_pairs={{2,0},{0,2},{3,1},{1,3},{6,4},{4,6},{7,5},{5,7},{10,8},{8,10},{11,... | collective-permute-start | bytes 1179656 | tf_op jit(solution)/shard_map/ppermute | solution.py:22
  118.3 20.8 %collective-permute-start.27 = (bf16[256,1024]{1,0:T(8,128)(2,1)S(1)}, bf16[256,1024]{1,0:T(8,128)(2,1)S(1)}, u32[]{:S(2)}, u32[]{:S(2)}) collective-permute-start(bf16[256,1024]{1,0:T(8,128)(2,1)S(1)} %add_convert_fusion), channel_id=1, source_target_pairs={{2,0},{0,2},{3,1},{1,3},{6,4},{4,6},{7,5},{5,7},{10,8},{8,10},{11,... | collective-permute-start | bytes 1572872 | tf_op jit(solution)/shard_map/ppermute | solution.py:22
  130.4 11.0 %collective-permute-start.33 = (bf16[2,64,768]{2,1,0:T(8,128)(2,1)S(1)}, bf16[2,64,768]{2,1,0:T(8,128)(2,1)S(1)}, u32[]{:S(2)}, u32[]{:S(2)}) collective-permute-start(bf16[2,64,768]{2,1,0:T(8,128)(2,1)S(1)} %fusion.15), channel_id=1, source_target_pairs={{4,0},{0,4},{12,8},{8,12},{5,1},{1,5},{13,9},{9,13},{6,2},{2,6},{1... | collective-permute-start | bytes 589832 | tf_op jit(solution)/shard_map/ppermute | solution.py:27
  139.4 9.3 %collective-permute-start.28 = (bf16[2,64,1024]{2,1,0:T(8,128)(2,1)S(1)}, bf16[2,64,1024]{2,1,0:T(8,128)(2,1)S(1)}, u32[]{:S(2)}, u32[]{:S(2)}) collective-permute-start(bf16[2,64,1024]{2,1,0:T(8,128)(2,1)S(1)} %fusion.12), channel_id=1, source_target_pairs={{4,0},{0,4},{12,8},{8,12},{5,1},{1,5},{13,9},{9,13},{6,2},{2,6},{1... | collective-permute-start | bytes 786440 | tf_op jit(solution)/shard_map/ppermute | solution.py:27
  141.5 7.9 %collective-permute-start.34 = (bf16[1,64,768]{2,1,0:T(8,128)(2,1)S(1)}, bf16[1,64,768]{2,1,0:T(8,128)(2,1)S(1)}, u32[]{:S(2)}, u32[]{:S(2)}) collective-permute-start(bf16[1,64,768]{2,1,0:T(8,128)(2,1)S(1)} %fusion.23), channel_id=1, source_target_pairs={{8,0},{12,4},{0,8},{4,12},{9,1},{13,5},{1,9},{5,13},{10,2},{14,6},... | collective-permute-start | bytes 294920 | tf_op jit(solution)/shard_map/ppermute | solution.py:27
  148.8 7.3 %collective-permute-start.29 = (bf16[1,64,1024]{2,1,0:T(8,128)(2,1)S(1)}, bf16[1,64,1024]{2,1,0:T(8,128)(2,1)S(1)}, u32[]{:S(2)}, u32[]{:S(2)}) collective-permute-start(bf16[1,64,1024]{2,1,0:T(8,128)(2,1)S(1)} %fusion.19), channel_id=1, source_target_pairs={{8,0},{12,4},{0,8},{4,12},{9,1},{13,5},{1,9},{5,13},{10,2},{14,6},... | collective-permute-start | bytes 393224 | tf_op jit(solution)/shard_map/ppermute | solution.py:27
  (30 other events, 475.0 us)

commit v6 on v5

--- a/solution.py
+++ b/solution.py
@@ -34,16 +34,21 @@
 STEP = 1024
 
 F32, BF16 = jnp.float32, jnp.bfloat16
-ANY = pl.BlockSpec(memory_space=pl.ANY)
 VMEM = pl.BlockSpec(memory_space=pltpu.VMEM)
-SMEM = pl.BlockSpec(memory_space=pltpu.SMEM)
+HBM = pl.BlockSpec(memory_space=pltpu.HBM)
 SMALL = pltpu.CompilerParams(vmem_limit_bytes=8 * 1024 * 1024)
 PARAMS = pltpu.CompilerParams(vmem_limit_bytes=60 * 1024 * 1024)
 
 
-def codes_kernel(experts, ids_ref, weights_ref, out_ref):
-    rows, choices = ids_ref.shape
-    ids = ids_ref[...]
+def codes_kernel(experts, count, ids_ref, weights_ref, *rest):
+    far, out_ref, near, sem_ref = rest[:count], rest[count], rest[count + 1 : -1], rest[-1]
+    copies = [
+        pltpu.make_async_copy(src, dst, sem_ref.at[n]) for n, (src, dst) in enumerate(zip(far, near))
+    ]
+    for copy in copies:
+        copy.start()
+    choices, rows = ids_ref.shape
+    ids = ids_ref[...].astype(F32).T.astype(jnp.int32)
     lanes = lax.broadcasted_iota(jnp.int32, (rows, experts), 1)
     picked = [(ids[:, k : k + 1] == lanes).astype(F32) for k in range(choices)]
     chosen = functools.reduce(jnp.add, picked)
@@ -55,15 +60,20 @@
     )
     slot = [jnp.sum(p * before, axis=1, keepdims=True) for p in picked]
     codes = jnp.concatenate(slot, axis=1) + ids.astype(F32) * SLOT
-    out_ref[...] = jnp.concatenate([codes, weights_ref[...]], axis=1).T
-
-
-def tables_kernel(choices, base_ref, *rest):
+    out_ref[:choices] = codes.T
+    out_ref[choices:] = weights_ref[...]
+    for copy in copies:
+        copy.wait()
+
+
+def tables_kernel(choices, *rest):
     routes, (place_ref, back_ref) = rest[:-2], rest[-2:]
     depth = len(routes)
     cores, group_slots, out_rows = place_ref.shape
     per = depth * SLOT
-    base = base_ref[0].astype(F32)
+    z = lax.axis_index("expert")
+    index = z * cores + lax.axis_index("dp")
+    base = (index * (group_slots // depth)).astype(F32)
     for i in range(cores):
         slots = []
         for o in range(depth):
@@ -73,7 +83,13 @@
             slots.append(jnp.where((local >= 0) & (local < group_slots // depth), slot, -1.0))
         slot = jnp.concatenate(slots, axis=1).astype(jnp.int32)
         down = lax.broadcasted_iota(jnp.int32, (group_slots, out_rows), 0)
-        hit = [slot[k : k + 1] == down for k in range(choices)]
+        if depth == 4:
+            inner = (z > 0) & (z < depth - 1)
+            second, third = jnp.where(inner, slots[3], slots[2]), jnp.where(inner, slots[2], slots[3])
+            arrived = jnp.concatenate(slots[:2] + [second, third], axis=1).astype(jnp.int32)
+        else:
+            arrived = slot
+        hit = [arrived[k : k + 1] == down for k in range(choices)]
         place_ref[i] = functools.reduce(jnp.logical_or, hit).astype(F32).astype(BF16)
         turned = slot.astype(F32).T.astype(jnp.int32)
         weights = jnp.concatenate([routes[o][i, choices:] for o in range(depth)], axis=1).T
@@ -82,6 +98,17 @@
         for k in range(choices):
             total = jnp.where(turned[:, k : k + 1] == along, weights[:, k : k + 1], total)
         back_ref[i] = total.astype(BF16)
+
+
+def project_kernel(attn_ref, attn_got_ref, res_ref, res_got_ref, weight_ref, kept_ref, sent_ref):
+    same = lax.axis_index("tensor") == lax.axis_index("dp")
+    weight = weight_ref[...]
+    own = jnp.dot(attn_ref[...], weight, preferred_element_type=F32)
+    other = jnp.dot(attn_got_ref[...], weight, preferred_element_type=F32)
+    own_sum = own + res_ref[...].astype(F32)
+    other_sum = other + res_got_ref[...].astype(F32)
+    kept_ref[...] = jnp.where(same, own_sum, other)
+    sent_ref[...] = jnp.where(same, other_sum, own).astype(BF16)
 
 
 def down_copies(wd_ref, wds_ref, sem_ref, first):
@@ -129,46 +156,16 @@
                     at += size
 
 
-def first_kernel(
-    dims, place_ref, back_ref, *rest
-):
-    cores, tensors, depth, groups, first = dims
-    lengths = depth if groups > 1 else 1
+def first_kernel(dims, place_ref, back_ref, *rest):
+    cores, tensors, lengths, groups, first = dims
     count = cores * tensors * lengths
     pieces, rest = rest[:count], rest[count:]
     wg_ref, wu_ref, wd_ref, act_ref = rest[:4]
     outs_ref = rest[4 : 4 + cores * tensors]
-    x_ref, s_ref, wgs_ref, wus_ref, wds_ref, mixed_ref, x_sem, w_sem, d_sem = rest[
-        4 + cores * tensors :
-    ]
+    s_ref, wgs_ref, wus_ref, wds_ref, mixed_ref, w_sem, d_sem = rest[4 + cores * tensors :]
     d, x = lax.axis_index("dp"), lax.axis_index("tensor")
-    held = wg_ref.shape[0]
-    part, cols = pieces[0].shape
-    width = x_ref.shape[-1]
-    copies = []
-    places = list(range(lengths))
-    if depth == 4 and groups > 1:
-        z = lax.axis_index("expert")
-        inner = jnp.where((z == 1) | (z == 2), 1, 0)
-        places[2:] = [2 + inner, 3 - inner]
-    for i in range(cores):
-        at = pl.multiple_of((d + i) % cores * cols, 128)
-        for k in range(tensors):
-            for o in range(lengths):
-                n = (i * tensors + k) * lengths + o
-                g, row = (k, places[o]) if groups > 1 else (0, k)
-                row = row * part if isinstance(row, int) else pl.multiple_of(row * part, part)
-                copies.append(
-                    pltpu.make_async_copy(
-                        pieces[n],
-                        x_ref.at[g, pl.ds(row, part), pl.ds(at, cols)],
-                        x_sem.at[n],
-                    )
-                )
-    for copy in copies:
-        copy.start()
-    for copy in copies:
-        copy.wait()
+    held, slots, _ = s_ref.shape
+    cols = pieces[0].shape[1]
 
     def weights(j):
         return [
@@ -185,17 +182,25 @@
                 copy.start()
 
     start(0)
-    per = s_ref.shape[1] // groups
-    step = min(STEP, width)
-    for g in range(groups):
-        kk = (d + g + tensors - x) % tensors if groups > 1 else 0
-        for n in range(width // step):
-            at = slice(n * step, (n + 1) * step)
-            rows = jnp.dot(place_ref[g], x_ref[kk, :, at], preferred_element_type=F32)
-            rows = rows.astype(BF16)
-            for j in range(held):
-                s_ref[j, g * per : (g + 1) * per, at] = rows[j * per : (j + 1) * per]
-        if g == 0:
+    per = slots // groups
+    step = min(STEP, cols)
+    for k in range(groups):
+        g = (x + k + cores - d) % cores if groups > 1 else 0
+        place = place_ref[g]
+        at_rows = pl.ds(pl.multiple_of(g * per, per), per) if groups > 1 else slice(0, per)
+        for i in range(cores):
+            base = (d + i) % cores * cols
+            first_piece = (i * tensors + k) * lengths
+            blocks = pieces[first_piece : first_piece + count // (cores * groups)]
+            for n in range(cols // step):
+                take = slice(n * step, (n + 1) * step)
+                rows = jnp.concatenate([block[:, take] for block in blocks], axis=0)
+                rows = jnp.dot(place, rows, preferred_element_type=F32).astype(BF16)
+                at = pl.ds(pl.multiple_of(base + n * step, step), step)
+                for j in range(held):
+                    s_ref[j, at_rows, at] = rows[j * per : (j + 1) * per]
+
+        if k == 0:
             start(1)
 
     for j in range(held):
@@ -235,26 +240,54 @@
     cols_out = width // tensors
     choices = expert_ids.shape[1]
 
-    attn_all = jnp.concatenate([fetch(attn, "dp", i) for i in range(cores)], axis=0)
-    res_all = jnp.concatenate([fetch(residual, "dp", i) for i in range(cores)], axis=0)
-    partial = jnp.dot(attn_all, o_weight, preferred_element_type=F32)
-    res_here = jnp.where(x // sub == d, res_all.astype(F32), 0.0)
-    if sub == 1:
-        partial = partial + res_here
-    else:
-        at = (x % sub) * cols_out
-        partial = lax.dynamic_update_slice_in_dim(
-            partial, lax.dynamic_slice_in_dim(partial, at, cols_out, 1) + res_here, at, 1
-        )
-    parts = partial.reshape(tensors, part, cols_core)
+    far = [o_weight, attn, residual] if cores == 2 and sub == 1 else []
+    route, *near = pl.pallas_call(
+        functools.partial(codes_kernel, experts, len(far)),
+        out_shape=[jax.ShapeDtypeStruct((2 * choices, rows), F32)]
+        + [pltpu.VMEM(v.shape, v.dtype) for v in far],
+        in_specs=[VMEM, VMEM] + [HBM] * len(far),
+        out_specs=[VMEM] * (1 + len(far)),
+        scratch_shapes=[pltpu.SemaphoreType.DMA((len(far) + 1,))],
+        compiler_params=pltpu.CompilerParams(vmem_limit_bytes=50 * 1024 * 1024),
+        name="codes",
+    )(expert_ids.T, route_weights.T, *far)
 
     def place(p):
         return ((p // sub - d) % cores) * sub + p % sub
 
-    hidden = pick(parts, place(x))
-    for k in range(1, tensors):
-        sent = pick(parts, place((x - k) % tensors)).astype(BF16)
-        hidden = hidden + fetch(sent, "tensor", k).astype(F32)
+    if cores == 2 and sub == 1:
+        attn_got = fetch(attn, "dp", 1)
+        res_got = fetch(residual, "dp", 1)
+        hidden, sent = pl.pallas_call(
+            project_kernel,
+            out_shape=[
+                jax.ShapeDtypeStruct((part, cols_core), F32),
+                jax.ShapeDtypeStruct((part, cols_core), BF16),
+            ],
+            in_specs=[VMEM] * 5,
+            out_specs=[VMEM] * 2,
+            compiler_params=pltpu.CompilerParams(vmem_limit_bytes=24 * 1024 * 1024),
+            name="project",
+        )(near[1], attn_got, near[2], res_got, near[0])
+        hidden = hidden + fetch(sent, "tensor", 1).astype(F32)
+    else:
+        attn_all = jnp.concatenate([fetch(attn, "dp", i) for i in range(cores)], axis=0)
+        res_all = jnp.concatenate([fetch(residual, "dp", i) for i in range(cores)], axis=0)
+        partial = jnp.dot(attn_all, o_weight, preferred_element_type=F32)
+        res_here = jnp.where(x // sub == d, res_all.astype(F32), 0.0)
+        if sub == 1:
+            partial = partial + res_here
+        else:
+            at = (x % sub) * cols_out
+            partial = lax.dynamic_update_slice_in_dim(
+                partial, lax.dynamic_slice_in_dim(partial, at, cols_out, 1) + res_here, at, 1
+            )
+        parts = partial.reshape(tensors, part, cols_core)
+
+        hidden = pick(parts, place(x))
+        for k in range(1, tensors):
+            sent = pick(parts, place((x - k) % tensors)).astype(BF16)
+            hidden = hidden + fetch(sent, "tensor", k).astype(F32)
     hidden = hidden.astype(BF16).astype(F32)
     squares = jnp.sum(hidden * hidden, axis=1, keepdims=True)
     total = squares
@@ -264,14 +297,6 @@
     gain = lax.dynamic_slice_in_dim(norm_gain, d * cols_core, cols_core, 0)
     normed = (hidden * inverse * gain.astype(F32)[None, :]).astype(BF16)
 
-    route = pl.pallas_call(
-        functools.partial(codes_kernel, experts),
-        out_shape=jax.ShapeDtypeStruct((2 * choices, rows), F32),
-        in_specs=[VMEM, VMEM],
-        out_specs=VMEM,
-        compiler_params=SMALL,
-        name="codes",
-    )(expert_ids, route_weights)
     route = jnp.stack([fetch(route, "dp", i) for i in range(cores)])
     routes = [route]
     for o in range(1, depth):
@@ -287,11 +312,11 @@
                 jax.ShapeDtypeStruct((cores, group_slots, depth * rows), BF16),
                 jax.ShapeDtypeStruct((cores, depth * rows, group_slots), BF16),
             ],
-            in_specs=[SMEM] + [VMEM] * depth,
+            in_specs=[VMEM] * depth,
             out_specs=[VMEM, VMEM],
             compiler_params=SMALL,
             name="tables",
-        )(first_code.astype(jnp.int32).reshape(1), *routes)
+        )(*routes)
     else:
         route = jnp.stack(routes)
         local = route[:, :, :choices] - first_code.astype(F32)
@@ -351,24 +376,20 @@
             pltpu.VMEM((groups, group_slots, min(STEP, span)), BF16),
         ]
 
+    lengths = depth if groups > 1 else 1
     activated, *outs = pl.pallas_call(
-        functools.partial(first_kernel, (cores, tensors, depth, groups, spans[0])),
+        functools.partial(first_kernel, (cores, tensors, lengths, groups, spans[0])),
         out_shape=[jax.ShapeDtypeStruct((held, slots, hidden_units), BF16)] + out_shapes(spans[0]),
-        in_specs=[VMEM, VMEM] + [ANY] * (len(pieces) + 3),
+        in_specs=[VMEM] * (2 + len(pieces)) + [HBM] * 3,
         out_specs=[VMEM] * (1 + cores * tensors),
         scratch_shapes=[
-            pltpu.VMEM((groups, tensors // groups * depth * part, width), BF16),
             pltpu.VMEM((held, slots, width), BF16),
             pltpu.VMEM(w_gate.shape, BF16),
             pltpu.VMEM(w_up.shape, BF16),
         ]
         + scratch(spans[0])
-        + [
-            pltpu.SemaphoreType.DMA((len(pieces),)),
-            pltpu.SemaphoreType.DMA((2, held)),
-            pltpu.SemaphoreType.DMA((tensors, held)),
-        ],
-        compiler_params=PARAMS,
+        + [pltpu.SemaphoreType.DMA((2, held)), pltpu.SemaphoreType.DMA((tensors, held))],
+        compiler_params=pltpu.CompilerParams(vmem_limit_bytes=56 * 1024 * 1024),
         name="experts_first",
     )(placing, back, *pieces, w_gate, w_up, w_down)
 
@@ -376,7 +397,7 @@
     outs += pl.pallas_call(
         functools.partial(later_kernel, (cores, tensors, groups, spans[0], spans[1:])),
         out_shape=[shape for span in spans[1:] for shape in out_shapes(span)],
-        in_specs=[VMEM, VMEM, ANY],
+        in_specs=[VMEM, VMEM, HBM],
         out_specs=[VMEM] * (cores * tensors * len(spans[1:])),
         scratch_shapes=scratch(more) + [pltpu.SemaphoreType.DMA((tensors, held))],
         compiler_params=PARAMS,
@@ -404,6 +425,13 @@
             narrow = narrow + got.astype(F32)
         narrow = narrow.reshape(depth, rows, span)
         flip = 1
+        if depth == 4 and n + 1 == len(spans):
+            whole = narrow[0]
+            for o in range(1, depth):
+                got = across(narrow[o].astype(BF16), "expert", o)
+                whole = whole + got.astype(F32)
+            results.append(whole.astype(BF16))
+            continue
         while flip < depth:
             narrow = narrow.reshape(-1, 2, rows, span)
             got = across(narrow[:, 1].astype(BF16), "expert", flip)
@@ -435,9 +463,4 @@
     )
     if mesh.shape["tensor"] != mesh.shape["dp"]:
         return step
-    depth = mesh.shape["expert"]
-    for _ in range(1, len(CHUNKS)):
-        flip = 1
-        while flip < depth:
-            flip *= 2
     return step

time: 157 us -> 155 us (0.987)
  Pallas kernels: 30.8 us -> 37.9 us
  waiting for transfers between devices: 80.3 us -> 73.7 us
  matrix products: 4.71 us -> 0 us
    pallas_call x2 -> x3, Pallas kernels: 20.1 us -> 27.3 us  [the longest x1 19.5 us: on_device(): pl.pallas_call(functools.partial(first_kernel, (cores, tensors, lengths,...]
    ppermute x10 -> x11, waiting for transfers between devices: 23.9 us -> 18 us  [across(): return lax.ppermute(value, axis, [(i ^ flip, i) for i in range(size)])]
    ppermute x26, waiting for transfers between devices: 53.4 us -> 47.8 us  [fetch(): lax.ppermute(value, axis, [((i + step) % size, i) for i in range(size)])]
    ppermute x1, waiting for transfers between devices: 3.09 us -> 7.9 us  [on_device(): outward_3 = lax.ppermute(middle_2, 'expert', outward)]
    dot_general x1 -> x0, matrix products: 4.71 us -> none  [on_device(): partial = jnp.dot(attn_all, o_weight, preferred_element_type=F32)]
    ppermute x10 -> x11, starting transfers between devices: 15.1 us -> 16.4 us  [across(): return lax.ppermute(value, axis, [(i ^ flip, i) for i in range(size)])]
  transfers between devices with their start and end apart: 40 -> 41, of which waited for: 20 -> 15; matrix products, arithmetic and copies ran while one was open for 3% -> 4% of each run, Pallas kernels for 2% -> 5%
where the time goes in v6:
time: 155 us
  waiting for transfers between devices  73.7 us (48%)
  Pallas kernels  37.9 us (24%)
  starting transfers between devices  33.5 us (22%)
  other arithmetic  6.52 us (4%)
  local copies, waits for them, and re-layouts  2.61 us (2%)
    ppermute x26, waiting for transfers between devices, fetch(): lax.ppermute(value, axis, [((i + step) % size, i) for i in range(size)])  47.8 us
    pallas_call x1, Pallas kernels, on_device(): pl.pallas_call(functools.partial(first_kernel, (cores, tensors, lengths,...  19.5 us
    ppermute x11, waiting for transfers between devices, across(): return lax.ppermute(value, axis, [(i ^ flip, i) for i in range(size)])  18 us
    ppermute x11, starting transfers between devices, across(): return lax.ppermute(value, axis, [(i ^ flip, i) for i in range(size)])  16.4 us
    ppermute x26, starting transfers between devices, fetch(): lax.ppermute(value, axis, [((i + step) % size, i) for i in range(size)])  13 us
    ppermute x1, waiting for transfers between devices, on_device(): outward_3 = lax.ppermute(middle_2, 'expert', outward)  7.9 us
    pallas_call x1, Pallas kernels, on_device(): pl.pallas_call(functools.partial(later_kernel, (cores, tensors, groups, s...  7.64 us
    pallas_call x1, Pallas kernels, on_device(): pl.pallas_call(functools.partial(codes_kernel, experts, len(far)), out_sh...  4.74 us
  transfers between devices with their start and end apart: 41, of which 15 were waited for; matrix products, arithmetic and copies ran while one was open for 4% of the time, Pallas kernels for 5%

profile of v6, /device:TPU:0, one launch (start us, length us, event | category | flops | bytes accessed | tf_op | source)
XLA Modules:
  0.0 154.9 jit_solution(9039659724879582198)
XLA Ops:
  0.6 4.7 %codes.1 = (f32[16,64]{1,0:T(8,128)}, bf16[2048,2048]{1,0:T(8,128)(2,1)S(1)}, bf16[64,2048]{1,0:T(8,128)(2,1)S(1)}, bf16[64,2048]{1,0:T(8,128)(2,1)S(1)}) custom-call(s32[8,64]{1,0:T(8,128)} %bitcast.60, f32[8,64]{1,0:T(8,128)} %bitcast.61, bf16[2048,2048]{1,0:T(8,128)(2,1)} %rest_0_.1, bf16[64,2048]{1,0:T(8,128)(2,1)} %rest_1_.1, bf16[64,2048]{1,0:T(8,128)(2,1)} %rest_2_.1), custom_call_target="tpu_custom_call" | custom-call | tf_op jit(solution)/shard_map/codes/pallas_call | solution.py:244
  5.3 3.0 %project.1 = (f32[64,2048]{1,0:T(8,128)S(1)}, bf16[64,2048]{1,0:T(8,128)(2,1)S(1)}) custom-call(bf16[64,2048]{1,0:T(8,128)(2,1)S(1)} %get-tuple-element.29.attn_ref, bf16[64,2048]{1,0:T(8,128)(2,1)S(1)} %collective-permute-done.4.attn_got_ref, bf16[64,2048]{1,0:T(8,128)(2,1)S(1)} %get-tuple-element.30.res_ref, ...), custom_call_target="tpu_custom_call" | custom-call | tf_op jit(solution)/shard_map/project/pallas_call | solution.py:261
  8.4 3.0 %collective-permute-start.6 = (bf16[64,2048]{1,0:T(8,128)(2,1)S(1)}, bf16[64,2048]{1,0:T(8,128)(2,1)S(1)}, u32[]{:S(2)}, u32[]{:S(2)}) collective-permute-start(bf16[64,2048]{1,0:T(8,128)(2,1)S(1)} %get-tuple-element.33), channel_id=1, source_target_pairs={{2,0},{0,2},{3,1},{1,3},{6,4},{4,6},{7,5},{5,7},{10,8},{8,10},{11,... | collective-permute-start | bytes 786440 | tf_op jit(solution)/shard_map/ppermute | solution.py:22
  11.4 6.5 %collective-permute-done.6 = bf16[64,2048]{1,0:T(8,128)(2,1)S(1)} collective-permute-done((bf16[64,2048]{1,0:T(8,128)(2,1)S(1)}, bf16[64,2048]{1,0:T(8,128)(2,1)S(1)}, u32[]{:S(2)}, u32[]{:S(2)}) %collective-permute-start.6) | collective-permute-done | bytes 262176 | tf_op jit(solution)/shard_map/ppermute | solution.py:22
  18.2 1.1 collective-permute-done.7
  19.4 1.9 %collective-permute-start.8 = (bf16[64,2048]{1,0:T(8,128)(2,1)S(1)}, bf16[64,2048]{1,0:T(8,128)(2,1)S(1)}, u32[]{:S(2)}, u32[]{:S(2)}) collective-permute-start(bf16[64,2048]{1,0:T(8,128)(2,1)S(1)} %fusion.2.rest_0_), channel_id=1, source_target_pairs={{4,0},{0,4},{12,8},{8,12},{5,1},{1,5},{13,9},{9,13},{6,2},{2,6},{1... | collective-permute-start | bytes 786440 | tf_op jit(solution)/shard_map/ppermute | solution.py:27
  22.0 6.0 %collective-permute-done.8.rest_1_ = bf16[64,2048]{1,0:T(8,128)(2,1)S(1)} collective-permute-done((bf16[64,2048]{1,0:T(8,128)(2,1)S(1)}, bf16[64,2048]{1,0:T(8,128)(2,1)S(1)}, u32[]{:S(2)}, u32[]{:S(2)}) %collective-permute-start.8) | collective-permute-done | bytes 262176 | tf_op jit(solution)/shard_map/ppermute | solution.py:27
  28.6 1.3 collective-permute-start.10
  30.0 1.4 collective-permute-done
  32.1 4.6 %collective-permute-start.1 = (f32[2,16,64]{2,1,0:T(8,128)S(1)}, f32[2,16,64]{2,1,0:T(8,128)S(1)}, u32[]{:S(2)}, u32[]{:S(2)}) collective-permute-start(f32[2,16,64]{2,1,0:T(8,128)S(1)} %pad_maximum_fusion.1.rest_0_), channel_id=1, source_target_pairs={{4,0},{0,4},{12,8},{8,12},{5,1},{1,5},{13,9},{9,13},{6,2},{2,6},{1... | collective-permute-start | bytes 24584 | tf_op jit(solution)/shard_map/ppermute | solution.py:27
  37.3 1.7 %collective-permute-start.3 = (f32[2,16,64]{2,1,0:T(8,128)S(1)}, f32[2,16,64]{2,1,0:T(8,128)S(1)}, u32[]{:S(2)}, u32[]{:S(2)}) collective-permute-start(f32[2,16,64]{2,1,0:T(8,128)S(1)} %pad_maximum_fusion.1.rest_0_), channel_id=1, source_target_pairs={{12,0},{8,4},{4,8},{0,12},{13,1},{9,5},{5,9},{1,13},{14,2},{10,6},... | collective-permute-start | bytes 24584 | tf_op jit(solution)/shard_map/ppermute | solution.py:27
  39.0 1.5 collective-permute-start.13
  40.5 1.5 collective-permute-start.12
  42.0 7.9 %collective-permute-done.12 = bf16[64,2048]{1,0:T(8,128)(2,1)S(1)} collective-permute-done((bf16[64,2048]{1,0:T(8,128)(2,1)S(1)}, bf16[64,2048]{1,0:T(8,128)(2,1)S(1)}, u32[]{:S(2)}, u32[]{:S(2)}) %collective-permute-start.12) | collective-permute-done | bytes 262176 | tf_op jit(solution)/shard_map/ppermute | solution.py:348
  51.1 1.5 collective-permute-start.15
  53.2 6.1 %collective-permute-done.14.rest_5_ = bf16[64,2048]{1,0:T(8,128)(2,1)S(1)} collective-permute-done((bf16[64,2048]{1,0:T(8,128)(2,1)S(1)}, bf16[64,2048]{1,0:T(8,128)(2,1)S(1)}, u32[]{:S(2)}, u32[]{:S(2)}) %collective-permute-start.14) | collective-permute-done | bytes 262176 | tf_op jit(solution)/shard_map/ppermute | solution.py:22
  59.9 5.0 %collective-permute-done.15.rest_6_ = bf16[64,2048]{1,0:T(8,128)(2,1)S(1)} collective-permute-done((bf16[64,2048]{1,0:T(8,128)(2,1)S(1)}, bf16[64,2048]{1,0:T(8,128)(2,1)S(1)}, u32[]{:S(2)}, u32[]{:S(2)}) %collective-permute-start.15) | collective-permute-done | bytes 262176 | tf_op jit(solution)/shard_map/ppermute | solution.py:22
  64.9 5.2 %collective-permute-done.16.rest_7_ = bf16[64,2048]{1,0:T(8,128)(2,1)S(1)} collective-permute-done((bf16[64,2048]{1,0:T(8,128)(2,1)S(1)}, bf16[64,2048]{1,0:T(8,128)(2,1)S(1)}, u32[]{:S(2)}, u32[]{:S(2)}) %collective-permute-start.16) | collective-permute-done | bytes 262176 | tf_op jit(solution)/shard_map/ppermute | solution.py:22
  70.0 3.0 %tables.1 = (bf16[2,384,256]{2,1,0:T(8,128)(2,1)S(1)}, bf16[2,256,384]{2,1,0:T(8,128)(2,1)S(1)}) custom-call(f32[2,16,64]{2,1,0:T(8,128)S(1)} %pad_maximum_fusion.1.rest_0_, f32[2,16,64]{2,1,0:T(8,128)S(1)} %collective-permute-done.1.rest_1_, f32[2,16,64]{2,1,0:T(8,128)S(1)} %collective-permute-done.2.rest_2_, f32[2,16,64]{2,1,0:T(8,128)S(1)} %collective-permute-done.3.rest_3_), custom_call_target="tpu_custom_call" | custom-call | tf_op jit(solution)/shard_map/tables/pallas_call | solution.py:309
  75.7 19.5 %experts_first.1 = (bf16[4,192,512]{2,1,0:T(8,128)(2,1)}, bf16[256,1024]{1,0:T(8,128)(2,1)}, bf16[256,1024]{1,0:T(8,128)(2,1)}, bf16[256,1024]{1,0:T(8,128)(2,1)}, bf16[256,1024]{1,0:T(8,128)(2,1)}) custom-call(bf16[2,384,256]{2,1,0:T(8,128)(2,1)} %copy-done.1, bf16[2,256,384]{2,1,0:T(8,128)(2,1)} %copy-done, bf16[64,2048]{1,0:T(8,128)(2,1)} %copy-done.2, ...), custom_call_target="tpu_custom_call" | custom-call | tf_op jit(solution)/shard_map/experts_first/pallas_call | solution.py:380
  95.2 7.6 %experts_later.1 = (bf16[256,768]{1,0:T(8,128)(2,1)}, bf16[256,768]{1,0:T(8,128)(2,1)}, bf16[256,768]{1,0:T(8,128)(2,1)}, bf16[256,768]{1,0:T(8,128)(2,1)}, bf16...) custom-call(bf16[2,256,384]{2,1,0:T(8,128)(2,1)} %copy-done, ...), custom_call_target="tpu_custom_call" | custom-call | flops 3221225472 | bytes 8388608 | tf_op jit(solution)/shard_map/experts_later/pallas_call | solution.py:397
  103.5 1.1 collective-permute-done.36
  106.8 4.6 %collective-permute-done.37 = bf16[256,256]{1,0:T(8,128)(2,1)S(1)} collective-permute-done((bf16[256,256]{1,0:T(8,128)(2,1)S(1)}, bf16[256,256]{1,0:T(8,128)(2,1)S(1)}, u32[]{:S(2)}, u32[]{:S(2)}) %collective-permute-start.37) | collective-permute-done | bytes 131104 | tf_op jit(solution)/shard_map/ppermute | solution.py:22
  112.5 2.7 %collective-permute-start.39 = (bf16[64,256]{1,0:T(8,128)(2,1)S(1)}, bf16[64,256]{1,0:T(8,128)(2,1)S(1)}, u32[]{:S(2)}, u32[]{:S(2)}) collective-permute-start(bf16[64,256]{1,0:T(8,128)(2,1)S(1)} %get-tuple-element.51), channel_id=1, source_target_pairs={{8,0},{12,4},{0,8},{4,12},{9,1},{13,5},{1,9},{5,13},{10,2},{14,6},... | collective-permute-start | bytes 98312 | tf_op jit(solution)/shard_map/ppermute | solution.py:27
  115.2 1.7 %collective-permute-start.40 = (bf16[64,256]{1,0:T(8,128)(2,1)S(1)}, bf16[64,256]{1,0:T(8,128)(2,1)S(1)}, u32[]{:S(2)}, u32[]{:S(2)}) collective-permute-start(bf16[64,256]{1,0:T(8,128)(2,1)S(1)} %get-tuple-element.50), channel_id=1, source_target_pairs={{12,0},{8,4},{4,8},{0,12},{13,1},{9,5},{5,9},{1,13},{14,2},{10,6},... | collective-permute-start | bytes 98312 | tf_op jit(solution)/shard_map/ppermute | solution.py:27
  118.9 1.6 %collective-permute-start.27 = (bf16[256,1024]{1,0:T(8,128)(2,1)S(1)}, bf16[256,1024]{1,0:T(8,128)(2,1)S(1)}, u32[]{:S(2)}, u32[]{:S(2)}) collective-permute-start(bf16[256,1024]{1,0:T(8,128)(2,1)S(1)} %add_convert_fusion), channel_id=1, source_target_pairs={{2,0},{0,2},{3,1},{1,3},{6,4},{4,6},{7,5},{5,7},{10,8},{8,10},{11,... | collective-permute-start | bytes 1572872 | tf_op jit(solution)/shard_map/ppermute | solution.py:22
  120.9 9.1 %collective-permute-done.32 = bf16[256,768]{1,0:T(8,128)(2,1)S(1)} collective-permute-done((bf16[256,768]{1,0:T(8,128)(2,1)S(1)}, bf16[256,768]{1,0:T(8,128)(2,1)S(1)}, u32[]{:S(2)}, u32[]{:S(2)}) %collective-permute-start.32) | collective-permute-done | bytes 393248 | tf_op jit(solution)/shard_map/ppermute | solution.py:22
  130.0 1.1 convert_add_fusion.1
  131.2 7.7 %collective-permute-done.27 = bf16[256,1024]{1,0:T(8,128)(2,1)S(1)} collective-permute-done((bf16[256,1024]{1,0:T(8,128)(2,1)S(1)}, bf16[256,1024]{1,0:T(8,128)(2,1)S(1)}, u32[]{:S(2)}, u32[]{:S(2)}) %collective-permute-start.27) | collective-permute-done | bytes 524320 | tf_op jit(solution)/shard_map/ppermute | solution.py:22
  139.4 2.7 %collective-permute-start.34 = (bf16[1,64,768]{2,1,0:T(8,128)(2,1)S(1)}, bf16[1,64,768]{2,1,0:T(8,128)(2,1)S(1)}, u32[]{:S(2)}, u32[]{:S(2)}) collective-permute-start(bf16[1,64,768]{2,1,0:T(8,128)(2,1)S(1)} %fusion.16), channel_id=1, source_target_pairs={{8,0},{12,4},{0,8},{4,12},{9,1},{13,5},{1,9},{5,13},{10,2},{14,6},... | collective-permute-start | bytes 294920 | tf_op jit(solution)/shard_map/ppermute | solution.py:27
  142.1 5.3 %collective-permute-done.28 = bf16[2,64,1024]{2,1,0:T(8,128)(2,1)S(1)} collective-permute-done((bf16[2,64,1024]{2,1,0:T(8,128)(2,1)S(1)}, bf16[2,64,1024]{2,1,0:T(8,128)(2,1)S(1)}, u32[]{:S(2)}, u32[]{:S(2)}) %collective-permute-start.28) | collective-permute-done | bytes 262176 | tf_op jit(solution)/shard_map/ppermute | solution.py:27
  147.9 6.2 %collective-permute-done.29 = bf16[1,64,1024]{2,1,0:T(8,128)(2,1)S(1)} collective-permute-done((bf16[1,64,1024]{2,1,0:T(8,128)(2,1)S(1)}, bf16[1,64,1024]{2,1,0:T(8,128)(2,1)S(1)}, u32[]{:S(2)}, u32[]{:S(2)}) %collective-permute-start.29) | collective-permute-done | bytes 131104 | tf_op jit(solution)/shard_map/ppermute | solution.py:27
  (125 shorter events, 16.5 us)
Async XLA Ops:
  8.4 9.5 %collective-permute-start.6 = (bf16[64,2048]{1,0:T(8,128)(2,1)S(1)}, bf16[64,2048]{1,0:T(8,128)(2,1)S(1)}, u32[]{:S(2)}, u32[]{:S(2)}) collective-permute-start(bf16[64,2048]{1,0:T(8,128)(2,1)S(1)} %get-tuple-element.33), channel_id=1, source_target_pairs={{2,0},{0,2},{3,1},{1,3},{6,4},{4,6},{7,5},{5,7},{10,8},{8,10},{11,... | collective-permute-start | bytes 786440 | tf_op jit(solution)/shard_map/ppermute | solution.py:22
  19.4 8.5 %collective-permute-start.8 = (bf16[64,2048]{1,0:T(8,128)(2,1)S(1)}, bf16[64,2048]{1,0:T(8,128)(2,1)S(1)}, u32[]{:S(2)}, u32[]{:S(2)}) collective-permute-start(bf16[64,2048]{1,0:T(8,128)(2,1)S(1)} %fusion.2.rest_0_), channel_id=1, source_target_pairs={{4,0},{0,4},{12,8},{8,12},{5,1},{1,5},{13,9},{9,13},{6,2},{2,6},{1... | collective-permute-start | bytes 786440 | tf_op jit(solution)/shard_map/ppermute | solution.py:27
  21.3 7.3 %collective-permute-start.9 = (bf16[64,2048]{1,0:T(8,128)(2,1)S(1)}, bf16[64,2048]{1,0:T(8,128)(2,1)S(1)}, u32[]{:S(2)}, u32[]{:S(2)}) collective-permute-start(bf16[64,2048]{1,0:T(8,128)(2,1)S(1)} %fusion.2.rest_0_), channel_id=1, source_target_pairs={{4,8},{8,4},{5,9},{9,5},{6,10},{10,6},{7,11},{11,7},{20,24},{24,20... | collective-permute-start | bytes 786440 | tf_op jit(solution)/shard_map/ppermute | solution.py:345
  28.0 11.1 %collective-permute-start.11 = (bf16[64,2048]{1,0:T(8,128)(2,1)S(1)}, bf16[64,2048]{1,0:T(8,128)(2,1)S(1)}, u32[]{:S(2)}, u32[]{:S(2)}) collective-permute-start(bf16[64,2048]{1,0:T(8,128)(2,1)S(1)} %collective-permute-done.8.rest_1_), channel_id=1, source_target_pairs={{4,8},{8,4},{5,9},{9,5},{6,10},{10,6},{7,11},{11,7},{20,24},{24,20... | collective-permute-start | bytes 786440 | tf_op jit(solution)/shard_map/ppermute | solution.py:346
  28.6 11.9 %collective-permute-start.10 = (bf16[64,2048]{1,0:T(8,128)(2,1)S(1)}, bf16[64,2048]{1,0:T(8,128)(2,1)S(1)}, u32[]{:S(2)}, u32[]{:S(2)}) collective-permute-start(bf16[64,2048]{1,0:T(8,128)(2,1)S(1)} %collective-permute-done.9), channel_id=1, source_target_pairs={{4,0},{8,12},{5,1},{9,13},{6,2},{10,14},{7,3},{11,15},{20,16},{24,... | collective-permute-start | bytes 786440 | tf_op jit(solution)/shard_map/ppermute | solution.py:347
  32.1 17.9 %collective-permute-start.1 = (f32[2,16,64]{2,1,0:T(8,128)S(1)}, f32[2,16,64]{2,1,0:T(8,128)S(1)}, u32[]{:S(2)}, u32[]{:S(2)}) collective-permute-start(f32[2,16,64]{2,1,0:T(8,128)S(1)} %pad_maximum_fusion.1.rest_0_), channel_id=1, source_target_pairs={{4,0},{0,4},{12,8},{8,12},{5,1},{1,5},{13,9},{9,13},{6,2},{2,6},{1... | collective-permute-start | bytes 24584 | tf_op jit(solution)/shard_map/ppermute | solution.py:27
  36.7 13.9 %collective-permute-start.2 = (f32[2,16,64]{2,1,0:T(8,128)S(1)}, f32[2,16,64]{2,1,0:T(8,128)S(1)}, u32[]{:S(2)}, u32[]{:S(2)}) collective-permute-start(f32[2,16,64]{2,1,0:T(8,128)S(1)} %pad_maximum_fusion.1.rest_0_), channel_id=1, source_target_pairs={{8,0},{12,4},{0,8},{4,12},{9,1},{13,5},{1,9},{5,13},{10,2},{14,6},... | collective-permute-start | bytes 24584 | tf_op jit(solution)/shard_map/ppermute | solution.py:27
  37.3 13.8 %collective-permute-start.3 = (f32[2,16,64]{2,1,0:T(8,128)S(1)}, f32[2,16,64]{2,1,0:T(8,128)S(1)}, u32[]{:S(2)}, u32[]{:S(2)}) collective-permute-start(f32[2,16,64]{2,1,0:T(8,128)S(1)} %pad_maximum_fusion.1.rest_0_), channel_id=1, source_target_pairs={{12,0},{8,4},{4,8},{0,12},{13,1},{9,5},{5,9},{1,13},{14,2},{10,6},... | collective-permute-start | bytes 24584 | tf_op jit(solution)/shard_map/ppermute | solution.py:27
  39.0 11.8 %collective-permute-start.13 = (bf16[64,2048]{1,0:T(8,128)(2,1)S(1)}, bf16[64,2048]{1,0:T(8,128)(2,1)S(1)}, u32[]{:S(2)}, u32[]{:S(2)}) collective-permute-start(bf16[64,2048]{1,0:T(8,128)(2,1)S(1)} %fusion.2.rest_0_), channel_id=1, source_target_pairs={{2,0},{0,2},{3,1},{1,3},{6,4},{4,6},{7,5},{5,7},{10,8},{8,10},{11,... | collective-permute-start | bytes 786440 | tf_op jit(solution)/shard_map/ppermute | solution.py:22
  40.5 9.4 %collective-permute-start.12 = (bf16[64,2048]{1,0:T(8,128)(2,1)S(1)}, bf16[64,2048]{1,0:T(8,128)(2,1)S(1)}, u32[]{:S(2)}, u32[]{:S(2)}) collective-permute-start(bf16[64,2048]{1,0:T(8,128)(2,1)S(1)} %collective-permute-done.11), channel_id=1, source_target_pairs={{4,0},{8,12},{5,1},{9,13},{6,2},{10,14},{7,3},{11,15},{20,16},{24,... | collective-permute-start | bytes 786440 | tf_op jit(solution)/shard_map/ppermute | solution.py:348
  50.0 9.2 %collective-permute-start.14 = (bf16[64,2048]{1,0:T(8,128)(2,1)S(1)}, bf16[64,2048]{1,0:T(8,128)(2,1)S(1)}, u32[]{:S(2)}, u32[]{:S(2)}) collective-permute-start(bf16[64,2048]{1,0:T(8,128)(2,1)S(1)} %collective-permute-done.8.rest_1_), channel_id=1, source_target_pairs={{2,0},{0,2},{3,1},{1,3},{6,4},{4,6},{7,5},{5,7},{10,8},{8,10},{11,... | collective-permute-start | bytes 786440 | tf_op jit(solution)/shard_map/ppermute | solution.py:22
  50.6 8.6 %collective-permute-start.18 = (bf16[64,2048]{1,0:T(8,128)(2,1)S(1)}, bf16[64,2048]{1,0:T(8,128)(2,1)S(1)}, u32[]{:S(2)}, u32[]{:S(2)}) collective-permute-start(bf16[64,2048]{1,0:T(8,128)(2,1)S(1)} %collective-permute-done.8.rest_1_), channel_id=1, source_target_pairs={{1,0},{0,1},{3,2},{2,3},{5,4},{4,5},{7,6},{6,7},{9,8},{8,9},{11,10... | collective-permute-start | bytes 786440 | tf_op jit(solution)/shard_map/ppermute | solution.py:22
  50.8 8.9 %collective-permute-start.21 = (bf16[64,2048]{1,0:T(8,128)(2,1)S(1)}, bf16[64,2048]{1,0:T(8,128)(2,1)S(1)}, u32[]{:S(2)}, u32[]{:S(2)}) collective-permute-start(bf16[64,2048]{1,0:T(8,128)(2,1)S(1)} %collective-permute-done.13.rest_4_), channel_id=1, source_target_pairs={{1,0},{0,1},{3,2},{2,3},{5,4},{4,5},{7,6},{6,7},{9,8},{8,9},{11,10... | collective-permute-start | bytes 786440 | tf_op jit(solution)/shard_map/ppermute | solution.py:22
  51.1 13.7 %collective-permute-start.15 = (bf16[64,2048]{1,0:T(8,128)(2,1)S(1)}, bf16[64,2048]{1,0:T(8,128)(2,1)S(1)}, u32[]{:S(2)}, u32[]{:S(2)}) collective-permute-start(bf16[64,2048]{1,0:T(8,128)(2,1)S(1)} %broadcast_select_fusion.1.rest_2_), channel_id=1, source_target_pairs={{2,0},{0,2},{3,1},{1,3},{6,4},{4,6},{7,5},{5,7},{10,8},{8,10},{11,... | collective-permute-start | bytes 786440 | tf_op jit(solution)/shard_map/ppermute | solution.py:22
  52.6 17.4 %collective-permute-start.16 = (bf16[64,2048]{1,0:T(8,128)(2,1)S(1)}, bf16[64,2048]{1,0:T(8,128)(2,1)S(1)}, u32[]{:S(2)}, u32[]{:S(2)}) collective-permute-start(bf16[64,2048]{1,0:T(8,128)(2,1)S(1)} %broadcast_select_fusion.rest_3_), channel_id=1, source_target_pairs={{2,0},{0,2},{3,1},{1,3},{6,4},{4,6},{7,5},{5,7},{10,8},{8,10},{11,... | collective-permute-start | bytes 786440 | tf_op jit(solution)/shard_map/ppermute | solution.py:22
  59.2 15.3 %collective-permute-start.19 = (bf16[64,2048]{1,0:T(8,128)(2,1)S(1)}, bf16[64,2048]{1,0:T(8,128)(2,1)S(1)}, u32[]{:S(2)}, u32[]{:S(2)}) collective-permute-start(bf16[64,2048]{1,0:T(8,128)(2,1)S(1)} %broadcast_select_fusion.1.rest_2_), channel_id=1, source_target_pairs={{1,0},{0,1},{3,2},{2,3},{5,4},{4,5},{7,6},{6,7},{9,8},{8,9},{11,10... | collective-permute-start | bytes 786440 | tf_op jit(solution)/shard_map/ppermute | solution.py:22
  59.3 15.3 %collective-permute-start.22 = (bf16[64,2048]{1,0:T(8,128)(2,1)S(1)}, bf16[64,2048]{1,0:T(8,128)(2,1)S(1)}, u32[]{:S(2)}, u32[]{:S(2)}) collective-permute-start(bf16[64,2048]{1,0:T(8,128)(2,1)S(1)} %collective-permute-done.14.rest_5_), channel_id=1, source_target_pairs={{1,0},{0,1},{3,2},{2,3},{5,4},{4,5},{7,6},{6,7},{9,8},{8,9},{11,10... | collective-permute-start | bytes 786440 | tf_op jit(solution)/shard_map/ppermute | solution.py:22
  59.8 14.8 %collective-permute-start.20 = (bf16[64,2048]{1,0:T(8,128)(2,1)S(1)}, bf16[64,2048]{1,0:T(8,128)(2,1)S(1)}, u32[]{:S(2)}, u32[]{:S(2)}) collective-permute-start(bf16[64,2048]{1,0:T(8,128)(2,1)S(1)} %broadcast_select_fusion.rest_3_), channel_id=1, source_target_pairs={{1,0},{0,1},{3,2},{2,3},{5,4},{4,5},{7,6},{6,7},{9,8},{8,9},{11,10... | collective-permute-start | bytes 786440 | tf_op jit(solution)/shard_map/ppermute | solution.py:22
  64.9 9.8 %collective-permute-start.23 = (bf16[64,2048]{1,0:T(8,128)(2,1)S(1)}, bf16[64,2048]{1,0:T(8,128)(2,1)S(1)}, u32[]{:S(2)}, u32[]{:S(2)}) collective-permute-start(bf16[64,2048]{1,0:T(8,128)(2,1)S(1)} %collective-permute-done.15.rest_6_), channel_id=1, source_target_pairs={{1,0},{0,1},{3,2},{2,3},{5,4},{4,5},{7,6},{6,7},{9,8},{8,9},{11,10... | collective-permute-start | bytes 786440 | tf_op jit(solution)/shard_map/ppermute | solution.py:22
  105.6 5.8 %collective-permute-start.37 = (bf16[256,256]{1,0:T(8,128)(2,1)S(1)}, bf16[256,256]{1,0:T(8,128)(2,1)S(1)}, u32[]{:S(2)}, u32[]{:S(2)}) collective-permute-start(bf16[256,256]{1,0:T(8,128)(2,1)S(1)} %add_convert_fusion.3), channel_id=1, source_target_pairs={{2,0},{0,2},{3,1},{1,3},{6,4},{4,6},{7,5},{5,7},{10,8},{8,10},{11,... | collective-permute-start | bytes 393224 | tf_op jit(solution)/shard_map/ppermute | solution.py:22
  106.2 11.8 %collective-permute-start.26 = (bf16[256,1024]{1,0:T(8,128)(2,1)S(1)}, bf16[256,1024]{1,0:T(8,128)(2,1)S(1)}, u32[]{:S(2)}, u32[]{:S(2)}) collective-permute-start(bf16[256,1024]{1,0:T(8,128)(2,1)S(1)} %copy-done.22), channel_id=1, source_target_pairs={{1,0},{0,1},{3,2},{2,3},{5,4},{4,5},{7,6},{6,7},{9,8},{8,9},{11,10... | collective-permute-start | bytes 1572872 | tf_op jit(solution)/shard_map/ppermute | solution.py:22
  106.3 8.9 %collective-permute-start.31 = (bf16[256,768]{1,0:T(8,128)(2,1)}, bf16[256,768]{1,0:T(8,128)(2,1)S(1)}, u32[]{:S(2)}, u32[]{:S(2)}) collective-permute-start(bf16[256,768]{1,0:T(8,128)(2,1)} %get-tuple-element.42), channel_id=1, source_target_pairs={{1,0},{0,1},{3,2},{2,3},{5,4},{4,5},{7,6},{6,7},{9,8},{8,9},{11,10... | collective-permute-start | bytes 1179656 | tf_op jit(solution)/shard_map/ppermute | solution.py:22
  106.7 14.2 %collective-permute-start.30 = (bf16[256,768]{1,0:T(8,128)(2,1)}, bf16[256,768]{1,0:T(8,128)(2,1)S(1)}, u32[]{:S(2)}, u32[]{:S(2)}) collective-permute-start(bf16[256,768]{1,0:T(8,128)(2,1)} %get-tuple-element.40), channel_id=1, source_target_pairs={{1,0},{0,1},{3,2},{2,3},{5,4},{4,5},{7,6},{6,7},{9,8},{8,9},{11,10... | collective-permute-start | bytes 1179656 | tf_op jit(solution)/shard_map/ppermute | solution.py:22
  112.4 6.4 %collective-permute-start.38 = (bf16[64,256]{1,0:T(8,128)(2,1)S(1)}, bf16[64,256]{1,0:T(8,128)(2,1)S(1)}, u32[]{:S(2)}, u32[]{:S(2)}) collective-permute-start(bf16[64,256]{1,0:T(8,128)(2,1)S(1)} %get-tuple-element.49), channel_id=1, source_target_pairs={{4,0},{0,4},{12,8},{8,12},{5,1},{1,5},{13,9},{9,13},{6,2},{2,6},{1... | collective-permute-start | bytes 98312 | tf_op jit(solution)/shard_map/ppermute | solution.py:27
  112.5 6.4 %collective-permute-start.39 = (bf16[64,256]{1,0:T(8,128)(2,1)S(1)}, bf16[64,256]{1,0:T(8,128)(2,1)S(1)}, u32[]{:S(2)}, u32[]{:S(2)}) collective-permute-start(bf16[64,256]{1,0:T(8,128)(2,1)S(1)} %get-tuple-element.51), channel_id=1, source_target_pairs={{8,0},{12,4},{0,8},{4,12},{9,1},{13,5},{1,9},{5,13},{10,2},{14,6},... | collective-permute-start | bytes 98312 | tf_op jit(solution)/shard_map/ppermute | solution.py:27
  118.0 12.1 %collective-permute-start.32 = (bf16[256,768]{1,0:T(8,128)(2,1)S(1)}, bf16[256,768]{1,0:T(8,128)(2,1)S(1)}, u32[]{:S(2)}, u32[]{:S(2)}) collective-permute-start(bf16[256,768]{1,0:T(8,128)(2,1)S(1)} %add_convert_fusion.1), channel_id=1, source_target_pairs={{2,0},{0,2},{3,1},{1,3},{6,4},{4,6},{7,5},{5,7},{10,8},{8,10},{11,... | collective-permute-start | bytes 1179656 | tf_op jit(solution)/shard_map/ppermute | solution.py:22
  118.8 12.5 %collective-permute-start.25 = (bf16[256,1024]{1,0:T(8,128)(2,1)S(1)}, bf16[256,1024]{1,0:T(8,128)(2,1)S(1)}, u32[]{:S(2)}, u32[]{:S(2)}) collective-permute-start(bf16[256,1024]{1,0:T(8,128)(2,1)S(1)} %copy-done.21), channel_id=1, source_target_pairs={{1,0},{0,1},{3,2},{2,3},{5,4},{4,5},{7,6},{6,7},{9,8},{8,9},{11,10... | collective-permute-start | bytes 1572872 | tf_op jit(solution)/shard_map/ppermute | solution.py:22
  118.9 20.1 %collective-permute-start.27 = (bf16[256,1024]{1,0:T(8,128)(2,1)S(1)}, bf16[256,1024]{1,0:T(8,128)(2,1)S(1)}, u32[]{:S(2)}, u32[]{:S(2)}) collective-permute-start(bf16[256,1024]{1,0:T(8,128)(2,1)S(1)} %add_convert_fusion), channel_id=1, source_target_pairs={{2,0},{0,2},{3,1},{1,3},{6,4},{4,6},{7,5},{5,7},{10,8},{8,10},{11,... | collective-permute-start | bytes 1572872 | tf_op jit(solution)/shard_map/ppermute | solution.py:22
  131.2 8.2 %collective-permute-start.33 = (bf16[2,64,768]{2,1,0:T(8,128)(2,1)S(1)}, bf16[2,64,768]{2,1,0:T(8,128)(2,1)S(1)}, u32[]{:S(2)}, u32[]{:S(2)}) collective-permute-start(bf16[2,64,768]{2,1,0:T(8,128)(2,1)S(1)} %fusion.10), channel_id=1, source_target_pairs={{4,0},{0,4},{12,8},{8,12},{5,1},{1,5},{13,9},{9,13},{6,2},{2,6},{1... | collective-permute-start | bytes 589832 | tf_op jit(solution)/shard_map/ppermute | solution.py:27
  139.2 8.2 %collective-permute-start.28 = (bf16[2,64,1024]{2,1,0:T(8,128)(2,1)S(1)}, bf16[2,64,1024]{2,1,0:T(8,128)(2,1)S(1)}, u32[]{:S(2)}, u32[]{:S(2)}) collective-permute-start(bf16[2,64,1024]{2,1,0:T(8,128)(2,1)S(1)} %fusion.7), channel_id=1, source_target_pairs={{4,0},{0,4},{12,8},{8,12},{5,1},{1,5},{13,9},{9,13},{6,2},{2,6},{1... | collective-permute-start | bytes 786440 | tf_op jit(solution)/shard_map/ppermute | solution.py:27
  139.4 8.4 %collective-permute-start.34 = (bf16[1,64,768]{2,1,0:T(8,128)(2,1)S(1)}, bf16[1,64,768]{2,1,0:T(8,128)(2,1)S(1)}, u32[]{:S(2)}, u32[]{:S(2)}) collective-permute-start(bf16[1,64,768]{2,1,0:T(8,128)(2,1)S(1)} %fusion.16), channel_id=1, source_target_pairs={{8,0},{12,4},{0,8},{4,12},{9,1},{13,5},{1,9},{5,13},{10,2},{14,6},... | collective-permute-start | bytes 294920 | tf_op jit(solution)/shard_map/ppermute | solution.py:27
  147.5 6.6 %collective-permute-start.29 = (bf16[1,64,1024]{2,1,0:T(8,128)(2,1)S(1)}, bf16[1,64,1024]{2,1,0:T(8,128)(2,1)S(1)}, u32[]{:S(2)}, u32[]{:S(2)}) collective-permute-start(bf16[1,64,1024]{2,1,0:T(8,128)(2,1)S(1)} %fusion.14), channel_id=1, source_target_pairs={{8,0},{12,4},{0,8},{4,12},{9,1},{13,5},{1,9},{5,13},{10,2},{14,6},... | collective-permute-start | bytes 393224 | tf_op jit(solution)/shard_map/ppermute | solution.py:27
  (32 other events, 422.4 us)

commit v7 on v6

--- a/solution.py
+++ b/solution.py
@@ -40,13 +40,7 @@
 PARAMS = pltpu.CompilerParams(vmem_limit_bytes=60 * 1024 * 1024)
 
 
-def codes_kernel(experts, count, ids_ref, weights_ref, *rest):
-    far, out_ref, near, sem_ref = rest[:count], rest[count], rest[count + 1 : -1], rest[-1]
-    copies = [
-        pltpu.make_async_copy(src, dst, sem_ref.at[n]) for n, (src, dst) in enumerate(zip(far, near))
-    ]
-    for copy in copies:
-        copy.start()
+def codes_kernel(experts, ids_ref, weights_ref, out_ref):
     choices, rows = ids_ref.shape
     ids = ids_ref[...].astype(F32).T.astype(jnp.int32)
     lanes = lax.broadcasted_iota(jnp.int32, (rows, experts), 1)
@@ -62,8 +56,6 @@
     codes = jnp.concatenate(slot, axis=1) + ids.astype(F32) * SLOT
     out_ref[:choices] = codes.T
     out_ref[choices:] = weights_ref[...]
-    for copy in copies:
-        copy.wait()
 
 
 def tables_kernel(choices, *rest):
@@ -100,17 +92,6 @@
         back_ref[i] = total.astype(BF16)
 
 
-def project_kernel(attn_ref, attn_got_ref, res_ref, res_got_ref, weight_ref, kept_ref, sent_ref):
-    same = lax.axis_index("tensor") == lax.axis_index("dp")
-    weight = weight_ref[...]
-    own = jnp.dot(attn_ref[...], weight, preferred_element_type=F32)
-    other = jnp.dot(attn_got_ref[...], weight, preferred_element_type=F32)
-    own_sum = own + res_ref[...].astype(F32)
-    other_sum = other + res_got_ref[...].astype(F32)
-    kept_ref[...] = jnp.where(same, own_sum, other)
-    sent_ref[...] = jnp.where(same, other_sum, own).astype(BF16)
-
-
 def down_copies(wd_ref, wds_ref, sem_ref, first):
     tensors, held, _, span = wds_ref.shape
     x = lax.axis_index("tensor")
@@ -240,54 +221,26 @@
     cols_out = width // tensors
     choices = expert_ids.shape[1]
 
-    far = [o_weight, attn, residual] if cores == 2 and sub == 1 else []
-    route, *near = pl.pallas_call(
-        functools.partial(codes_kernel, experts, len(far)),
-        out_shape=[jax.ShapeDtypeStruct((2 * choices, rows), F32)]
-        + [pltpu.VMEM(v.shape, v.dtype) for v in far],
-        in_specs=[VMEM, VMEM] + [HBM] * len(far),
-        out_specs=[VMEM] * (1 + len(far)),
-        scratch_shapes=[pltpu.SemaphoreType.DMA((len(far) + 1,))],
-        compiler_params=pltpu.CompilerParams(vmem_limit_bytes=50 * 1024 * 1024),
-        name="codes",
-    )(expert_ids.T, route_weights.T, *far)
+    attn_all = jnp.concatenate([fetch(attn, "dp", i) for i in range(cores)], axis=0)
+    res_all = jnp.concatenate([fetch(residual, "dp", i) for i in range(cores)], axis=0)
+    partial = jnp.dot(attn_all, o_weight, preferred_element_type=F32)
+    res_here = jnp.where(x // sub == d, res_all.astype(F32), 0.0)
+    if sub == 1:
+        partial = partial + res_here
+    else:
+        at = (x % sub) * cols_out
+        partial = lax.dynamic_update_slice_in_dim(
+            partial, lax.dynamic_slice_in_dim(partial, at, cols_out, 1) + res_here, at, 1
+        )
+    parts = partial.reshape(tensors, part, cols_core)
 
     def place(p):
         return ((p // sub - d) % cores) * sub + p % sub
 
-    if cores == 2 and sub == 1:
-        attn_got = fetch(attn, "dp", 1)
-        res_got = fetch(residual, "dp", 1)
-        hidden, sent = pl.pallas_call(
-            project_kernel,
-            out_shape=[
-                jax.ShapeDtypeStruct((part, cols_core), F32),
-                jax.ShapeDtypeStruct((part, cols_core), BF16),
-            ],
-            in_specs=[VMEM] * 5,
-            out_specs=[VMEM] * 2,
-            compiler_params=pltpu.CompilerParams(vmem_limit_bytes=24 * 1024 * 1024),
-            name="project",
-        )(near[1], attn_got, near[2], res_got, near[0])
-        hidden = hidden + fetch(sent, "tensor", 1).astype(F32)
-    else:
-        attn_all = jnp.concatenate([fetch(attn, "dp", i) for i in range(cores)], axis=0)
-        res_all = jnp.concatenate([fetch(residual, "dp", i) for i in range(cores)], axis=0)
-        partial = jnp.dot(attn_all, o_weight, preferred_element_type=F32)
-        res_here = jnp.where(x // sub == d, res_all.astype(F32), 0.0)
-        if sub == 1:
-            partial = partial + res_here
-        else:
-            at = (x % sub) * cols_out
-            partial = lax.dynamic_update_slice_in_dim(
-                partial, lax.dynamic_slice_in_dim(partial, at, cols_out, 1) + res_here, at, 1
-            )
-        parts = partial.reshape(tensors, part, cols_core)
-
-        hidden = pick(parts, place(x))
-        for k in range(1, tensors):
-            sent = pick(parts, place((x - k) % tensors)).astype(BF16)
-            hidden = hidden + fetch(sent, "tensor", k).astype(F32)
+    hidden = pick(parts, place(x))
+    for k in range(1, tensors):
+        sent = pick(parts, place((x - k) % tensors)).astype(BF16)
+        hidden = hidden + fetch(sent, "tensor", k).astype(F32)
     hidden = hidden.astype(BF16).astype(F32)
     squares = jnp.sum(hidden * hidden, axis=1, keepdims=True)
     total = squares
@@ -297,6 +250,14 @@
     gain = lax.dynamic_slice_in_dim(norm_gain, d * cols_core, cols_core, 0)
     normed = (hidden * inverse * gain.astype(F32)[None, :]).astype(BF16)
 
+    route = pl.pallas_call(
+        functools.partial(codes_kernel, experts),
+        out_shape=jax.ShapeDtypeStruct((2 * choices, rows), F32),
+        in_specs=[VMEM, VMEM],
+        out_specs=VMEM,
+        compiler_params=SMALL,
+        name="codes",
+    )(expert_ids.T, route_weights.T)
     route = jnp.stack([fetch(route, "dp", i) for i in range(cores)])
     routes = [route]
     for o in range(1, depth):

time: 155 us -> 154 us (level)
  Pallas kernels: 37.9 us -> 30.7 us
  matrix products: 0 us -> 4.71 us
    pallas_call x2 -> x1, Pallas kernels: 7.78 us -> 0.57 us  [on_device(): pl.pallas_call(functools.partial(codes_kernel, experts), out_shape=jax.Sh...]
    ppermute x26, waiting for transfers between devices: 47.8 us -> 54 us  [fetch(): lax.ppermute(value, axis, [((i + step) % size, i) for i in range(size)])]
    ppermute x1, waiting for transfers between devices: 7.9 us -> 3.09 us  [on_device(): outward_3 = lax.ppermute(middle_2, 'expert', outward)]
    dot_general x0 -> x1, matrix products: none -> 4.71 us  [on_device(): partial = jnp.dot(attn_all, o_weight, preferred_element_type=F32)]
    ppermute x11, starting transfers between devices: 16.4 us -> 18.4 us  [across(): return lax.ppermute(value, axis, [(i ^ flip, i) for i in range(size)])]
  transfers between devices with their start and end apart: 41 -> 41, of which waited for: 15 -> 18; matrix products, arithmetic and copies ran while one was open for 4% -> 3% of each run, Pallas kernels for 5% -> 2%
where the time goes in v7:
time: 154 us
  waiting for transfers between devices  74.9 us (49%)
  starting transfers between devices  34.6 us (22%)
  Pallas kernels  30.7 us (20%)
  other arithmetic  5.84 us (4%)
  matrix products  4.71 us (3%)
  local copies, waits for them, and re-layouts  2.66 us (2%)
    ppermute x26, waiting for transfers between devices, fetch(): lax.ppermute(value, axis, [((i + step) % size, i) for i in range(size)])  54 us
    pallas_call x1, Pallas kernels, on_device(): pl.pallas_call(functools.partial(first_kernel, (cores, tensors, lengths,...  19.5 us
    ppermute x11, starting transfers between devices, across(): return lax.ppermute(value, axis, [(i ^ flip, i) for i in range(size)])  18.4 us
    ppermute x11, waiting for transfers between devices, across(): return lax.ppermute(value, axis, [(i ^ flip, i) for i in range(size)])  17.7 us
    ppermute x26, starting transfers between devices, fetch(): lax.ppermute(value, axis, [((i + step) % size, i) for i in range(size)])  12.2 us
    pallas_call x1, Pallas kernels, on_device(): pl.pallas_call(functools.partial(later_kernel, (cores, tensors, groups, s...  7.63 us
    dot_general x1, matrix products, on_device(): partial = jnp.dot(attn_all, o_weight, preferred_element_type=F32)  4.71 us
    ppermute x1, waiting for transfers between devices, on_device(): outward_3 = lax.ppermute(middle_2, 'expert', outward)  3.09 us
  transfers between devices with their start and end apart: 41, of which 18 were waited for; matrix products, arithmetic and copies ran while one was open for 3% of the time, Pallas kernels for 2%

profile of v7, /device:TPU:0, one launch (start us, length us, event | category | flops | bytes accessed | tf_op | source)
XLA Modules:
  0.0 153.9 jit_solution(12200107810431874671)
XLA Ops:
  0.6 1.3 collective-permute-done.4
  2.2 4.7 %convolution_add_fusion = f32[128,2048]{1,0:T(8,128)S(1)} fusion(bf16[2048,2048]{1,0:T(8,128)(2,1)} %param.10, bf16[64,2048]{1,0:T(8,128)(2,1)S(1)} %collective-permute-done.4, bf16[64,2048]{1,0:T(8,128)(2,1)} %param.9, bf16[64,2048]{1,0:T(8,128)(2,1)S(1)} %collective-permute-done.5, bf16[64,2048]{1,0:T(8,128)(2,1)} %param.11, pred[]{:T(512)S(6)} %eq.15), kind=kOutput, calls=%fused_computation | convolution fusion | flops 1076363264 | bytes 10485761 | tf_op jit(solution)/shard_map/dot_general | solution.py:226
  7.0 2.9 %collective-permute-start.6 = (bf16[64,2048]{1,0:T(8,128)(2,1)S(1)}, bf16[64,2048]{1,0:T(8,128)(2,1)S(1)}, u32[]{:S(2)}, u32[]{:S(2)}) collective-permute-start(bf16[64,2048]{1,0:T(8,128)(2,1)S(1)} %fusion.11), channel_id=1, source_target_pairs={{2,0},{0,2},{3,1},{1,3},{6,4},{4,6},{7,5},{5,7},{10,8},{8,10},{11,... | collective-permute-start | bytes 786440 | tf_op jit(solution)/shard_map/ppermute | solution.py:22
  9.9 6.6 %collective-permute-done.6 = bf16[64,2048]{1,0:T(8,128)(2,1)S(1)} collective-permute-done((bf16[64,2048]{1,0:T(8,128)(2,1)S(1)}, bf16[64,2048]{1,0:T(8,128)(2,1)S(1)}, u32[]{:S(2)}, u32[]{:S(2)}) %collective-permute-start.6) | collective-permute-done | bytes 262176 | tf_op jit(solution)/shard_map/ppermute | solution.py:22
  18.8 4.7 %collective-permute-start.8 = (bf16[64,2048]{1,0:T(8,128)(2,1)S(1)}, bf16[64,2048]{1,0:T(8,128)(2,1)S(1)}, u32[]{:S(2)}, u32[]{:S(2)}) collective-permute-start(bf16[64,2048]{1,0:T(8,128)(2,1)S(1)} %fusion.2.rest_0_), channel_id=1, source_target_pairs={{4,0},{0,4},{12,8},{8,12},{5,1},{1,5},{13,9},{9,13},{6,2},{2,6},{1... | collective-permute-start | bytes 786440 | tf_op jit(solution)/shard_map/ppermute | solution.py:27
  23.5 1.3 collective-permute-start.10
  24.8 5.1 %collective-permute-done.8.rest_1_ = bf16[64,2048]{1,0:T(8,128)(2,1)S(1)} collective-permute-done((bf16[64,2048]{1,0:T(8,128)(2,1)S(1)}, bf16[64,2048]{1,0:T(8,128)(2,1)S(1)}, u32[]{:S(2)}, u32[]{:S(2)}) %collective-permute-start.8) | collective-permute-done | bytes 262176 | tf_op jit(solution)/shard_map/ppermute | solution.py:27
  31.1 1.1 collective-permute-done
  32.3 1.4 collective-permute-start.3
  33.7 4.6 %collective-permute-start.2 = (f32[2,16,64]{2,1,0:T(8,128)S(1)}, f32[2,16,64]{2,1,0:T(8,128)S(1)}, u32[]{:S(2)}, u32[]{:S(2)}) collective-permute-start(f32[2,16,64]{2,1,0:T(8,128)S(1)} %pad_maximum_fusion.1.rest_0_), channel_id=1, source_target_pairs={{8,0},{12,4},{0,8},{4,12},{9,1},{13,5},{1,9},{5,13},{10,2},{14,6},... | collective-permute-start | bytes 24584 | tf_op jit(solution)/shard_map/ppermute | solution.py:27
  38.3 1.5 collective-permute-start.13
  39.8 1.5 collective-permute-start.12
  41.3 4.8 %collective-permute-done.13.rest_4_ = bf16[64,2048]{1,0:T(8,128)(2,1)S(1)} collective-permute-done((bf16[64,2048]{1,0:T(8,128)(2,1)S(1)}, bf16[64,2048]{1,0:T(8,128)(2,1)S(1)}, u32[]{:S(2)}, u32[]{:S(2)}) %collective-permute-start.13) | collective-permute-done | bytes 262176 | tf_op jit(solution)/shard_map/ppermute | solution.py:22
  46.1 3.1 %collective-permute-done.12 = bf16[64,2048]{1,0:T(8,128)(2,1)S(1)} collective-permute-done((bf16[64,2048]{1,0:T(8,128)(2,1)S(1)}, bf16[64,2048]{1,0:T(8,128)(2,1)S(1)}, u32[]{:S(2)}, u32[]{:S(2)}) %collective-permute-start.12) | collective-permute-done | bytes 262176 | tf_op jit(solution)/shard_map/ppermute | solution.py:309
  50.1 1.5 collective-permute-start.15
  52.1 6.4 %collective-permute-done.14.rest_5_ = bf16[64,2048]{1,0:T(8,128)(2,1)S(1)} collective-permute-done((bf16[64,2048]{1,0:T(8,128)(2,1)S(1)}, bf16[64,2048]{1,0:T(8,128)(2,1)S(1)}, u32[]{:S(2)}, u32[]{:S(2)}) %collective-permute-start.14) | collective-permute-done | bytes 262176 | tf_op jit(solution)/shard_map/ppermute | solution.py:22
  59.0 5.1 %collective-permute-done.15.rest_6_ = bf16[64,2048]{1,0:T(8,128)(2,1)S(1)} collective-permute-done((bf16[64,2048]{1,0:T(8,128)(2,1)S(1)}, bf16[64,2048]{1,0:T(8,128)(2,1)S(1)}, u32[]{:S(2)}, u32[]{:S(2)}) %collective-permute-start.15) | collective-permute-done | bytes 262176 | tf_op jit(solution)/shard_map/ppermute | solution.py:22
  64.1 5.2 %collective-permute-done.16.rest_7_ = bf16[64,2048]{1,0:T(8,128)(2,1)S(1)} collective-permute-done((bf16[64,2048]{1,0:T(8,128)(2,1)S(1)}, bf16[64,2048]{1,0:T(8,128)(2,1)S(1)}, u32[]{:S(2)}, u32[]{:S(2)}) %collective-permute-start.16) | collective-permute-done | bytes 262176 | tf_op jit(solution)/shard_map/ppermute | solution.py:22
  69.3 3.0 %tables.1 = (bf16[2,384,256]{2,1,0:T(8,128)(2,1)S(1)}, bf16[2,256,384]{2,1,0:T(8,128)(2,1)S(1)}) custom-call(f32[2,16,64]{2,1,0:T(8,128)S(1)} %pad_maximum_fusion.1.rest_0_, f32[2,16,64]{2,1,0:T(8,128)S(1)} %collective-permute-done.1.rest_1_, f32[2,16,64]{2,1,0:T(8,128)S(1)} %collective-permute-done.2.rest_2_, f32[2,16,64]{2,1,0:T(8,128)S(1)} %collective-permute-done.3.rest_3_), custom_call_target="tpu_custom_call" | custom-call | tf_op jit(solution)/shard_map/tables/pallas_call | solution.py:270
  75.0 19.5 %experts_first.1 = (bf16[4,192,512]{2,1,0:T(8,128)(2,1)}, bf16[256,1024]{1,0:T(8,128)(2,1)}, bf16[256,1024]{1,0:T(8,128)(2,1)}, bf16[256,1024]{1,0:T(8,128)(2,1)}, bf16[256,1024]{1,0:T(8,128)(2,1)}) custom-call(bf16[2,384,256]{2,1,0:T(8,128)(2,1)} %copy-done.1, bf16[2,256,384]{2,1,0:T(8,128)(2,1)} %copy-done, bf16[64,2048]{1,0:T(8,128)(2,1)} %copy-done.4, ...), custom_call_target="tpu_custom_call" | custom-call | tf_op jit(solution)/shard_map/experts_first/pallas_call | solution.py:341
  94.5 7.6 %experts_later.1 = (bf16[256,768]{1,0:T(8,128)(2,1)}, bf16[256,768]{1,0:T(8,128)(2,1)}, bf16[256,768]{1,0:T(8,128)(2,1)}, bf16[256,768]{1,0:T(8,128)(2,1)}, bf16...) custom-call(bf16[2,256,384]{2,1,0:T(8,128)(2,1)} %copy-done, ...), custom_call_target="tpu_custom_call" | custom-call | flops 3221225472 | bytes 8388608 | tf_op jit(solution)/shard_map/experts_later/pallas_call | solution.py:358
  102.7 1.1 collective-permute-done.36
  106.0 4.6 %collective-permute-done.37 = bf16[256,256]{1,0:T(8,128)(2,1)S(1)} collective-permute-done((bf16[256,256]{1,0:T(8,128)(2,1)S(1)}, bf16[256,256]{1,0:T(8,128)(2,1)S(1)}, u32[]{:S(2)}, u32[]{:S(2)}) %collective-permute-start.37) | collective-permute-done | bytes 131104 | tf_op jit(solution)/shard_map/ppermute | solution.py:22
  111.7 1.5 collective-permute-start.40
  113.2 1.9 %collective-permute-start.39 = (bf16[64,256]{1,0:T(8,128)(2,1)S(1)}, bf16[64,256]{1,0:T(8,128)(2,1)S(1)}, u32[]{:S(2)}, u32[]{:S(2)}) collective-permute-start(bf16[64,256]{1,0:T(8,128)(2,1)S(1)} %get-tuple-element.41), channel_id=1, source_target_pairs={{8,0},{12,4},{0,8},{4,12},{9,1},{13,5},{1,9},{5,13},{10,2},{14,6},... | collective-permute-start | bytes 98312 | tf_op jit(solution)/shard_map/ppermute | solution.py:27
  117.5 1.3 collective-permute-start.27
  118.8 9.5 %collective-permute-done.32 = bf16[256,768]{1,0:T(8,128)(2,1)S(1)} collective-permute-done((bf16[256,768]{1,0:T(8,128)(2,1)S(1)}, bf16[256,768]{1,0:T(8,128)(2,1)S(1)}, u32[]{:S(2)}, u32[]{:S(2)}) %collective-permute-start.32) | collective-permute-done | bytes 393248 | tf_op jit(solution)/shard_map/ppermute | solution.py:22
  128.3 1.1 convert_add_fusion.1
  130.5 6.7 %collective-permute-done.27 = bf16[256,1024]{1,0:T(8,128)(2,1)S(1)} collective-permute-done((bf16[256,1024]{1,0:T(8,128)(2,1)S(1)}, bf16[256,1024]{1,0:T(8,128)(2,1)S(1)}, u32[]{:S(2)}, u32[]{:S(2)}) %collective-permute-start.27) | collective-permute-done | bytes 524320 | tf_op jit(solution)/shard_map/ppermute | solution.py:22
  137.6 1.3 collective-permute-start.28
  139.8 6.0 %collective-permute-done.28 = bf16[2,64,1024]{2,1,0:T(8,128)(2,1)S(1)} collective-permute-done((bf16[2,64,1024]{2,1,0:T(8,128)(2,1)S(1)}, bf16[2,64,1024]{2,1,0:T(8,128)(2,1)S(1)}, u32[]{:S(2)}, u32[]{:S(2)}) %collective-permute-start.28) | collective-permute-done | bytes 262176 | tf_op jit(solution)/shard_map/ppermute | solution.py:27
  146.8 6.4 %collective-permute-done.29 = bf16[1,64,1024]{2,1,0:T(8,128)(2,1)S(1)} collective-permute-done((bf16[1,64,1024]{2,1,0:T(8,128)(2,1)S(1)}, bf16[1,64,1024]{2,1,0:T(8,128)(2,1)S(1)}, u32[]{:S(2)}, u32[]{:S(2)}) %collective-permute-start.29) | collective-permute-done | bytes 131104 | tf_op jit(solution)/shard_map/ppermute | solution.py:27
  (130 shorter events, 19.1 us)
Async XLA Ops:
  7.0 9.5 %collective-permute-start.6 = (bf16[64,2048]{1,0:T(8,128)(2,1)S(1)}, bf16[64,2048]{1,0:T(8,128)(2,1)S(1)}, u32[]{:S(2)}, u32[]{:S(2)}) collective-permute-start(bf16[64,2048]{1,0:T(8,128)(2,1)S(1)} %fusion.11), channel_id=1, source_target_pairs={{2,0},{0,2},{3,1},{1,3},{6,4},{4,6},{7,5},{5,7},{10,8},{8,10},{11,... | collective-permute-start | bytes 786440 | tf_op jit(solution)/shard_map/ppermute | solution.py:22
  18.8 11.1 %collective-permute-start.8 = (bf16[64,2048]{1,0:T(8,128)(2,1)S(1)}, bf16[64,2048]{1,0:T(8,128)(2,1)S(1)}, u32[]{:S(2)}, u32[]{:S(2)}) collective-permute-start(bf16[64,2048]{1,0:T(8,128)(2,1)S(1)} %fusion.2.rest_0_), channel_id=1, source_target_pairs={{4,0},{0,4},{12,8},{8,12},{5,1},{1,5},{13,9},{9,13},{6,2},{2,6},{1... | collective-permute-start | bytes 786440 | tf_op jit(solution)/shard_map/ppermute | solution.py:27
  23.5 14.8 %collective-permute-start.10 = (bf16[64,2048]{1,0:T(8,128)(2,1)S(1)}, bf16[64,2048]{1,0:T(8,128)(2,1)S(1)}, u32[]{:S(2)}, u32[]{:S(2)}) collective-permute-start(bf16[64,2048]{1,0:T(8,128)(2,1)S(1)} %collective-permute-done.9), channel_id=1, source_target_pairs={{4,0},{8,12},{5,1},{9,13},{6,2},{10,14},{7,3},{11,15},{20,16},{24,... | collective-permute-start | bytes 786440 | tf_op jit(solution)/shard_map/ppermute | solution.py:308
  29.8 9.9 %collective-permute-start.11 = (bf16[64,2048]{1,0:T(8,128)(2,1)S(1)}, bf16[64,2048]{1,0:T(8,128)(2,1)S(1)}, u32[]{:S(2)}, u32[]{:S(2)}) collective-permute-start(bf16[64,2048]{1,0:T(8,128)(2,1)S(1)} %collective-permute-done.8.rest_1_), channel_id=1, source_target_pairs={{4,8},{8,4},{5,9},{9,5},{6,10},{10,6},{7,11},{11,7},{20,24},{24,20... | collective-permute-start | bytes 786440 | tf_op jit(solution)/shard_map/ppermute | solution.py:307
  32.3 16.9 %collective-permute-start.3 = (f32[2,16,64]{2,1,0:T(8,128)S(1)}, f32[2,16,64]{2,1,0:T(8,128)S(1)}, u32[]{:S(2)}, u32[]{:S(2)}) collective-permute-start(f32[2,16,64]{2,1,0:T(8,128)S(1)} %pad_maximum_fusion.1.rest_0_), channel_id=1, source_target_pairs={{12,0},{8,4},{4,8},{0,12},{13,1},{9,5},{5,9},{1,13},{14,2},{10,6},... | collective-permute-start | bytes 24584 | tf_op jit(solution)/shard_map/ppermute | solution.py:27
  33.7 16.2 %collective-permute-start.2 = (f32[2,16,64]{2,1,0:T(8,128)S(1)}, f32[2,16,64]{2,1,0:T(8,128)S(1)}, u32[]{:S(2)}, u32[]{:S(2)}) collective-permute-start(f32[2,16,64]{2,1,0:T(8,128)S(1)} %pad_maximum_fusion.1.rest_0_), channel_id=1, source_target_pairs={{8,0},{12,4},{0,8},{4,12},{9,1},{13,5},{1,9},{5,13},{10,2},{14,6},... | collective-permute-start | bytes 24584 | tf_op jit(solution)/shard_map/ppermute | solution.py:27
  38.3 11.8 %collective-permute-start.1 = (f32[2,16,64]{2,1,0:T(8,128)S(1)}, f32[2,16,64]{2,1,0:T(8,128)S(1)}, u32[]{:S(2)}, u32[]{:S(2)}) collective-permute-start(f32[2,16,64]{2,1,0:T(8,128)S(1)} %pad_maximum_fusion.1.rest_0_), channel_id=1, source_target_pairs={{4,0},{0,4},{12,8},{8,12},{5,1},{1,5},{13,9},{9,13},{6,2},{2,6},{1... | collective-permute-start | bytes 24584 | tf_op jit(solution)/shard_map/ppermute | solution.py:27
  38.3 7.8 %collective-permute-start.13 = (bf16[64,2048]{1,0:T(8,128)(2,1)S(1)}, bf16[64,2048]{1,0:T(8,128)(2,1)S(1)}, u32[]{:S(2)}, u32[]{:S(2)}) collective-permute-start(bf16[64,2048]{1,0:T(8,128)(2,1)S(1)} %fusion.2.rest_0_), channel_id=1, source_target_pairs={{2,0},{0,2},{3,1},{1,3},{6,4},{4,6},{7,5},{5,7},{10,8},{8,10},{11,... | collective-permute-start | bytes 786440 | tf_op jit(solution)/shard_map/ppermute | solution.py:22
  39.8 9.4 %collective-permute-start.12 = (bf16[64,2048]{1,0:T(8,128)(2,1)S(1)}, bf16[64,2048]{1,0:T(8,128)(2,1)S(1)}, u32[]{:S(2)}, u32[]{:S(2)}) collective-permute-start(bf16[64,2048]{1,0:T(8,128)(2,1)S(1)} %collective-permute-done.11), channel_id=1, source_target_pairs={{4,0},{8,12},{5,1},{9,13},{6,2},{10,14},{7,3},{11,15},{20,16},{24,... | collective-permute-start | bytes 786440 | tf_op jit(solution)/shard_map/ppermute | solution.py:309
  46.1 5.5 %collective-permute-start.17 = (bf16[64,2048]{1,0:T(8,128)(2,1)S(1)}, bf16[64,2048]{1,0:T(8,128)(2,1)S(1)}, u32[]{:S(2)}, u32[]{:S(2)}) collective-permute-start(bf16[64,2048]{1,0:T(8,128)(2,1)S(1)} %fusion.2.rest_0_), channel_id=1, source_target_pairs={{1,0},{0,1},{3,2},{2,3},{5,4},{4,5},{7,6},{6,7},{9,8},{8,9},{11,10... | collective-permute-start | bytes 786440 | tf_op jit(solution)/shard_map/ppermute | solution.py:22
  49.2 9.2 %collective-permute-start.14 = (bf16[64,2048]{1,0:T(8,128)(2,1)S(1)}, bf16[64,2048]{1,0:T(8,128)(2,1)S(1)}, u32[]{:S(2)}, u32[]{:S(2)}) collective-permute-start(bf16[64,2048]{1,0:T(8,128)(2,1)S(1)} %collective-permute-done.8.rest_1_), channel_id=1, source_target_pairs={{2,0},{0,2},{3,1},{1,3},{6,4},{4,6},{7,5},{5,7},{10,8},{8,10},{11,... | collective-permute-start | bytes 786440 | tf_op jit(solution)/shard_map/ppermute | solution.py:22
  49.8 8.7 %collective-permute-start.18 = (bf16[64,2048]{1,0:T(8,128)(2,1)S(1)}, bf16[64,2048]{1,0:T(8,128)(2,1)S(1)}, u32[]{:S(2)}, u32[]{:S(2)}) collective-permute-start(bf16[64,2048]{1,0:T(8,128)(2,1)S(1)} %collective-permute-done.8.rest_1_), channel_id=1, source_target_pairs={{1,0},{0,1},{3,2},{2,3},{5,4},{4,5},{7,6},{6,7},{9,8},{8,9},{11,10... | collective-permute-start | bytes 786440 | tf_op jit(solution)/shard_map/ppermute | solution.py:22
  50.1 14.0 %collective-permute-start.15 = (bf16[64,2048]{1,0:T(8,128)(2,1)S(1)}, bf16[64,2048]{1,0:T(8,128)(2,1)S(1)}, u32[]{:S(2)}, u32[]{:S(2)}) collective-permute-start(bf16[64,2048]{1,0:T(8,128)(2,1)S(1)} %broadcast_select_fusion.1.rest_2_), channel_id=1, source_target_pairs={{2,0},{0,2},{3,1},{1,3},{6,4},{4,6},{7,5},{5,7},{10,8},{8,10},{11,... | collective-permute-start | bytes 786440 | tf_op jit(solution)/shard_map/ppermute | solution.py:22
  51.6 17.7 %collective-permute-start.16 = (bf16[64,2048]{1,0:T(8,128)(2,1)S(1)}, bf16[64,2048]{1,0:T(8,128)(2,1)S(1)}, u32[]{:S(2)}, u32[]{:S(2)}) collective-permute-start(bf16[64,2048]{1,0:T(8,128)(2,1)S(1)} %broadcast_select_fusion.rest_3_), channel_id=1, source_target_pairs={{2,0},{0,2},{3,1},{1,3},{6,4},{4,6},{7,5},{5,7},{10,8},{8,10},{11,... | collective-permute-start | bytes 786440 | tf_op jit(solution)/shard_map/ppermute | solution.py:22
  52.1 21.7 %collective-permute-start.19 = (bf16[64,2048]{1,0:T(8,128)(2,1)S(1)}, bf16[64,2048]{1,0:T(8,128)(2,1)S(1)}, u32[]{:S(2)}, u32[]{:S(2)}) collective-permute-start(bf16[64,2048]{1,0:T(8,128)(2,1)S(1)} %broadcast_select_fusion.1.rest_2_), channel_id=1, source_target_pairs={{1,0},{0,1},{3,2},{2,3},{5,4},{4,5},{7,6},{6,7},{9,8},{8,9},{11,10... | collective-permute-start | bytes 786440 | tf_op jit(solution)/shard_map/ppermute | solution.py:22
  58.5 15.3 %collective-permute-start.22 = (bf16[64,2048]{1,0:T(8,128)(2,1)S(1)}, bf16[64,2048]{1,0:T(8,128)(2,1)S(1)}, u32[]{:S(2)}, u32[]{:S(2)}) collective-permute-start(bf16[64,2048]{1,0:T(8,128)(2,1)S(1)} %collective-permute-done.14.rest_5_), channel_id=1, source_target_pairs={{1,0},{0,1},{3,2},{2,3},{5,4},{4,5},{7,6},{6,7},{9,8},{8,9},{11,10... | collective-permute-start | bytes 786440 | tf_op jit(solution)/shard_map/ppermute | solution.py:22
  58.5 15.3 %collective-permute-start.20 = (bf16[64,2048]{1,0:T(8,128)(2,1)S(1)}, bf16[64,2048]{1,0:T(8,128)(2,1)S(1)}, u32[]{:S(2)}, u32[]{:S(2)}) collective-permute-start(bf16[64,2048]{1,0:T(8,128)(2,1)S(1)} %broadcast_select_fusion.rest_3_), channel_id=1, source_target_pairs={{1,0},{0,1},{3,2},{2,3},{5,4},{4,5},{7,6},{6,7},{9,8},{8,9},{11,10... | collective-permute-start | bytes 786440 | tf_op jit(solution)/shard_map/ppermute | solution.py:22
  64.1 9.7 %collective-permute-start.23 = (bf16[64,2048]{1,0:T(8,128)(2,1)S(1)}, bf16[64,2048]{1,0:T(8,128)(2,1)S(1)}, u32[]{:S(2)}, u32[]{:S(2)}) collective-permute-start(bf16[64,2048]{1,0:T(8,128)(2,1)S(1)} %collective-permute-done.15.rest_6_), channel_id=1, source_target_pairs={{1,0},{0,1},{3,2},{2,3},{5,4},{4,5},{7,6},{6,7},{9,8},{8,9},{11,10... | collective-permute-start | bytes 786440 | tf_op jit(solution)/shard_map/ppermute | solution.py:22
  104.8 5.8 %collective-permute-start.37 = (bf16[256,256]{1,0:T(8,128)(2,1)S(1)}, bf16[256,256]{1,0:T(8,128)(2,1)S(1)}, u32[]{:S(2)}, u32[]{:S(2)}) collective-permute-start(bf16[256,256]{1,0:T(8,128)(2,1)S(1)} %add_convert_fusion.2), channel_id=1, source_target_pairs={{2,0},{0,2},{3,1},{1,3},{6,4},{4,6},{7,5},{5,7},{10,8},{8,10},{11,... | collective-permute-start | bytes 393224 | tf_op jit(solution)/shard_map/ppermute | solution.py:22
  105.4 10.9 %collective-permute-start.26 = (bf16[256,1024]{1,0:T(8,128)(2,1)S(1)}, bf16[256,1024]{1,0:T(8,128)(2,1)S(1)}, u32[]{:S(2)}, u32[]{:S(2)}) collective-permute-start(bf16[256,1024]{1,0:T(8,128)(2,1)S(1)} %copy-done.24), channel_id=1, source_target_pairs={{1,0},{0,1},{3,2},{2,3},{5,4},{4,5},{7,6},{6,7},{9,8},{8,9},{11,10... | collective-permute-start | bytes 1572872 | tf_op jit(solution)/shard_map/ppermute | solution.py:22
  105.5 13.3 %collective-permute-start.30 = (bf16[256,768]{1,0:T(8,128)(2,1)}, bf16[256,768]{1,0:T(8,128)(2,1)S(1)}, u32[]{:S(2)}, u32[]{:S(2)}) collective-permute-start(bf16[256,768]{1,0:T(8,128)(2,1)} %get-tuple-element.28), channel_id=1, source_target_pairs={{1,0},{0,1},{3,2},{2,3},{5,4},{4,5},{7,6},{6,7},{9,8},{8,9},{11,10... | collective-permute-start | bytes 1179656 | tf_op jit(solution)/shard_map/ppermute | solution.py:22
  105.9 7.3 %collective-permute-start.31 = (bf16[256,768]{1,0:T(8,128)(2,1)}, bf16[256,768]{1,0:T(8,128)(2,1)S(1)}, u32[]{:S(2)}, u32[]{:S(2)}) collective-permute-start(bf16[256,768]{1,0:T(8,128)(2,1)} %get-tuple-element.30), channel_id=1, source_target_pairs={{1,0},{0,1},{3,2},{2,3},{5,4},{4,5},{7,6},{6,7},{9,8},{8,9},{11,10... | collective-permute-start | bytes 1179656 | tf_op jit(solution)/shard_map/ppermute | solution.py:22
  111.6 5.5 %collective-permute-start.38 = (bf16[64,256]{1,0:T(8,128)(2,1)S(1)}, bf16[64,256]{1,0:T(8,128)(2,1)S(1)}, u32[]{:S(2)}, u32[]{:S(2)}) collective-permute-start(bf16[64,256]{1,0:T(8,128)(2,1)S(1)} %get-tuple-element.39), channel_id=1, source_target_pairs={{4,0},{0,4},{12,8},{8,12},{5,1},{1,5},{13,9},{9,13},{6,2},{2,6},{1... | collective-permute-start | bytes 98312 | tf_op jit(solution)/shard_map/ppermute | solution.py:27
  111.7 5.8 %collective-permute-start.40 = (bf16[64,256]{1,0:T(8,128)(2,1)S(1)}, bf16[64,256]{1,0:T(8,128)(2,1)S(1)}, u32[]{:S(2)}, u32[]{:S(2)}) collective-permute-start(bf16[64,256]{1,0:T(8,128)(2,1)S(1)} %get-tuple-element.40), channel_id=1, source_target_pairs={{12,0},{8,4},{4,8},{0,12},{13,1},{9,5},{5,9},{1,13},{14,2},{10,6},... | collective-permute-start | bytes 98312 | tf_op jit(solution)/shard_map/ppermute | solution.py:27
  113.2 5.5 %collective-permute-start.39 = (bf16[64,256]{1,0:T(8,128)(2,1)S(1)}, bf16[64,256]{1,0:T(8,128)(2,1)S(1)}, u32[]{:S(2)}, u32[]{:S(2)}) collective-permute-start(bf16[64,256]{1,0:T(8,128)(2,1)S(1)} %get-tuple-element.41), channel_id=1, source_target_pairs={{8,0},{12,4},{0,8},{4,12},{9,1},{13,5},{1,9},{5,13},{10,2},{14,6},... | collective-permute-start | bytes 98312 | tf_op jit(solution)/shard_map/ppermute | solution.py:27
  116.3 12.1 %collective-permute-start.32 = (bf16[256,768]{1,0:T(8,128)(2,1)S(1)}, bf16[256,768]{1,0:T(8,128)(2,1)S(1)}, u32[]{:S(2)}, u32[]{:S(2)}) collective-permute-start(bf16[256,768]{1,0:T(8,128)(2,1)S(1)} %add_convert_fusion.1), channel_id=1, source_target_pairs={{2,0},{0,2},{3,1},{1,3},{6,4},{4,6},{7,5},{5,7},{10,8},{8,10},{11,... | collective-permute-start | bytes 1179656 | tf_op jit(solution)/shard_map/ppermute | solution.py:22
  117.1 13.4 %collective-permute-start.25 = (bf16[256,1024]{1,0:T(8,128)(2,1)S(1)}, bf16[256,1024]{1,0:T(8,128)(2,1)S(1)}, u32[]{:S(2)}, u32[]{:S(2)}) collective-permute-start(bf16[256,1024]{1,0:T(8,128)(2,1)S(1)} %copy-done.23), channel_id=1, source_target_pairs={{1,0},{0,1},{3,2},{2,3},{5,4},{4,5},{7,6},{6,7},{9,8},{8,9},{11,10... | collective-permute-start | bytes 1572872 | tf_op jit(solution)/shard_map/ppermute | solution.py:22
  117.5 19.8 %collective-permute-start.27 = (bf16[256,1024]{1,0:T(8,128)(2,1)S(1)}, bf16[256,1024]{1,0:T(8,128)(2,1)S(1)}, u32[]{:S(2)}, u32[]{:S(2)}) collective-permute-start(bf16[256,1024]{1,0:T(8,128)(2,1)S(1)} %add_convert_fusion), channel_id=1, source_target_pairs={{2,0},{0,2},{3,1},{1,3},{6,4},{4,6},{7,5},{5,7},{10,8},{8,10},{11,... | collective-permute-start | bytes 1572872 | tf_op jit(solution)/shard_map/ppermute | solution.py:22
  129.5 9.4 %collective-permute-start.33 = (bf16[2,64,768]{2,1,0:T(8,128)(2,1)S(1)}, bf16[2,64,768]{2,1,0:T(8,128)(2,1)S(1)}, u32[]{:S(2)}, u32[]{:S(2)}) collective-permute-start(bf16[2,64,768]{2,1,0:T(8,128)(2,1)S(1)} %fusion.15), channel_id=1, source_target_pairs={{4,0},{0,4},{12,8},{8,12},{5,1},{1,5},{13,9},{9,13},{6,2},{2,6},{1... | collective-permute-start | bytes 589832 | tf_op jit(solution)/shard_map/ppermute | solution.py:27
  137.6 8.2 %collective-permute-start.28 = (bf16[2,64,1024]{2,1,0:T(8,128)(2,1)S(1)}, bf16[2,64,1024]{2,1,0:T(8,128)(2,1)S(1)}, u32[]{:S(2)}, u32[]{:S(2)}) collective-permute-start(bf16[2,64,1024]{2,1,0:T(8,128)(2,1)S(1)} %fusion.12), channel_id=1, source_target_pairs={{4,0},{0,4},{12,8},{8,12},{5,1},{1,5},{13,9},{9,13},{6,2},{2,6},{1... | collective-permute-start | bytes 786440 | tf_op jit(solution)/shard_map/ppermute | solution.py:27
  139.0 7.8 %collective-permute-start.34 = (bf16[1,64,768]{2,1,0:T(8,128)(2,1)S(1)}, bf16[1,64,768]{2,1,0:T(8,128)(2,1)S(1)}, u32[]{:S(2)}, u32[]{:S(2)}) collective-permute-start(bf16[1,64,768]{2,1,0:T(8,128)(2,1)S(1)} %fusion.21), channel_id=1, source_target_pairs={{8,0},{12,4},{0,8},{4,12},{9,1},{13,5},{1,9},{5,13},{10,2},{14,6},... | collective-permute-start | bytes 294920 | tf_op jit(solution)/shard_map/ppermute | solution.py:27
  145.9 7.3 %collective-permute-start.29 = (bf16[1,64,1024]{2,1,0:T(8,128)(2,1)S(1)}, bf16[1,64,1024]{2,1,0:T(8,128)(2,1)S(1)}, u32[]{:S(2)}, u32[]{:S(2)}) collective-permute-start(bf16[1,64,1024]{2,1,0:T(8,128)(2,1)S(1)} %fusion.19), channel_id=1, source_target_pairs={{8,0},{12,4},{0,8},{4,12},{9,1},{13,5},{1,9},{5,13},{10,2},{14,6},... | collective-permute-start | bytes 393224 | tf_op jit(solution)/shard_map/ppermute | solution.py:27
  (34 other events, 480.4 us)
